TPU v7x, 32 devices: a whole 2x2x4 slice. The times are simulated.
32 devices in a mesh: grp: 2 (over y), sv: 4 (over z), tv: 4 (over x, core).
Axes of the slice: x: 2, y: 2, z: 4, core: 2. Of those that a mesh axis runs over, the one named last changes fastest.
Arguments:
- student_states: bfloat16 [512, 1792], P('grp', 'tv'), parts along dimension 0, may hold values from -60 to 60
- teacher_states: bfloat16 [512, 2304], P('grp', 'tv'), parts along dimension 0, may hold values from -60 to 60
- student_queries: bfloat16 [512, 256], P('grp', 'tv'), parts along dimension 0, may hold values from -60 to 60
- teacher_keys: bfloat16 [512, 256], P('grp', 'tv'), parts along dimension 0, may hold values from -6 to 6
- student_targets: int32 [512], P('grp'), parts along dimension 0, may hold values from 0 to 8191
- teacher_targets: int32 [512], P('grp'), parts along dimension 0, may hold values from 0 to 8191
- student_lengths: int32 [4], P('grp'), parts along dimension 0, may hold values from 64 to 128
- teacher_lengths: int32 [4], P('grp'), parts along dimension 0, may hold values from 64 to 128
- to_teacher: bfloat16 [1792, 2304], P('tv', 'sv'), may hold values from -0.125 to 0.125
- to_student: bfloat16 [2304, 1792], P('tv', 'sv'), may hold values from -0.125 to 0.125
- student_head: bfloat16 [1792, 8192], P(None, ('sv', 'tv')), may hold values from -0.125 to 0.125
- teacher_head: bfloat16 [2304, 8192], P(None, ('sv', 'tv')), may hold values from -0.125 to 0.125
Outputs:
- student_loss: float32 [512], P('grp'), parts along dimension 0
- teacher_loss: float32 [512], P('grp'), parts along dimension 0
- student_grad: bfloat16 [512, 8192], P('grp', ('sv', 'tv')), parts along dimension 0
- teacher_grad: bfloat16 [512, 8192], P('grp', ('sv', 'tv')), parts along dimension 0
There are 2 independent parts, one for each index of `grp`. A program takes and returns all parts, laid end to end along the dimension named above; an argument that names none is the same for every part. Nothing has to cross between parts.
All inputs are finite; a program needn't handle non-finite values.
Results may differ from a plain program's by a relative error of at most 0.0086.
Values may be sent and summed in bfloat16 or wider, within the bound.
No kernel may reach another device: no remote copies, remote signals or barrier semaphores. Data moves between devices by JAX's collectives and lax.ppermute only.
A program may use at most 64 MiB of HBM per device.

v0:
```python
import jax
import jax.numpy as jnp
from jax import lax
from jax.sharding import PartitionSpec as P

DK = 256


floor_value = -1e30


def combined_all(part, axis, combine):
    gathered = jax.tree.map(lambda a: lax.all_gather(a, axis), part)

    def take(source):
        return jax.tree.map(lambda a: lax.dynamic_index_in_dim(a, source, 0, False), gathered)

    return lax.fori_loop(
        1, lax.axis_size(axis), lambda source, state: combine(state, take(source)), take(0)
    )


def align_block(student_queries, teacher_keys, teacher_states, teacher_lengths):
    sequences = teacher_lengths.shape[0]
    query_cols = student_queries.shape[1]
    queries = student_queries.reshape(sequences, -1, query_cols)
    keyset = teacher_keys.reshape(sequences, -1, query_cols)
    partial_scores = jnp.einsum("sid,sjd->sij", queries, keyset, preferred_element_type=jnp.float32)
    scores = lax.psum(partial_scores, "tv") * DK ** (-0.5)
    positions = lax.broadcasted_iota(jnp.int32, scores.shape, 2)
    scores = jnp.where(positions < teacher_lengths[:, None, None], scores, floor_value)
    highest = jnp.max(scores, axis=2, keepdims=True)
    weights = jnp.exp(scores - highest)
    weights = (weights / jnp.sum(weights, axis=2, keepdims=True)).astype(jnp.bfloat16)
    states = teacher_states.reshape(sequences, -1, teacher_states.shape[1])
    aligned = jnp.einsum("sij,sjd->sid", weights, states, preferred_element_type=jnp.float32)
    return aligned.astype(jnp.bfloat16).reshape(-1, teacher_states.shape[1])


def live_rows(row_count, lengths, sequence_length):
    indices = lax.broadcasted_iota(jnp.int32, (row_count,), 0)
    sequence = indices // sequence_length
    position = indices % sequence_length
    owners = lax.broadcasted_iota(jnp.int32, (row_count, lengths.shape[0]), 1)
    length_limit = jnp.sum(jnp.where(sequence[:, None] == owners, lengths[None, :], 0), axis=1)
    return (position < length_limit).astype(jnp.float32)


def local_stats(logits, target_cols, kind_index):
    other_kind = 1 - kind_index
    highest = jnp.max(logits, axis=2)
    scaled = jnp.exp(logits - highest[:, :, None])
    totals = jnp.sum(scaled, axis=2)
    spread = jnp.sum(
        scaled[:, kind_index] * (logits[:, kind_index] - logits[:, other_kind]), axis=1
    )
    column = lax.broadcasted_iota(jnp.int32, logits.shape, 2)
    picked = jnp.sum(jnp.where(column == target_cols[:, None, None], logits, 0.0), axis=2)
    return (highest, totals, spread, picked)


def side_combine(former, latter, kind_index):
    highest = jnp.maximum(former[0], latter[0])
    former_scale = jnp.exp(former[0] - highest)
    latter_scale = jnp.exp(latter[0] - highest)
    totals = former[1] * former_scale + latter[1] * latter_scale
    spread = former[2] * former_scale[:, kind_index] + latter[2] * latter_scale[:, kind_index]
    return (highest, totals, spread, former[3] + latter[3])


def student_combine(former, latter):
    return side_combine(former, latter, 1)


def teacher_combine(former, latter):
    return side_combine(former, latter, 0)


def side_terms(logits, statistics, target_cols):
    highest, totals = (statistics[0], statistics[1])
    log_total = highest + jnp.log(totals)
    chances = jnp.exp(logits - log_total[:, :, None])
    column = lax.broadcasted_iota(jnp.int32, chances[:, 0].shape, 1)
    target_hot = (column == target_cols[:, None]).astype(jnp.float32)
    return (log_total, chances, target_hot)


def student_side(logits, statistics, target_cols, live_mask):
    log_total, chances, target_hot = side_terms(logits, statistics, target_cols)
    totals, spread, picked = (statistics[1], statistics[2], statistics[3])
    diverge = spread / totals[:, 1] - log_total[:, 1] + log_total[:, 0]
    row_loss = live_mask * (
        log_total[:, 0] - picked[:, 0] + log_total[:, 1] - picked[:, 1] + diverge
    )
    gradient = live_mask[:, None] * (2.0 * chances[:, 0] - target_hot - chances[:, 1])
    return (row_loss, gradient.astype(jnp.bfloat16))


def teacher_side(logits, statistics, target_cols, live_mask):
    log_total, chances, target_hot = side_terms(logits, statistics, target_cols)
    totals, spread, picked = (statistics[1], statistics[2], statistics[3])
    diverge = spread / totals[:, 0] - log_total[:, 0] + log_total[:, 1]
    row_loss = live_mask * (diverge + log_total[:, 1] - picked[:, 1])
    gradient = live_mask[:, None] * (2.0 * chances[:, 1] - chances[:, 0] - target_hot)
    return (row_loss, gradient.astype(jnp.bfloat16))


def body(
    student_states,
    teacher_states,
    student_queries,
    teacher_keys,
    student_targets,
    teacher_targets,
    student_lengths,
    teacher_lengths,
    to_teacher,
    to_student,
    student_head,
    teacher_head,
):
    row_total = student_states.shape[0]
    sequence_length = row_total // student_lengths.shape[0]
    sv_index = lax.axis_index("sv")
    tv_index = lax.axis_index("tv")
    tv_count = lax.axis_size("tv")
    vocab_block = sv_index * tv_count + tv_index
    aligned_block = align_block(student_queries, teacher_keys, teacher_states, teacher_lengths)
    full_student = lax.all_gather(student_states, "tv", axis=1, tiled=True)
    full_aligned = lax.all_gather(aligned_block, "tv", axis=1, tiled=True)
    teacher_part = lax.psum(
        jnp.dot(student_states, to_teacher, preferred_element_type=jnp.float32), "tv"
    )
    student_part = lax.psum(
        jnp.dot(aligned_block, to_student, preferred_element_type=jnp.float32), "tv"
    )
    into_teacher = lax.all_gather(teacher_part.astype(jnp.bfloat16), "sv", axis=1, tiled=True)
    into_student = lax.all_gather(student_part.astype(jnp.bfloat16), "sv", axis=1, tiled=True)
    student_logits = jnp.stack(
        [
            jnp.dot(full_student, student_head, preferred_element_type=jnp.float32),
            jnp.dot(into_student, student_head, preferred_element_type=jnp.float32),
        ],
        axis=1,
    )
    student_cols = student_targets - vocab_block * student_head.shape[1]
    student_stats = local_stats(student_logits, student_cols, 1)
    teacher_logits = jnp.stack(
        [
            jnp.dot(full_aligned, teacher_head, preferred_element_type=jnp.float32),
            jnp.dot(into_teacher, teacher_head, preferred_element_type=jnp.float32),
        ],
        axis=1,
    )
    teacher_cols = teacher_targets - vocab_block * teacher_head.shape[1]
    teacher_stats = local_stats(teacher_logits, teacher_cols, 0)
    student_stats = combined_all(student_stats, ("sv", "tv"), student_combine)
    teacher_stats = combined_all(teacher_stats, ("sv", "tv"), teacher_combine)
    every_live = live_rows(row_total, student_lengths, sequence_length)
    student_loss, student_grad = student_side(
        student_logits, student_stats, student_cols, every_live
    )
    teacher_loss, teacher_grad = teacher_side(
        teacher_logits, teacher_stats, teacher_cols, every_live
    )
    return (student_loss, teacher_loss, student_grad, teacher_grad)


def solution(mesh):
    in_specs = (
        P("grp", "tv"),
        P("grp", "tv"),
        P("grp", "tv"),
        P("grp", "tv"),
        P("grp"),
        P("grp"),
        P("grp"),
        P("grp"),
        P("tv", "sv"),
        P("tv", "sv"),
        P(None, ("sv", "tv")),
        P(None, ("sv", "tv")),
    )
    out_specs = (P("grp"), P("grp"), P("grp", ("sv", "tv")), P("grp", ("sv", "tv")))
    return jax.shard_map(body, mesh=mesh, in_specs=in_specs, out_specs=out_specs, check_vma=False)
```

profile of v0, /device:TPU:0, one launch (start us, length us, event | category | flops | bytes accessed | tf_op | source)
XLA Modules:
  0.0 294.7 jit_solution(5090712872728876629)
XLA Ops:
  7.2 0.0 copy-start
  7.2 0.0 all-reduce.4.cloned.1.call-start
  7.3 1.8 fusion.30
  9.1 0.0 all-reduce.4.cloned.1.call-update
  9.1 0.0 all-gather.15.cloned.1.call-start
  9.2 12.4 %all_gather.60 = bf16[256,1792]{0,1:T(8,128)(2,1)} all-gather(bf16[256,448]{0,1:T(8,128)(2,1)} %param.16), channel_id=1, replica_groups=mesh['grp'=2,'sv'=4,'tv'=4] {'tv'}, dimensions={1}, use_global_device_ids=true | all-gather | bytes 1146880 | tf_op jit(solution)/shard_map/all_gather | solution.py:129
  21.6 1.3 fusion.60
  23.0 0.1 fusion.35
  23.0 22.0 %all-reduce.4.cloned.1.call-done = f32[2,128,128]{2,1,0:T(8,128)} async-done(((f32[2,128,128]{2,1,0:T(8,128)}), f32[2,128,128]{2,1,0:T(8,128)}) %all-reduce.4.cloned.1.call-update) | async-done | bytes 131088 | tf_op jit(solution)/shard_map/psum | solution.py:29
  45.1 1.2 fusion.56
  46.3 2.4 fusion.5
  48.7 1.5 fusion.48
  50.1 26.0 %all-reduce.5 = (bf16[256,448]{0,1:T(8,128)(2,1)}, bf16[256,576]{0,1:T(8,128)(2,1)}) all-reduce(f32[256,448]{0,1:T(8,128)S(1)} %fusion.48, f32[256,576]{0,1:T(8,128)S(1)} %fusion.60), channel_id=1, replica_groups=mesh['grp'=2,'sv'=4,'tv'=4] {'tv'}, use_global_device_ids=true, to_apply=%region_4.5 | all-reduce | flops 262144 | bytes 1572864 | tf_op jit(solution)/shard_map/psum | solution.py:134
  76.2 0.0 all-gather.15.cloned.1.call-update
  76.2 0.0 all-gather.13.cloned.1.call-start
  76.2 0.6 fusion.47
  76.8 2.6 fusion.57
  79.4 0.8 copy.53
  80.2 33.6 %all_gather.61 = bf16[256,1792]{0,1:T(8,128)(2,1)S(1)} all-gather(bf16[256,448]{0,1:T(8,128)(2,1)S(1)} %copy-done.6), channel_id=1, replica_groups=mesh['grp'=2,'sv'=4,'tv'=4] {'sv'}, dimensions={1}, use_global_device_ids=true | all-gather | bytes 1146880 | tf_op jit(solution)/shard_map/all_gather | solution.py:138
  113.8 0.7 fusion.58
  114.5 0.4 select_reduce_fusion.1
  114.8 0.3 fusion.52
  115.1 0.2 fusion.20
  115.3 20.8 %all-gather.8 = f32[16,1,256]{2,1,0:T(1,128)S(1)} all-gather(f32[1,1,256]{2,1,0:T(1,128)S(1)} %bitcast.187), channel_id=4, replica_groups=mesh['grp'=2,'sv'=4,'tv'=4] {'sv','tv'}, dimensions={0}, use_global_device_ids=true | all-gather | bytes 17408 | tf_op jit(solution)/shard_map/all_gather | solution.py:13
  136.1 17.5 %all-gather = f32[4096,2]{0,1:T(2,128)S(1)} all-gather(f32[256,2]{0,1:T(2,128)S(1)} %get-tuple-element.461), channel_id=2, replica_groups=mesh['grp'=2,'sv'=4,'tv'=4] {'sv','tv'}, dimensions={0}, use_global_device_ids=true | all-gather | bytes 34816 | tf_op jit(solution)/shard_map/all_gather | solution.py:13
  153.6 18.9 %all-gather.1 = f32[4096,2]{0,1:T(2,128)S(1)} all-gather(f32[256,2]{0,1:T(2,128)S(1)} %get-tuple-element.510), channel_id=3, replica_groups=mesh['grp'=2,'sv'=4,'tv'=4] {'sv','tv'}, dimensions={0}, use_global_device_ids=true | all-gather | bytes 34816 | tf_op jit(solution)/shard_map/all_gather | solution.py:13
  172.4 17.5 %all-gather.3 = f32[4096,2]{0,1:T(2,128)S(1)} all-gather(f32[256,2]{0,1:T(2,128)S(1)} %get-tuple-element.460), channel_id=5, replica_groups=mesh['grp'=2,'sv'=4,'tv'=4] {'sv','tv'}, dimensions={0}, use_global_device_ids=true | all-gather | bytes 34816 | tf_op jit(solution)/shard_map/all_gather | solution.py:13
  189.9 0.0 all-gather.13.cloned.1.call-update
  189.9 1.6 while.42
  191.5 0.6 slice.101
  192.1 0.6 fusion.55
  192.7 0.6 fusion.54
  193.3 2.9 fusion.61
  196.2 9.7 %all-gather.13.cloned.1.call-done = bf16[256,2304]{0,1:T(8,128)(2,1)} async-done(((bf16[256,576]{0,1:T(8,128)(2,1)}), bf16[256,2304]{0,1:T(8,128)(2,1)}) %all-gather.13.cloned.1.call-update) | async-done | bytes 1179664 | tf_op jit(solution)/shard_map/all_gather | solution.py:130
  205.9 2.1 fusion.59
  208.1 0.4 select_reduce_fusion
  208.4 20.5 %all-gather.4 = f32[4096,2]{0,1:T(2,128)S(1)} all-gather(f32[256,2]{0,1:T(2,128)S(1)} %get-tuple-element.459), channel_id=6, replica_groups=mesh['grp'=2,'sv'=4,'tv'=4] {'sv','tv'}, dimensions={0}, use_global_device_ids=true | all-gather | bytes 34816 | tf_op jit(solution)/shard_map/all_gather | solution.py:13
  228.9 0.3 fusion.51
  229.2 0.2 fusion.18
  229.4 17.4 %all-gather.9 = f32[16,1,256]{2,1,0:T(1,128)S(1)} all-gather(f32[1,1,256]{2,1,0:T(1,128)S(1)} %bitcast.188), channel_id=8, replica_groups=mesh['grp'=2,'sv'=4,'tv'=4] {'sv','tv'}, dimensions={0}, use_global_device_ids=true | all-gather | bytes 17408 | tf_op jit(solution)/shard_map/all_gather | solution.py:13
  246.8 18.8 %all-gather.5 = f32[4096,2]{0,1:T(2,128)S(1)} all-gather(f32[256,2]{0,1:T(2,128)S(1)} %get-tuple-element.508), channel_id=7, replica_groups=mesh['grp'=2,'sv'=4,'tv'=4] {'sv','tv'}, dimensions={0}, use_global_device_ids=true | all-gather | bytes 34816 | tf_op jit(solution)/shard_map/all_gather | solution.py:13
  265.7 17.5 %all-gather.7 = f32[4096,2]{0,1:T(2,128)S(1)} all-gather(f32[256,2]{0,1:T(2,128)S(1)} %get-tuple-element.458), channel_id=9, replica_groups=mesh['grp'=2,'sv'=4,'tv'=4] {'sv','tv'}, dimensions={0}, use_global_device_ids=true | all-gather | bytes 34816 | tf_op jit(solution)/shard_map/all_gather | solution.py:13
  283.2 1.6 while.43
  284.8 1.5 subtract_exponential_fusion.2
  286.4 0.0 copy-start.8
  286.4 0.0 copy-start.11
  286.4 1.1 fusion.11
  287.6 0.6 fusion.37
  (204 shorter events, 2.0 us)
Async XLA Ops:
  7.2 186.1 %copy-start = (bf16[2304,512]{1,0:T(8,128)(2,1)S(1)}, bf16[2304,512]{1,0:T(8,128)(2,1)}, u32[]{:S(2)}) copy-start(bf16[2304,512]{1,0:T(8,128)(2,1)} %param.27) | copy-start | bytes 7077892
  7.2 14.4 %copy-start.5 = (bf16[448,576]{1,0:T(8,128)(2,1)S(1)}, bf16[448,576]{1,0:T(8,128)(2,1)}, u32[]{:S(2)}) copy-start(bf16[448,576]{1,0:T(8,128)(2,1)} %param.24) | copy-start | bytes 1548292
  7.2 15.7 %copy-start.15 = (s32[256]{0:T(256)S(1)}, s32[256]{0:T(256)}, u32[]{:S(2)}) copy-start(s32[256]{0:T(256)} %param.21) | copy-start | bytes 3076
  7.2 15.7 %copy-start.16 = (s32[256]{0:T(256)S(1)}, s32[256]{0:T(256)}, u32[]{:S(2)}) copy-start(s32[256]{0:T(256)} %param.20) | copy-start | bytes 3076
  7.2 15.7 %copy-start.17 = (s32[2]{0:T(128)S(1)}, s32[2]{0:T(128)}, u32[]{:S(2)}) copy-start(s32[2]{0:T(128)} %param.22) | copy-start | bytes 28
  7.2 37.9 %copy-start.18 = (s32[2]{0:T(128)S(1)}, s32[2]{0:T(128)}, u32[]{:S(2)}) copy-start(s32[2]{0:T(128)} %param.23) | copy-start | bytes 28
  7.2 37.9 %all-reduce.4.cloned.1.call-start = ((), (), s32[]{:S(2)}) async-start(), calls=%async_computation | async-start | bytes 262144 | tf_op jit(solution)/shard_map/psum | solution.py:29
  9.1 184.2 %all-gather.15.cloned.1.call-start = ((), (), s32[]{:S(2)}) async-start(), calls=%async_computation.2 | async-start | bytes 1474560 | tf_op jit(solution)/shard_map/all_gather | solution.py:137
  23.0 53.2 %copy-start.7 = (s32[256]{0:T(256)}, s32[256]{0:T(256)S(1)}, u32[]{:S(2)}) copy-start(s32[256]{0:T(256)S(1)} %fusion.35) | copy-start | bytes 3076
  76.2 3.2 %copy-start.4 = (bf16[2,72,8,128]{3,2,1,0:T(8,128)(2,1)S(1)}, bf16[2,72,8,128]{3,2,1,0:T(8,128)(2,1)}, u32[]{:S(2)}) copy-start(bf16[2,72,8,128]{3,2,1,0:T(8,128)(2,1)} %fusion.5) | copy-start | bytes 884740
  76.2 129.7 %all-gather.13.cloned.1.call-start = ((), (), s32[]{:S(2)}) async-start(), calls=%async_computation.1 | async-start | bytes 1474560 | tf_op jit(solution)/shard_map/all_gather | solution.py:130
  76.8 3.4 %copy-start.6 = (bf16[256,448]{0,1:T(8,128)(2,1)S(1)}, bf16[256,448]{0,1:T(8,128)(2,1)}, u32[]{:S(2)}) copy-start(bf16[256,448]{0,1:T(8,128)(2,1)} %get-tuple-element.498) | copy-start | bytes 688132
  76.8 37.0 %copy-start.3 = (bf16[1792,512]{1,0:T(8,128)(2,1)S(1)}, bf16[1792,512]{1,0:T(8,128)(2,1)}, u32[]{:S(2)}) copy-start(bf16[1792,512]{1,0:T(8,128)(2,1)} %param.26) | copy-start | bytes 5505028
  205.9 2.1 copy-start.1
  208.0 21.3 %copy-start.2 = (f32[256,512]{1,0:T(8,128)}, f32[256,512]{1,0:T(8,128)S(1)}, u32[]{:S(2)}) copy-start(f32[256,512]{1,0:T(8,128)S(1)} %fusion.59) | copy-start | bytes 1572868
  284.8 1.6 copy-start.9
  286.4 1.2 copy-start.8
  286.4 1.2 copy-start.10
  286.4 1.2 copy-start.11
  286.4 1.2 copy-start.12
  286.4 1.2 copy-start.13
  286.4 1.2 copy-start.14
Sparse Core Ops, SparseCore 0:
  11.0 34.0 all-reduce.3
  76.3 43.0 all-gather.14
  190.0 15.8 all-gather.12
where the time goes:
time: 295 us
  blocking collectives  221 us (75%)
  waiting for transfers between devices  31.8 us (11%)
  matrix products  15.3 us (5%)
  between operations  14.1 us (5%)
  other arithmetic  8 us (3%)
  local copies, waits for them, and re-layouts  3.24 us (1%)
    all_gather x8, blocking collectives, combined_all(): gathered = jax.tree.map(lambda a: lax.all_gather(a, axis), part)  149 us
    all_gather x1, blocking collectives, body(): lax.all_gather(student_part.astype(jnp.bfloat16), 'sv', axis=1, tiled=True)  33.6 us
    psum x1, blocking collectives, body(): lax.psum(jnp.dot(aligned_block, to_student, preferred_element_type=jnp.fl...  26 us
    psum x1, waiting for transfers between devices, align_block(): scores = lax.psum(partial_scores, 'tv') * DK ** (-0.5)  22 us
    all_gather x1, blocking collectives, body(): full_student = lax.all_gather(student_states, 'tv', axis=1, tiled=True)  12.4 us
    all_gather x1, waiting for transfers between devices, body(): full_aligned = lax.all_gather(aligned_block, 'tv', axis=1, tiled=True)  9.69 us
  transfers between devices with their start and end apart: 3, of which 2 were waited for; matrix products, arithmetic and copies ran while one was open for 4% of the time, Pallas kernels for 0%

commit v1 on v0

v1 whole, which is shorter than its diff:
```python
import functools

import jax
import jax.numpy as jnp
from jax import lax
from jax.experimental import pallas as pl
from jax.experimental.pallas import tpu as pltpu
from jax.sharding import PartitionSpec as P

DK = 256
FLOOR = -1e30
CORES = 2
STATS = 8
F32 = jnp.float32
BF16 = jnp.bfloat16

VMEM = pl.BlockSpec(memory_space=pltpu.VMEM)
SMEM = pl.BlockSpec(memory_space=pltpu.SMEM)


def kernel_call(body, out_shape, in_specs, scratch=(), cost=1_000_000):
    single = not isinstance(out_shape, (tuple, list))
    return pl.pallas_call(
        body,
        out_shape=out_shape,
        in_specs=in_specs,
        out_specs=VMEM if single else [VMEM] * len(out_shape),
        scratch_shapes=list(scratch),
        compiler_params=pltpu.CompilerParams(vmem_limit_bytes=48 * 2**20),
        cost_estimate=pl.CostEstimate(flops=cost, bytes_accessed=cost, transcendentals=0),
    )


def dot00(a, b):
    return lax.dot_general(a, b, (((0,), (0,)), ((), ())), preferred_element_type=F32)


def dot10(a, b):
    return lax.dot_general(a, b, (((1,), (0,)), ((), ())), preferred_element_type=F32)


def half(core, width):
    return pl.ds(pl.multiple_of(core * width, width), width)


def project_teacher(core_ref, own_s, mate_s, own_w, mate_w, out_ref):
    cols = half(core_ref[0], out_ref.shape[1])
    out_ref[...] = dot00(own_w[...], own_s[:, cols]) + dot00(mate_w[...], mate_s[:, cols])


def attend(core_ref, lens_ref, q_ref, k_ref, own_t, mate_t, own_w, mate_w, out_ref, weights_ref):
    sequences = lens_ref.shape[0]
    width = q_ref.shape[1] // sequences
    for s in range(sequences):
        tokens = slice(s * width, (s + 1) * width)
        scores = dot00(k_ref[:, tokens], q_ref[:, tokens]) * DK ** (-0.5)
        position = lax.broadcasted_iota(jnp.int32, scores.shape, 0)
        scores = jnp.where(position < lens_ref[s], scores, FLOOR)
        raised = jnp.exp(scores - jnp.max(scores, axis=0, keepdims=True))
        weights_ref[s] = (raised / jnp.sum(raised, axis=0, keepdims=True)).astype(BF16)
    per_core = sequences // CORES
    for n in range(per_core):
        s = core_ref[0] * per_core + n
        weights = weights_ref[s]
        tokens = half(s, width)
        own = dot10(own_t[:, tokens], weights).astype(BF16)
        mate = dot10(mate_t[:, tokens], weights).astype(BF16)
        out_ref[:, n * width : (n + 1) * width] = dot10(own_w[...], own) + dot10(mate_w[...], mate)


def own_logits(blocks, index_ref, weights_ref, *refs):
    s_refs, t_refs = refs[:blocks], refs[blocks : 2 * blocks]
    s_head, t_head, s_out, t_out, s_all, t_all = refs[2 * blocks :]
    sequences, width, _ = weights_ref.shape
    s_rows, t_rows = s_refs[0].shape[0], t_refs[0].shape[0]
    for n in range(blocks):
        index = index_ref[n]
        s_all[half(index, s_rows), :] = s_refs[n][...]
        for s in range(sequences):
            tokens = slice(s * width, (s + 1) * width)
            t_all[half(index, t_rows), tokens] = dot10(t_refs[n][:, tokens], weights_ref[s]).astype(BF16)
    s_out[...] = dot00(s_all[...], s_head[...])
    t_out[...] = dot00(t_all[...], t_head[...])


def local_side(own, mapped, columns, forward, pick_both):
    def total(logits):
        highest = jnp.max(logits, axis=1, keepdims=True)
        raised = jnp.exp(logits - highest)
        summed = jnp.sum(raised, axis=1, keepdims=True)
        return raised, summed, highest + jnp.log(summed)

    own_raised, own_sum, own_total = total(own)
    mapped_raised, mapped_sum, mapped_total = total(mapped)
    if forward == "mapped":
        spread = jnp.sum(mapped_raised * (mapped - own), axis=1, keepdims=True) / mapped_sum
    else:
        spread = jnp.sum(own_raised * (own - mapped), axis=1, keepdims=True) / own_sum
    lane = lax.broadcasted_iota(jnp.int32, own.shape, 1)
    picked = own + mapped if pick_both else mapped
    picked = jnp.sum(jnp.where(lane == columns, picked, 0.0), axis=1, keepdims=True)
    return own_total, mapped_total, spread, picked


def target_columns(refs, base):
    row = lax.broadcasted_iota(jnp.int32, (STATS, refs[0].shape[1]), 0)
    stacked = jnp.where(row == 0, refs[0][...] - base, refs[1][...] - base).astype(F32)
    turned = jnp.transpose(stacked)
    return turned[:, 0:1].astype(jnp.int32), turned[:, 1:2].astype(jnp.int32)


def mapped_logits(blocks, index_ref, s_targets, t_targets, s_own, t_own, *refs):
    s_refs, t_refs = refs[: 2 * blocks], refs[2 * blocks : 4 * blocks]
    s_head, t_head, s_out, t_out, stats_out, s_all, t_all = refs[4 * blocks :]
    core, base = index_ref[blocks], index_ref[blocks + 1]
    width = s_refs[0].shape[1]
    for n in range(blocks):
        index = index_ref[n]
        for side in range(CORES):
            tokens = half(core if side == 0 else 1 - core, width)
            s_all[half(index, s_refs[0].shape[0]), tokens] = s_refs[2 * n + side][...]
            t_all[half(index, t_refs[0].shape[0]), tokens] = t_refs[2 * n + side][...]
    s_mapped = dot00(s_all[...], s_head[...])
    s_out[...] = s_mapped
    t_mapped = dot00(t_all[...], t_head[...])
    t_out[...] = t_mapped
    s_columns, t_columns = target_columns((s_targets, t_targets), base)
    so, sm, s_spread, s_picked = local_side(s_own[...], s_mapped, s_columns, "mapped", True)
    to, tm, t_spread, t_picked = local_side(t_own[...], t_mapped, t_columns, "own", False)
    lane = lax.broadcasted_iota(jnp.int32, (so.shape[0], 128), 1)
    packed = jnp.zeros(lane.shape, F32)
    for k, column in enumerate((so, sm, to, tm, s_spread, s_picked, t_spread, t_picked)):
        packed = jnp.where(lane == k, column, packed)
    stats_out[...] = jnp.transpose(packed)[:STATS]


def merge_stats(parts):
    highest = parts[0]
    for part in parts[1:]:
        highest = jnp.maximum(highest, part)
    scales = [jnp.exp(part - highest) for part in parts]
    total = highest + jnp.log(sum(scales))
    shares = [jnp.exp(part - total) for part in parts]
    s_spread = sum(share[1:2] * part[4:5] for share, part in zip(shares, parts))
    t_spread = sum(share[2:3] * part[6:7] for share, part in zip(shares, parts))
    s_picked = sum(part[5:6] for part in parts)
    t_picked = sum(part[7:8] for part in parts)
    return total, s_spread, s_picked, t_spread, t_picked


def merge_kernel(parts, in_ref, out_ref):
    total, *rest = merge_stats([in_ref[n * STATS : (n + 1) * STATS, :] for n in range(parts)])
    row = lax.broadcasted_iota(jnp.int32, total.shape, 0)
    for k, value in enumerate(rest):
        total = jnp.where(row == 4 + k, value, total)
    out_ref[...] = total


def finish(parts, index_ref, lens_ref, s_targets, t_targets, so_ref, sm_ref, to_ref, tm_ref, *refs):
    s_loss, t_loss, s_grad, t_grad = refs[parts:]
    totals, s_spread, s_picked, t_spread, t_picked = merge_stats([ref[...] for ref in refs[:parts]])
    so, sm, to, tm = (totals[k : k + 1] for k in range(4))
    rows = s_loss.shape[1]
    sequences = lens_ref.shape[0]
    width = rows // sequences

    def live(shape, dim):
        place = lax.broadcasted_iota(jnp.int32, shape, dim)
        mask = jnp.zeros(shape, jnp.bool_)
        for s in range(sequences):
            mask |= (place >= s * width) & (place < s * width + lens_ref[s])
        return mask.astype(F32)

    live_row = live((1, rows), 1)
    s_loss[...] = live_row * (so + sm - s_picked + (s_spread - sm + so))
    t_loss[...] = live_row * ((t_spread - to + tm) + tm - t_picked)
    turned = jnp.transpose(totals)
    live_column = live((rows, 1), 0)
    s_columns, t_columns = target_columns((s_targets, t_targets), index_ref[0])
    lane = lax.broadcasted_iota(jnp.int32, so_ref.shape, 1)
    s_hot = (lane == s_columns).astype(F32)
    t_hot = (lane == t_columns).astype(F32)
    so_chance = jnp.exp(so_ref[...] - turned[:, 0:1])
    sm_chance = jnp.exp(sm_ref[...] - turned[:, 1:2])
    to_chance = jnp.exp(to_ref[...] - turned[:, 2:3])
    tm_chance = jnp.exp(tm_ref[...] - turned[:, 3:4])
    s_grad[...] = (live_column * (2.0 * so_chance - s_hot - sm_chance)).astype(BF16)
    t_grad[...] = (live_column * (2.0 * tm_chance - to_chance - t_hot)).astype(BF16)


def body(
    student_states,
    teacher_states,
    student_queries,
    teacher_keys,
    student_targets,
    teacher_targets,
    student_lengths,
    teacher_lengths,
    to_teacher,
    to_student,
    student_head,
    teacher_head,
):
    rows = student_states.shape[0]
    tv_count, sv_count = lax.axis_size("tv"), lax.axis_size("sv")
    chips = tv_count // CORES
    tv, sv = lax.axis_index("tv"), lax.axis_index("sv")
    core = tv % CORES
    vocab = student_head.shape[1]
    base = (sv * tv_count + tv) * vocab

    def swap(a):
        return lax.ppermute(a, "tv", [(t, t ^ 1) for t in range(tv_count)])

    def across(a):
        return [
            lax.ppermute(a, "tv", [(t, (t + CORES * n) % tv_count) for t in range(tv_count)])
            for n in range(1, chips)
        ]

    def along(a):
        return [
            lax.ppermute(a, "sv", [(z, (z + n) % sv_count) for z in range(sv_count)])
            for n in range(1, sv_count)
        ]

    s_t, t_t = student_states.T, teacher_states.T
    w_t, w_s = to_teacher, to_student.T
    core_index = core.astype(jnp.int32).reshape(1)

    mate_w_t, mate_s = swap(w_t), swap(s_t)
    mate_t, mate_w_s = swap(t_t), swap(w_s)
    tokens = rows // CORES
    part_t = kernel_call(
        project_teacher,
        jax.ShapeDtypeStruct((w_t.shape[1], tokens), F32),
        [SMEM] + [VMEM] * 4,
    )(core_index, s_t, mate_s, w_t, mate_w_t)
    other_t = across(part_t)

    queries = lax.all_gather(student_queries.T, "tv", axis=0, tiled=True)
    keys = lax.all_gather(teacher_keys.T, "tv", axis=0, tiled=True)
    sequences = teacher_lengths.shape[0]
    width = rows // sequences
    part_s, weights = kernel_call(
        attend,
        (
            jax.ShapeDtypeStruct((w_s.shape[0], tokens), F32),
            jax.ShapeDtypeStruct((sequences, width, width), BF16),
        ),
        [SMEM] * 2 + [VMEM] * 6,
    )(core_index, teacher_lengths, queries, keys, t_t, mate_t, w_s, mate_w_s)
    other_s = across(part_s)

    into_t = functools.reduce(jnp.add, other_t, part_t).astype(BF16)
    into_t = [into_t] + along(into_t)
    into_s = functools.reduce(jnp.add, other_s, part_s).astype(BF16)
    into_s = [into_s] + along(into_s)

    far_s, far_t = across(s_t), across(t_t)
    s_blocks, t_blocks = [s_t, mate_s], [t_t, mate_t]
    for a, b in zip(far_s, far_t):
        s_blocks += [a, swap(a)]
        t_blocks += [b, swap(b)]
    own_index = []
    for n in range(chips):
        source = (tv - CORES * n) % tv_count
        own_index += [source, source ^ 1]
    own_index = jnp.stack(own_index).astype(jnp.int32)
    logits = jax.ShapeDtypeStruct((rows, vocab), F32)
    s_own, t_own = kernel_call(
        functools.partial(own_logits, tv_count),
        (logits, logits),
        [SMEM] + [VMEM] * (1 + 2 * tv_count + 2),
        [
            pltpu.VMEM((student_head.shape[0], rows), BF16),
            pltpu.VMEM((teacher_head.shape[0], rows), BF16),
        ],
    )(own_index, weights, *s_blocks, *t_blocks, student_head, teacher_head)

    s_pieces = [p for a in into_s for p in (a, swap(a))]
    t_pieces = [p for a in into_t for p in (a, swap(a))]
    mapped_index = jnp.stack(
        [(sv - n) % sv_count for n in range(sv_count)] + [core, base]
    ).astype(jnp.int32)
    s_targets, t_targets = student_targets.reshape(1, rows), teacher_targets.reshape(1, rows)
    s_mapped, t_mapped, stats = kernel_call(
        functools.partial(mapped_logits, sv_count),
        (logits, logits, jax.ShapeDtypeStruct((STATS, rows), F32)),
        [SMEM] + [VMEM] * (4 + 4 * sv_count + 2),
        [
            pltpu.VMEM((student_head.shape[0], rows), BF16),
            pltpu.VMEM((teacher_head.shape[0], rows), BF16),
        ],
    )(mapped_index, s_targets, t_targets, s_own, t_own, *s_pieces, *t_pieces, student_head, teacher_head)

    stats = lax.all_gather(stats, "tv", axis=0, tiled=True)
    stats = kernel_call(
        functools.partial(merge_kernel, tv_count),
        jax.ShapeDtypeStruct((STATS, rows), F32),
        [VMEM],
    )(stats)
    stats = [stats] + along(stats)
    loss = jax.ShapeDtypeStruct((1, rows), F32)
    grad = jax.ShapeDtypeStruct((rows, vocab), BF16)
    s_loss, t_loss, s_grad, t_grad = kernel_call(
        functools.partial(finish, sv_count),
        (loss, loss, grad, grad),
        [SMEM] * 2 + [VMEM] * (6 + sv_count),
    )(
        base.astype(jnp.int32).reshape(1),
        student_lengths,
        s_targets,
        t_targets,
        s_own,
        s_mapped,
        t_own,
        t_mapped,
        *stats,
    )
    return s_loss.reshape(rows), t_loss.reshape(rows), s_grad, t_grad


def solution(mesh):
    in_specs = (
        P("grp", "tv"),
        P("grp", "tv"),
        P("grp", "tv"),
        P("grp", "tv"),
        P("grp"),
        P("grp"),
        P("grp"),
        P("grp"),
        P("tv", "sv"),
        P("tv", "sv"),
        P(None, ("sv", "tv")),
        P(None, ("sv", "tv")),
    )
    out_specs = (P("grp"), P("grp"), P("grp", ("sv", "tv")), P("grp", ("sv", "tv")))
    return jax.shard_map(body, mesh=mesh, in_specs=in_specs, out_specs=out_specs, check_vma=False)
```

time: 295 us -> 88.5 us (0.30)
  blocking collectives: 221 us -> 20.5 us
  starting transfers between devices: 0.12 us -> 23.5 us
  matrix products: 15.3 us -> 0 us
  between operations: 14.1 us -> 0.93 us
  Pallas kernels: 0 us -> 13 us
  waiting for transfers between devices: 31.8 us -> 20.7 us
  other arithmetic: 8 us -> 0.15 us
  local copies, waits for them, and re-layouts: 3.24 us -> 9.26 us
    all_gather x10 -> x3, blocking collectives: 195 us -> 20.5 us  [the longest x1 9.63 us: body(): queries = lax.all_gather(student_queries.T, 'tv', axis=0, tiled=True)]
    psum x1 -> x0, blocking collectives: 26 us -> none  [body(): lax.psum(jnp.dot(aligned_block, to_student, preferred_element_type=jnp.fl...]
    ppermute x0 -> x27, starting transfers between devices: none -> 23.5 us  [the longest x9 13.8 us: along(): lax.ppermute(a, 'sv', [(z, (z + n) % sv_count) for z in range(sv_count)])]
    psum x1 -> x0, waiting for transfers between devices: 22 us -> none  [align_block(): scores = lax.psum(partial_scores, 'tv') * DK ** (-0.5)]
    ppermute x0 -> x27, waiting for transfers between devices: none -> 20.7 us  [the longest x9 16.7 us: along(): lax.ppermute(a, 'sv', [(z, (z + n) % sv_count) for z in range(sv_count)])]
    dot_general x8 -> x0, matrix products: 15.3 us -> none  [the longest x1 2.92 us: body(): jnp.dot(into_teacher, teacher_head, preferred_element_type=jnp.float32)]
    pallas_call x0 -> x6, Pallas kernels: none -> 13 us  [the longest x1 4.43 us: body(): kernel_call(functools.partial(mapped_logits, sv_count), (logits, logits,...]
    all_gather x2 -> x0, waiting for transfers between devices: 9.69 us -> none  [the longest x1 9.69 us: body(): full_aligned = lax.all_gather(aligned_block, 'tv', axis=1, tiled=True)]
  transfers between devices with their start and end apart: 3 -> 27, of which waited for: 2 -> 7; matrix products, arithmetic and copies ran while one was open for 4% -> 1% of each run, Pallas kernels for 0% -> 7%
where the time goes in v1:
time: 88.5 us; the launch traced here: 87.9 us
  starting transfers between devices  23.5 us (27%)
  waiting for transfers between devices  20.7 us (23%)
  blocking collectives  20.5 us (23%)
  Pallas kernels  13 us (15%)
  local copies, waits for them, and re-layouts  9.26 us (10%)
  between operations  0.93 us (1%)
    ppermute x9, waiting for transfers between devices, along(): lax.ppermute(a, 'sv', [(z, (z + n) % sv_count) for z in range(sv_count)])  16.7 us
    ppermute x9, starting transfers between devices, along(): lax.ppermute(a, 'sv', [(z, (z + n) % sv_count) for z in range(sv_count)])  13.8 us
    all_gather x1, blocking collectives, body(): queries = lax.all_gather(student_queries.T, 'tv', axis=0, tiled=True)  9.63 us
    unnamed x48, local copies, waits for them, and re-layouts  8.67 us
    ppermute x4, starting transfers between devices, across(): lax.ppermute(a, 'tv', [(t, (t + CORES * n) % tv_count) for t in range(tv_...  6.37 us
    all_gather x1, blocking collectives, body(): keys = lax.all_gather(teacher_keys.T, 'tv', axis=0, tiled=True)  5.67 us
    all_gather x1, blocking collectives, body(): stats = lax.all_gather(stats, 'tv', axis=0, tiled=True)  5.18 us
    pallas_call x1, Pallas kernels, body(): kernel_call(functools.partial(mapped_logits, sv_count), (logits, logits,...  4.43 us
  transfers between devices with their start and end apart: 27, of which 7 were waited for; matrix products, arithmetic and copies ran while one was open for 1% of the time, Pallas kernels for 7%

profile of v1, /device:TPU:0, one launch (start us, length us, event | category | flops | bytes accessed | tf_op | source)
XLA Modules:
  0.0 87.9 jit_solution(10846459102542540191)
XLA Ops:
  0.6 0.5 collective-permute-start.1
  1.2 0.1 collective-permute-start.15
  1.2 0.4 collective-permute-start
  1.7 2.6 %collective-permute-start.5 = (bf16[576,256]{1,0:T(8,128)(2,1)}, bf16[576,256]{1,0:T(8,128)(2,1)}, u32[]{:S(2)}, u32[]{:S(2)}) collective-permute-start(bf16[576,256]{1,0:T(8,128)(2,1)} %bitcast.20), channel_id=1, source_target_pairs={{0,2},{1,3},{2,0},{3,1},{4,6},{5,7},{6,4},{7,5},{8,10},{9,11},{10,... | collective-permute-start | bytes 884744 | tf_op jit(solution)/shard_map/ppermute | solution.py:218
  4.2 0.2 collective-permute-start.2
  4.4 9.6 %all_gather.9.q_ref = bf16[256,256]{1,0:T(8,128)(2,1)} all-gather(bf16[64,256]{1,0:T(8,128)(2,1)} %bitcast.33), channel_id=1, replica_groups=mesh['grp'=2,'sv'=4,'tv'=4] {'tv'}, dimensions={0}, use_global_device_ids=true | all-gather | bytes 163840 | tf_op jit(solution)/shard_map/all_gather | solution.py:242
  14.0 5.7 %all_gather.10.k_ref = bf16[256,256]{1,0:T(8,128)(2,1)S(1)} all-gather(bf16[64,256]{1,0:T(8,128)(2,1)} %bitcast.34), channel_id=1, replica_groups=mesh['grp'=2,'sv'=4,'tv'=4] {'tv'}, dimensions={0}, use_global_device_ids=true | all-gather | bytes 163840 | tf_op jit(solution)/shard_map/all_gather | solution.py:243
  19.7 1.7 %collective-permute-start.3 = (bf16[448,256]{1,0:T(8,128)(2,1)}, bf16[448,256]{1,0:T(8,128)(2,1)S(1)}, u32[]{:S(2)}, u32[]{:S(2)}) collective-permute-start(bf16[448,256]{1,0:T(8,128)(2,1)} %bitcast.24), channel_id=1, source_target_pairs={{0,2},{1,3},{2,0},{3,1},{4,6},{5,7},{6,4},{7,5},{8,10},{9,11},{10,... | collective-permute-start | bytes 688136 | tf_op jit(solution)/shard_map/ppermute | solution.py:218
  21.4 1.0 %copy-done.1 = bf16[256,576]{0,1:T(8,128)(2,1)S(1)} copy-done((bf16[256,576]{0,1:T(8,128)(2,1)S(1)}, bf16[256,576]{0,1:T(8,128)(2,1)}, u32[]{:S(2)}) %copy-start.1) | copy-done | bytes 294936
  22.4 1.1 %copy-done.4 = bf16[576,448]{0,1:T(8,128)(2,1)S(1)} copy-done((bf16[576,448]{0,1:T(8,128)(2,1)S(1)}, bf16[576,448]{0,1:T(8,128)(2,1)}, u32[]{:S(2)}) %copy-start.4) | copy-done | bytes 516120
  23.4 0.9 %copy-done.6 = bf16[256,256]{1,0:T(8,128)(2,1)S(1)} copy-done((bf16[256,256]{1,0:T(8,128)(2,1)S(1)}, bf16[256,256]{1,0:T(8,128)(2,1)}, u32[]{:S(2)}) %copy-start.6) | copy-done | bytes 131096
  24.3 0.7 copy-done.22
  25.0 1.5 %shard_map.147 = (f32[448,128]{1,0:T(8,128)S(1)}, bf16[2,128,128]{2,1,0:T(8,128)(2,1)S(1)}) custom-call(s32[1]{0:T(128)} %bitcast.7.core_ref, s32[2]{0:T(128)S(1)} %copy-done.22, bf16[256,256]{1,0:T(8,128)(2,1)S(1)} %copy-done.6, bf16[256,256]{1,0:T(8,128)(2,1)S(1)} %all_gather.10.k_ref, bf16[576,256]{1,0:T(8,128)(2,1)S(1)} %bitcast.21, ...), custom_call_target="tpu_custom_call" | custom-call | flops 1000000 | bytes 1000000 | tf_op jit(solution)/shard_map/pallas_call | solution.py:246
  26.5 0.6 copy-done.17
  27.1 0.3 collective-permute-start.7
  27.4 1.1 %copy-done.5 = bf16[448,576]{1,0:T(8,128)(2,1)S(1)} copy-done((bf16[448,576]{1,0:T(8,128)(2,1)S(1)}, bf16[448,576]{1,0:T(8,128)(2,1)}, u32[]{:S(2)}) %copy-start.5) | copy-done | bytes 516120
  28.5 1.6 %shard_map.149 = f32[576,128]{1,0:T(8,128)S(1)} custom-call(s32[1]{0:T(128)} %bitcast.7.core_ref, bf16[448,256]{1,0:T(8,128)(2,1)S(1)} %bitcast.25, bf16[448,256]{1,0:T(8,128)(2,1)S(1)} %collective-permute-done.2.refs_1_.mate_s, bf16[448,576]{1,0:T(8,128)(2,1)S(1)} %copy-done.5, bf16[448,576]{1,0:T(8,128)(2,1)} %collective-permute-done.15.mate_w), custom_call_target="tpu_custom_call" | custom-call | flops 1000000 | bytes 1000000 | tf_op jit(solution)/shard_map/pallas_call | solution.py:235
  30.1 1.8 %collective-permute-start.16 = (f32[576,128]{1,0:T(8,128)S(1)}, f32[576,128]{1,0:T(8,128)S(1)}, u32[]{:S(2)}, u32[]{:S(2)}) collective-permute-start(f32[576,128]{1,0:T(8,128)S(1)} %shard_map.149), channel_id=1, source_target_pairs={{0,2},{1,3},{2,0},{3,1},{4,6},{5,7},{6,4},{7,5},{8,10},{9,11},{10,... | collective-permute-start | bytes 884744 | tf_op jit(solution)/shard_map/ppermute | solution.py:218
  31.9 0.5 collective-permute-start.6
  32.4 3.2 %collective-permute-done.7 = f32[448,128]{1,0:T(8,128)S(1)} collective-permute-done((f32[448,128]{1,0:T(8,128)S(1)}, f32[448,128]{1,0:T(8,128)S(1)}, u32[]{:S(2)}, u32[]{:S(2)}) %collective-permute-start.7) | collective-permute-done | bytes 229408 | tf_op jit(solution)/shard_map/ppermute | solution.py:218
  35.6 3.7 %collective-permute-start.13 = (bf16[448,128]{1,0:T(8,128)(2,1)S(1)}, bf16[448,128]{1,0:T(8,128)(2,1)S(1)}, u32[]{:S(2)}, u32[]{:S(2)}) collective-permute-start(bf16[448,128]{1,0:T(8,128)(2,1)S(1)} %add_convert_fusion.1.refs_0_), channel_id=1, source_target_pairs={{0,12},{4,0},{8,4},{12,8},{1,13},{5,1},{9,5},{13,9},{2,14},{6,2},{... | collective-permute-start | bytes 344072 | tf_op jit(solution)/shard_map/ppermute | solution.py:224
  39.3 1.0 %collective-permute-start.9 = (bf16[448,128]{1,0:T(8,128)(2,1)S(1)}, bf16[448,128]{1,0:T(8,128)(2,1)S(1)}, u32[]{:S(2)}, u32[]{:S(2)}) collective-permute-start(bf16[448,128]{1,0:T(8,128)(2,1)S(1)} %add_convert_fusion.1.refs_0_), channel_id=1, source_target_pairs={{0,4},{4,8},{8,12},{12,0},{1,5},{5,9},{9,13},{13,1},{2,6},{6,10},{... | collective-permute-start | bytes 344072 | tf_op jit(solution)/shard_map/ppermute | solution.py:224
  40.3 0.7 collective-permute-done.16
  41.1 3.7 %collective-permute-start.22 = (bf16[576,128]{1,0:T(8,128)(2,1)S(1)}, bf16[576,128]{1,0:T(8,128)(2,1)}, u32[]{:S(2)}, u32[]{:S(2)}) collective-permute-start(bf16[576,128]{1,0:T(8,128)(2,1)S(1)} %add_convert_fusion.refs_8_), channel_id=1, source_target_pairs={{0,12},{4,0},{8,4},{12,8},{1,13},{5,1},{9,5},{13,9},{2,14},{6,2},{... | collective-permute-start | bytes 442376 | tf_op jit(solution)/shard_map/ppermute | solution.py:224
  44.7 2.0 %collective-permute-start.20 = (bf16[576,128]{1,0:T(8,128)(2,1)S(1)}, bf16[576,128]{1,0:T(8,128)(2,1)}, u32[]{:S(2)}, u32[]{:S(2)}) collective-permute-start(bf16[576,128]{1,0:T(8,128)(2,1)S(1)} %add_convert_fusion.refs_8_), channel_id=1, source_target_pairs={{0,8},{4,12},{8,0},{12,4},{1,9},{5,13},{9,1},{13,5},{2,10},{6,14},... | collective-permute-start | bytes 442376 | tf_op jit(solution)/shard_map/ppermute | solution.py:224
  46.7 4.5 %collective-permute-done.11.refs_4_ = bf16[448,128]{1,0:T(8,128)(2,1)S(1)} collective-permute-done((bf16[448,128]{1,0:T(8,128)(2,1)S(1)}, bf16[448,128]{1,0:T(8,128)(2,1)S(1)}, u32[]{:S(2)}, u32[]{:S(2)}) %collective-permute-start.11) | collective-permute-done | bytes 114720 | tf_op jit(solution)/shard_map/ppermute | solution.py:224
  51.2 0.1 collective-permute-start.17
  51.3 0.6 copy-done.15
  52.0 0.5 collective-permute-start.14
  52.5 8.7 %collective-permute-done.20.refs_12_ = bf16[576,128]{1,0:T(8,128)(2,1)} collective-permute-done((bf16[576,128]{1,0:T(8,128)(2,1)S(1)}, bf16[576,128]{1,0:T(8,128)(2,1)}, u32[]{:S(2)}, u32[]{:S(2)}) %collective-permute-start.20) | collective-permute-done | bytes 147488 | tf_op jit(solution)/shard_map/ppermute | solution.py:224
  61.3 0.6 collective-permute-start.19
  61.8 0.1 collective-permute-start.12
  62.0 0.4 collective-permute-start.10
  62.3 0.6 stack.41.index_ref
  62.9 0.1 pad_add_fusion.index_ref
  63.0 0.9 %copy-done.8 = bf16[448,256]{1,0:T(8,128)(2,1)S(1)} copy-done((bf16[448,256]{1,0:T(8,128)(2,1)S(1)}, bf16[448,256]{1,0:T(8,128)(2,1)}, u32[]{:S(2)}) %copy-start.8) | copy-done | bytes 229400
  64.0 0.9 %copy-done.10 = bf16[448,256]{1,0:T(8,128)(2,1)S(1)} copy-done((bf16[448,256]{1,0:T(8,128)(2,1)S(1)}, bf16[448,256]{1,0:T(8,128)(2,1)}, u32[]{:S(2)}) %copy-start.10) | copy-done | bytes 229400
  64.9 0.8 copy-done.18
  65.8 3.4 %shard_map.148 = (f32[256,512]{1,0:T(8,128)S(1)}, f32[256,512]{1,0:T(8,128)S(1)}) custom-call(s32[4]{0:T(128)S(1)} %pad_add_fusion.index_ref, bf16[2,128,128]{2,1,0:T(8,128)(2,1)S(1)} %copy-done.18, bf16[448,256]{1,0:T(8,128)(2,1)S(1)} %bitcast.26, bf16[448,256]{1,0:T(8,128)(2,1)S(1)} %collective-permute-done.2.refs_1_.mate_s, ...), custom_call_target="tpu_custom_call" | custom-call | flops 1000000 | bytes 1000000 | tf_op jit(solution)/shard_map/pallas_call | solution.py:272
  69.3 4.4 %shard_map.150 = (f32[256,512]{1,0:T(8,128)S(1)}, f32[256,512]{1,0:T(8,128)S(1)}, f32[8,256]{1,0:T(8,128)S(1)}) custom-call(s32[6]{0:T(128)S(1)} %copy-done.21, s32[1,256]{1,0:T(1,128)S(1)} %bitcast.29, s32[1,256]{1,0:T(1,128)S(1)} %bitcast.31, f32[256,512]{1,0:T(8,128)S(1)} %get-tuple-element.16.s_own.so_ref, ...), custom_call_target="tpu_custom_call" | custom-call | flops 1000000 | bytes 1000000 | tf_op jit(solution)/shard_map/pallas_call | solution.py:288
  73.7 5.2 %all_gather.11.in_ref = f32[32,256]{1,0:T(8,128)S(1)} all-gather(f32[8,256]{1,0:T(8,128)S(1)} %get-tuple-element.21), channel_id=1, replica_groups=mesh['grp'=2,'sv'=4,'tv'=4] {'tv'}, dimensions={0}, use_global_device_ids=true | all-gather | bytes 40960 | tf_op jit(solution)/shard_map/all_gather | solution.py:298
  78.9 0.4 collective-permute-start.26
  79.3 1.1 %collective-permute-start.25 = (f32[8,256]{1,0:T(8,128)S(1)}, f32[8,256]{1,0:T(8,128)S(1)}, u32[]{:S(2)}, u32[]{:S(2)}) collective-permute-start(f32[8,256]{1,0:T(8,128)S(1)} %shard_map.151.refs_0_), channel_id=1, source_target_pairs={{0,8},{4,12},{8,0},{12,4},{1,9},{5,13},{9,1},{13,5},{2,10},{6,14},... | collective-permute-start | bytes 24584 | tf_op jit(solution)/shard_map/ppermute | solution.py:224
  80.4 1.9 %collective-permute-start.24 = (f32[8,256]{1,0:T(8,128)S(1)}, f32[8,256]{1,0:T(8,128)S(1)}, u32[]{:S(2)}, u32[]{:S(2)}) collective-permute-start(f32[8,256]{1,0:T(8,128)S(1)} %shard_map.151.refs_0_), channel_id=1, source_target_pairs={{0,4},{4,8},{8,12},{12,0},{1,5},{5,9},{9,13},{13,1},{2,6},{6,10},{... | collective-permute-start | bytes 24584 | tf_op jit(solution)/shard_map/ppermute | solution.py:224
  82.4 0.3 collective-permute-done.26.refs_3_
  82.7 1.2 %collective-permute-done.25.refs_2_ = f32[8,256]{1,0:T(8,128)S(1)} collective-permute-done((f32[8,256]{1,0:T(8,128)S(1)}, f32[8,256]{1,0:T(8,128)S(1)}, u32[]{:S(2)}, u32[]{:S(2)}) %collective-permute-start.25) | collective-permute-done | bytes 8224 | tf_op jit(solution)/shard_map/ppermute | solution.py:224
  83.9 2.0 %collective-permute-done.24.refs_1_ = f32[8,256]{1,0:T(8,128)S(1)} collective-permute-done((f32[8,256]{1,0:T(8,128)S(1)}, f32[8,256]{1,0:T(8,128)S(1)}, u32[]{:S(2)}, u32[]{:S(2)}) %collective-permute-start.24) | collective-permute-done | bytes 8224 | tf_op jit(solution)/shard_map/ppermute | solution.py:224
  85.9 2.0 %shard_map.152 = (f32[1,256]{1,0:T(1,128)}, f32[1,256]{1,0:T(1,128)}, bf16[256,512]{1,0:T(8,128)(2,1)}, bf16[256,512]{1,0:T(8,128)(2,1)}) custom-call(s32[1]{0:T(128)} %bitcast.index_ref, s32[2]{0:T(128)S(1)} %copy-done.23, s32[1,256]{1,0:T(1,128)S(1)} %bitcast.30, s32[1,256]{1,0:T(1,128)S(1)} %bitcast.32, f32[256,512]{1,0:T(8,128)S(1)} %get-tuple-element.16.s_own.so_ref, ...), custom_call_target="tpu_custom_call" | custom-call | flops 1000000 | bytes 1000000 | tf_op jit(solution)/shard_map/pallas_call | solution.py:307
  (67 shorter events, 0.3 us)
Async XLA Ops:
  0.6 26.8 %copy-start.3 = (bf16[256,448]{0,1:T(8,128)(2,1)S(1)}, bf16[256,448]{0,1:T(8,128)(2,1)}, u32[]{:S(2)}) copy-start(bf16[256,448]{0,1:T(8,128)(2,1)} %param.12) | copy-start | bytes 688132
  0.6 20.8 %collective-permute-start.1 = (bf16[448,576]{1,0:T(8,128)(2,1)}, bf16[448,576]{1,0:T(8,128)(2,1)S(1)}, u32[]{:S(2)}, u32[]{:S(2)}) collective-permute-start(bf16[448,576]{1,0:T(8,128)(2,1)} %bitcast.27), channel_id=1, source_target_pairs={{0,1},{1,0},{2,3},{3,2},{4,5},{5,4},{6,7},{7,6},{8,9},{9,8},{10,11... | collective-permute-start | bytes 1548296 | tf_op jit(solution)/shard_map/ppermute | solution.py:214
  1.2 26.3 %collective-permute-start.15 = (bf16[448,576]{1,0:T(8,128)(2,1)}, bf16[448,576]{1,0:T(8,128)(2,1)}, u32[]{:S(2)}, u32[]{:S(2)}) collective-permute-start(bf16[448,576]{1,0:T(8,128)(2,1)} %own_w.1), channel_id=1, source_target_pairs={{0,1},{1,0},{2,3},{3,2},{4,5},{5,4},{6,7},{7,6},{8,9},{9,8},{10,11... | collective-permute-start | bytes 1548296 | tf_op jit(solution)/shard_map/ppermute | solution.py:214
  1.2 18.5 %collective-permute-start = (bf16[576,256]{1,0:T(8,128)(2,1)}, bf16[576,256]{1,0:T(8,128)(2,1)S(1)}, u32[]{:S(2)}, u32[]{:S(2)}) collective-permute-start(bf16[576,256]{1,0:T(8,128)(2,1)} %bitcast.19), channel_id=1, source_target_pairs={{0,1},{1,0},{2,3},{3,2},{4,5},{5,4},{6,7},{7,6},{8,9},{9,8},{10,11... | collective-permute-start | bytes 884744 | tf_op jit(solution)/shard_map/ppermute | solution.py:214
  1.7 30.2 %collective-permute-start.5 = (bf16[576,256]{1,0:T(8,128)(2,1)}, bf16[576,256]{1,0:T(8,128)(2,1)}, u32[]{:S(2)}, u32[]{:S(2)}) collective-permute-start(bf16[576,256]{1,0:T(8,128)(2,1)} %bitcast.20), channel_id=1, source_target_pairs={{0,2},{1,3},{2,0},{3,1},{4,6},{5,7},{6,4},{7,5},{8,10},{9,11},{10,... | collective-permute-start | bytes 884744 | tf_op jit(solution)/shard_map/ppermute | solution.py:218
  4.2 23.2 %collective-permute-start.2 = (bf16[448,256]{1,0:T(8,128)(2,1)}, bf16[448,256]{1,0:T(8,128)(2,1)S(1)}, u32[]{:S(2)}, u32[]{:S(2)}) collective-permute-start(bf16[448,256]{1,0:T(8,128)(2,1)} %bitcast.23), channel_id=1, source_target_pairs={{0,1},{1,0},{2,3},{3,2},{4,5},{5,4},{6,7},{7,6},{8,9},{9,8},{10,11... | collective-permute-start | bytes 688136 | tf_op jit(solution)/shard_map/ppermute | solution.py:214
  19.7 12.2 %collective-permute-start.3 = (bf16[448,256]{1,0:T(8,128)(2,1)}, bf16[448,256]{1,0:T(8,128)(2,1)S(1)}, u32[]{:S(2)}, u32[]{:S(2)}) collective-permute-start(bf16[448,256]{1,0:T(8,128)(2,1)} %bitcast.24), channel_id=1, source_target_pairs={{0,2},{1,3},{2,0},{3,1},{4,6},{5,7},{6,4},{7,5},{8,10},{9,11},{10,... | collective-permute-start | bytes 688136 | tf_op jit(solution)/shard_map/ppermute | solution.py:218
  21.4 1.0 %copy-start.1 = (bf16[256,576]{0,1:T(8,128)(2,1)S(1)}, bf16[256,576]{0,1:T(8,128)(2,1)}, u32[]{:S(2)}) copy-start(bf16[256,576]{0,1:T(8,128)(2,1)} %param.13) | copy-start | bytes 884740
  22.4 1.1 %copy-start.4 = (bf16[576,448]{0,1:T(8,128)(2,1)S(1)}, bf16[576,448]{0,1:T(8,128)(2,1)}, u32[]{:S(2)}) copy-start(bf16[576,448]{0,1:T(8,128)(2,1)} %param.21) | copy-start | bytes 1548292
  23.4 0.9 %copy-start.6 = (bf16[256,256]{1,0:T(8,128)(2,1)S(1)}, bf16[256,256]{1,0:T(8,128)(2,1)}, u32[]{:S(2)}) copy-start(bf16[256,256]{1,0:T(8,128)(2,1)} %all_gather.9.q_ref) | copy-start | bytes 393220
  25.0 38.0 %copy-start = (bf16[1792,512]{1,0:T(8,128)(2,1)S(1)}, bf16[1792,512]{1,0:T(8,128)(2,1)}, u32[]{:S(2)}) copy-start(bf16[1792,512]{1,0:T(8,128)(2,1)} %refs_16_.1) | copy-start | bytes 5505028
  25.0 38.0 %copy-start.2 = (bf16[256,576]{0,1:T(8,128)(2,1)S(1)}, bf16[256,576]{0,1:T(8,128)(2,1)}, u32[]{:S(2)}) copy-start(bf16[256,576]{0,1:T(8,128)(2,1)} %param.13) | copy-start | bytes 884740
  27.1 8.5 %collective-permute-start.7 = (f32[448,128]{1,0:T(8,128)S(1)}, f32[448,128]{1,0:T(8,128)S(1)}, u32[]{:S(2)}, u32[]{:S(2)}) collective-permute-start(f32[448,128]{1,0:T(8,128)S(1)} %get-tuple-element.18), channel_id=1, source_target_pairs={{0,2},{1,3},{2,0},{3,1},{4,6},{5,7},{6,4},{7,5},{8,10},{9,11},{10,... | collective-permute-start | bytes 688136 | tf_op jit(solution)/shard_map/ppermute | solution.py:218
  27.4 1.1 %copy-start.5 = (bf16[448,576]{1,0:T(8,128)(2,1)S(1)}, bf16[448,576]{1,0:T(8,128)(2,1)}, u32[]{:S(2)}) copy-start(bf16[448,576]{1,0:T(8,128)(2,1)} %own_w.1) | copy-start | bytes 1548292
  30.1 10.9 %collective-permute-start.16 = (f32[576,128]{1,0:T(8,128)S(1)}, f32[576,128]{1,0:T(8,128)S(1)}, u32[]{:S(2)}, u32[]{:S(2)}) collective-permute-start(f32[576,128]{1,0:T(8,128)S(1)} %shard_map.149), channel_id=1, source_target_pairs={{0,2},{1,3},{2,0},{3,1},{4,6},{5,7},{6,4},{7,5},{8,10},{9,11},{10,... | collective-permute-start | bytes 884744 | tf_op jit(solution)/shard_map/ppermute | solution.py:218
  31.9 29.4 %copy-start.7 = (bf16[448,256]{1,0:T(8,128)(2,1)}, bf16[448,256]{1,0:T(8,128)(2,1)S(1)}, u32[]{:S(2)}) copy-start(bf16[448,256]{1,0:T(8,128)(2,1)S(1)} %collective-permute-done.3.refs_2_) | copy-start | bytes 688132
  31.9 7.4 %collective-permute-start.4 = (bf16[448,256]{1,0:T(8,128)(2,1)S(1)}, bf16[448,256]{1,0:T(8,128)(2,1)S(1)}, u32[]{:S(2)}, u32[]{:S(2)}) collective-permute-start(bf16[448,256]{1,0:T(8,128)(2,1)S(1)} %collective-permute-done.3.refs_2_), channel_id=1, source_target_pairs={{0,1},{1,0},{2,3},{3,2},{4,5},{5,4},{6,7},{7,6},{8,9},{9,8},{10,11... | collective-permute-start | bytes 688136 | tf_op jit(solution)/shard_map/ppermute | solution.py:214
  31.9 9.2 %collective-permute-start.6 = (bf16[576,256]{1,0:T(8,128)(2,1)}, bf16[576,256]{1,0:T(8,128)(2,1)S(1)}, u32[]{:S(2)}, u32[]{:S(2)}) collective-permute-start(bf16[576,256]{1,0:T(8,128)(2,1)} %collective-permute-done.5.refs_6_), channel_id=1, source_target_pairs={{0,1},{1,0},{2,3},{3,2},{4,5},{5,4},{6,7},{7,6},{8,9},{9,8},{10,11... | collective-permute-start | bytes 884744 | tf_op jit(solution)/shard_map/ppermute | solution.py:214
  35.6 9.1 %collective-permute-start.13 = (bf16[448,128]{1,0:T(8,128)(2,1)S(1)}, bf16[448,128]{1,0:T(8,128)(2,1)S(1)}, u32[]{:S(2)}, u32[]{:S(2)}) collective-permute-start(bf16[448,128]{1,0:T(8,128)(2,1)S(1)} %add_convert_fusion.1.refs_0_), channel_id=1, source_target_pairs={{0,12},{4,0},{8,4},{12,8},{1,13},{5,1},{9,5},{13,9},{2,14},{6,2},{... | collective-permute-start | bytes 344072 | tf_op jit(solution)/shard_map/ppermute | solution.py:224
  39.2 12.0 %collective-permute-start.11 = (bf16[448,128]{1,0:T(8,128)(2,1)S(1)}, bf16[448,128]{1,0:T(8,128)(2,1)S(1)}, u32[]{:S(2)}, u32[]{:S(2)}) collective-permute-start(bf16[448,128]{1,0:T(8,128)(2,1)S(1)} %add_convert_fusion.1.refs_0_), channel_id=1, source_target_pairs={{0,8},{4,12},{8,0},{12,4},{1,9},{5,13},{9,1},{13,5},{2,10},{6,14},... | collective-permute-start | bytes 344072 | tf_op jit(solution)/shard_map/ppermute | solution.py:224
  39.3 22.0 %copy-start.9 = (bf16[448,256]{1,0:T(8,128)(2,1)}, bf16[448,256]{1,0:T(8,128)(2,1)S(1)}, u32[]{:S(2)}) copy-start(bf16[448,256]{1,0:T(8,128)(2,1)S(1)} %collective-permute-done.4.refs_3_) | copy-start | bytes 688132
  39.3 12.0 %collective-permute-start.9 = (bf16[448,128]{1,0:T(8,128)(2,1)S(1)}, bf16[448,128]{1,0:T(8,128)(2,1)S(1)}, u32[]{:S(2)}, u32[]{:S(2)}) collective-permute-start(bf16[448,128]{1,0:T(8,128)(2,1)S(1)} %add_convert_fusion.1.refs_0_), channel_id=1, source_target_pairs={{0,4},{4,8},{8,12},{12,0},{1,5},{5,9},{9,13},{13,1},{2,6},{6,10},{... | collective-permute-start | bytes 344072 | tf_op jit(solution)/shard_map/ppermute | solution.py:224
  41.0 10.3 %collective-permute-start.8 = (bf16[448,128]{1,0:T(8,128)(2,1)S(1)}, bf16[448,128]{1,0:T(8,128)(2,1)S(1)}, u32[]{:S(2)}, u32[]{:S(2)}) collective-permute-start(bf16[448,128]{1,0:T(8,128)(2,1)S(1)} %add_convert_fusion.1.refs_0_), channel_id=1, source_target_pairs={{0,1},{1,0},{2,3},{3,2},{4,5},{5,4},{6,7},{7,6},{8,9},{9,8},{10,11... | collective-permute-start | bytes 344072 | tf_op jit(solution)/shard_map/ppermute | solution.py:214
  41.1 11.4 %collective-permute-start.22 = (bf16[576,128]{1,0:T(8,128)(2,1)S(1)}, bf16[576,128]{1,0:T(8,128)(2,1)}, u32[]{:S(2)}, u32[]{:S(2)}) collective-permute-start(bf16[576,128]{1,0:T(8,128)(2,1)S(1)} %add_convert_fusion.refs_8_), channel_id=1, source_target_pairs={{0,12},{4,0},{8,4},{12,8},{1,13},{5,1},{9,5},{13,9},{2,14},{6,2},{... | collective-permute-start | bytes 442376 | tf_op jit(solution)/shard_map/ppermute | solution.py:224
  44.7 16.5 %collective-permute-start.20 = (bf16[576,128]{1,0:T(8,128)(2,1)S(1)}, bf16[576,128]{1,0:T(8,128)(2,1)}, u32[]{:S(2)}, u32[]{:S(2)}) collective-permute-start(bf16[576,128]{1,0:T(8,128)(2,1)S(1)} %add_convert_fusion.refs_8_), channel_id=1, source_target_pairs={{0,8},{4,12},{8,0},{12,4},{1,9},{5,13},{9,1},{13,5},{2,10},{6,14},... | collective-permute-start | bytes 442376 | tf_op jit(solution)/shard_map/ppermute | solution.py:224
  51.2 10.0 %copy-start.11 = (bf16[448,128]{1,0:T(8,128)(2,1)}, bf16[448,128]{1,0:T(8,128)(2,1)S(1)}, u32[]{:S(2)}) copy-start(bf16[448,128]{1,0:T(8,128)(2,1)S(1)} %collective-permute-done.11.refs_4_) | copy-start | bytes 344068
  51.2 10.0 %collective-permute-start.18 = (bf16[576,128]{1,0:T(8,128)(2,1)S(1)}, bf16[576,128]{1,0:T(8,128)(2,1)}, u32[]{:S(2)}, u32[]{:S(2)}) collective-permute-start(bf16[576,128]{1,0:T(8,128)(2,1)S(1)} %add_convert_fusion.refs_8_), channel_id=1, source_target_pairs={{0,4},{4,8},{8,12},{12,0},{1,5},{5,9},{9,13},{13,1},{2,6},{6,10},{... | collective-permute-start | bytes 442376 | tf_op jit(solution)/shard_map/ppermute | solution.py:224
  51.2 10.0 %copy-start.13 = (bf16[448,128]{1,0:T(8,128)(2,1)}, bf16[448,128]{1,0:T(8,128)(2,1)S(1)}, u32[]{:S(2)}) copy-start(bf16[448,128]{1,0:T(8,128)(2,1)S(1)} %collective-permute-done.9.refs_2_) | copy-start | bytes 344068
  51.2 10.6 %collective-permute-start.17 = (bf16[576,128]{1,0:T(8,128)(2,1)S(1)}, bf16[576,128]{1,0:T(8,128)(2,1)}, u32[]{:S(2)}, u32[]{:S(2)}) collective-permute-start(bf16[576,128]{1,0:T(8,128)(2,1)S(1)} %add_convert_fusion.refs_8_), channel_id=1, source_target_pairs={{0,1},{1,0},{2,3},{3,2},{4,5},{5,4},{6,7},{7,6},{8,9},{9,8},{10,11... | collective-permute-start | bytes 442376 | tf_op jit(solution)/shard_map/ppermute | solution.py:214
  52.0 10.0 %collective-permute-start.14 = (bf16[448,128]{1,0:T(8,128)(2,1)S(1)}, bf16[448,128]{1,0:T(8,128)(2,1)}, u32[]{:S(2)}, u32[]{:S(2)}) collective-permute-start(bf16[448,128]{1,0:T(8,128)(2,1)S(1)} %collective-permute-done.13.refs_6_), channel_id=1, source_target_pairs={{0,1},{1,0},{2,3},{3,2},{4,5},{5,4},{6,7},{7,6},{8,9},{9,8},{10,11... | collective-permute-start | bytes 344072 | tf_op jit(solution)/shard_map/ppermute | solution.py:214
  52.5 16.7 %collective-permute-start.23 = (bf16[576,128]{1,0:T(8,128)(2,1)}, bf16[576,128]{1,0:T(8,128)(2,1)}, u32[]{:S(2)}, u32[]{:S(2)}) collective-permute-start(bf16[576,128]{1,0:T(8,128)(2,1)} %collective-permute-done.22.refs_14_), channel_id=1, source_target_pairs={{0,1},{1,0},{2,3},{3,2},{4,5},{5,4},{6,7},{7,6},{8,9},{9,8},{10,11... | collective-permute-start | bytes 442376 | tf_op jit(solution)/shard_map/ppermute | solution.py:214
  61.2 8.0 %collective-permute-start.21 = (bf16[576,128]{1,0:T(8,128)(2,1)}, bf16[576,128]{1,0:T(8,128)(2,1)}, u32[]{:S(2)}, u32[]{:S(2)}) collective-permute-start(bf16[576,128]{1,0:T(8,128)(2,1)} %collective-permute-done.20.refs_12_), channel_id=1, source_target_pairs={{0,1},{1,0},{2,3},{3,2},{4,5},{5,4},{6,7},{7,6},{8,9},{9,8},{10,11... | collective-permute-start | bytes 442376 | tf_op jit(solution)/shard_map/ppermute | solution.py:214
  61.3 7.9 %collective-permute-start.19 = (bf16[576,128]{1,0:T(8,128)(2,1)}, bf16[576,128]{1,0:T(8,128)(2,1)}, u32[]{:S(2)}, u32[]{:S(2)}) collective-permute-start(bf16[576,128]{1,0:T(8,128)(2,1)} %collective-permute-done.18.refs_10_), channel_id=1, source_target_pairs={{0,1},{1,0},{2,3},{3,2},{4,5},{5,4},{6,7},{7,6},{8,9},{9,8},{10,11... | collective-permute-start | bytes 442376 | tf_op jit(solution)/shard_map/ppermute | solution.py:214
  61.8 7.3 %collective-permute-start.12 = (bf16[448,128]{1,0:T(8,128)(2,1)}, bf16[448,128]{1,0:T(8,128)(2,1)}, u32[]{:S(2)}, u32[]{:S(2)}) collective-permute-start(bf16[448,128]{1,0:T(8,128)(2,1)} %copy-done.11), channel_id=1, source_target_pairs={{0,1},{1,0},{2,3},{3,2},{4,5},{5,4},{6,7},{7,6},{8,9},{9,8},{10,11... | collective-permute-start | bytes 344072 | tf_op jit(solution)/shard_map/ppermute | solution.py:214
  62.0 7.2 %collective-permute-start.10 = (bf16[448,128]{1,0:T(8,128)(2,1)}, bf16[448,128]{1,0:T(8,128)(2,1)}, u32[]{:S(2)}, u32[]{:S(2)}) collective-permute-start(bf16[448,128]{1,0:T(8,128)(2,1)} %copy-done.13), channel_id=1, source_target_pairs={{0,1},{1,0},{2,3},{3,2},{4,5},{5,4},{6,7},{7,6},{8,9},{9,8},{10,11... | collective-permute-start | bytes 344072 | tf_op jit(solution)/shard_map/ppermute | solution.py:214
  63.0 0.9 %copy-start.8 = (bf16[448,256]{1,0:T(8,128)(2,1)S(1)}, bf16[448,256]{1,0:T(8,128)(2,1)}, u32[]{:S(2)}) copy-start(bf16[448,256]{1,0:T(8,128)(2,1)} %copy-done.7) | copy-start | bytes 688132
  64.0 0.9 %copy-start.10 = (bf16[448,256]{1,0:T(8,128)(2,1)S(1)}, bf16[448,256]{1,0:T(8,128)(2,1)}, u32[]{:S(2)}) copy-start(bf16[448,256]{1,0:T(8,128)(2,1)} %copy-done.9) | copy-start | bytes 688132
  64.9 0.8 copy-start.18
  65.7 3.5 %copy-start.12 = (bf16[448,128]{1,0:T(8,128)(2,1)S(1)}, bf16[448,128]{1,0:T(8,128)(2,1)}, u32[]{:S(2)}) copy-start(bf16[448,128]{1,0:T(8,128)(2,1)} %copy-done.11) | copy-start | bytes 344068
  65.7 3.5 %copy-start.14 = (bf16[448,128]{1,0:T(8,128)(2,1)S(1)}, bf16[448,128]{1,0:T(8,128)(2,1)}, u32[]{:S(2)}) copy-start(bf16[448,128]{1,0:T(8,128)(2,1)} %copy-done.13) | copy-start | bytes 344068
  65.7 3.5 %copy-start.16 = (bf16[448,128]{1,0:T(8,128)(2,1)S(1)}, bf16[448,128]{1,0:T(8,128)(2,1)}, u32[]{:S(2)}) copy-start(bf16[448,128]{1,0:T(8,128)(2,1)} %copy-done.15) | copy-start | bytes 344068
  65.7 3.5 %copy-start.19 = (s32[256]{0:T(256)S(1)}, s32[256]{0:T(256)}, u32[]{:S(2)}) copy-start(s32[256]{0:T(256)} %param.16) | copy-start | bytes 3076
  65.7 3.5 %copy-start.20 = (s32[256]{0:T(256)S(1)}, s32[256]{0:T(256)}, u32[]{:S(2)}) copy-start(s32[256]{0:T(256)} %param.17) | copy-start | bytes 3076
  65.8 3.5 %copy-start.21 = (s32[6]{0:T(128)S(1)}, s32[6]{0:T(128)}, u32[]{:S(2)}) copy-start(s32[6]{0:T(128)} %stack.41.index_ref) | copy-start | bytes 76
  69.3 16.6 %copy-start.23 = (s32[2]{0:T(128)S(1)}, s32[2]{0:T(128)}, u32[]{:S(2)}) copy-start(s32[2]{0:T(128)} %lens_ref.3) | copy-start | bytes 28
  78.9 3.7 %collective-permute-start.26 = (f32[8,256]{1,0:T(8,128)S(1)}, f32[8,256]{1,0:T(8,128)S(1)}, u32[]{:S(2)}, u32[]{:S(2)}) collective-permute-start(f32[8,256]{1,0:T(8,128)S(1)} %shard_map.151.refs_0_), channel_id=1, source_target_pairs={{0,12},{4,0},{8,4},{12,8},{1,13},{5,1},{9,5},{13,9},{2,14},{6,2},{... | collective-permute-start | bytes 24584 | tf_op jit(solution)/shard_map/ppermute | solution.py:224
  79.3 4.5 %collective-permute-start.25 = (f32[8,256]{1,0:T(8,128)S(1)}, f32[8,256]{1,0:T(8,128)S(1)}, u32[]{:S(2)}, u32[]{:S(2)}) collective-permute-start(f32[8,256]{1,0:T(8,128)S(1)} %shard_map.151.refs_0_), channel_id=1, source_target_pairs={{0,8},{4,12},{8,0},{12,4},{1,9},{5,13},{9,1},{13,5},{2,10},{6,14},... | collective-permute-start | bytes 24584 | tf_op jit(solution)/shard_map/ppermute | solution.py:224
  80.4 5.4 %collective-permute-start.24 = (f32[8,256]{1,0:T(8,128)S(1)}, f32[8,256]{1,0:T(8,128)S(1)}, u32[]{:S(2)}, u32[]{:S(2)}) collective-permute-start(f32[8,256]{1,0:T(8,128)S(1)} %shard_map.151.refs_0_), channel_id=1, source_target_pairs={{0,4},{4,8},{8,12},{12,0},{1,5},{5,9},{9,13},{13,1},{2,6},{6,10},{... | collective-permute-start | bytes 24584 | tf_op jit(solution)/shard_map/ppermute | solution.py:224
  (3 other events, 1.9 us)

commit v2 on v1

v2 whole, which is shorter than its diff:
```python
import functools

import jax
import jax.numpy as jnp
from jax import lax
from jax.experimental import pallas as pl
from jax.experimental.pallas import tpu as pltpu
from jax.sharding import PartitionSpec as P

DK = 256
FLOOR = -1e30
CORES = 2
STATS = 8
F32 = jnp.float32
BF16 = jnp.bfloat16

VMEM = pl.BlockSpec(memory_space=pltpu.VMEM)
SMEM = pl.BlockSpec(memory_space=pltpu.SMEM)
HBM = pl.BlockSpec(memory_space=pltpu.HBM)


def shape(dims, dtype=F32):
    return jax.ShapeDtypeStruct(dims, dtype)


def kernel_call(body, out_shape, in_specs, scratch=(), limit=32):
    single = not isinstance(out_shape, (tuple, list))
    return pl.pallas_call(
        body,
        out_shape=out_shape,
        in_specs=in_specs,
        out_specs=VMEM if single else [VMEM] * len(out_shape),
        scratch_shapes=list(scratch),
        compiler_params=pltpu.CompilerParams(vmem_limit_bytes=limit * 2**20),

    )


def dot00(a, b):
    return lax.dot_general(a, b, (((0,), (0,)), ((), ())), preferred_element_type=F32)


def dot10(a, b):
    return lax.dot_general(a, b, (((1,), (0,)), ((), ())), preferred_element_type=F32)


def part_of(index, width):
    return pl.ds(pl.multiple_of(index * width, width), width)


def behind(axis, offset):
    count = lax.axis_size(axis)
    return lax.rem(lax.axis_index(axis) - offset + count, count)


def vocab_base(vocab):
    place = lax.axis_index("sv") * lax.axis_size("x") + lax.axis_index("x")
    return (place * CORES + lax.axis_index("core")) * vocab


def fetch(sems, *pairs):
    copies = [pltpu.make_async_copy(a, b, sems.at[n]) for n, (a, b) in enumerate(pairs)]
    for copy in copies:
        copy.start()
    return copies


def pack_kernel(q_ref, k_ref, out_ref, sems):
    rows = q_ref.shape[0]
    for copy in fetch(sems, (q_ref, out_ref.at[:rows]), (k_ref, out_ref.at[rows:])):
        copy.wait()


def project(states, matrix, *out_refs):
    *shares, total = out_refs
    total[...] = dot00(matrix[...], states[:, part_of(lax.axis_index("core"), total.shape[1])])
    rows = shares[0].shape[0]
    for n, share in enumerate(shares):
        share[...] = total[part_of(behind("x", lax.axis_size("x") - n), rows), :]


def collect(axis, *refs):
    *blocks, out_ref = refs
    rows = blocks[0].shape[0]
    for n, block in enumerate(blocks):
        out_ref[part_of(behind(axis, n), rows), :] = block[...]


def attend(blocks, lens_ref, states, matrix, *refs):
    qk_refs = refs[:blocks]
    out_ref, weights_ref, q_all, k_all = refs[blocks:]
    rows = qk_refs[0].shape[0] // 2
    for n, ref in enumerate(qk_refs):
        q_all[n * rows : (n + 1) * rows, :] = ref[:rows]
        k_all[n * rows : (n + 1) * rows, :] = ref[rows:]
    sequences = lens_ref.shape[0]
    width = q_all.shape[1] // sequences
    for s in range(sequences):
        tokens = slice(s * width, (s + 1) * width)
        scores = dot00(k_all[:, tokens], q_all[:, tokens]) * DK ** (-0.5)
        position = lax.broadcasted_iota(jnp.int32, scores.shape, 0)
        scores = jnp.where(position < lens_ref[s], scores, FLOOR)
        raised = jnp.exp(scores - jnp.max(scores, axis=0, keepdims=True))
        weights_ref[s] = (raised / jnp.sum(raised, axis=0, keepdims=True)).astype(BF16)
    per_core = sequences // CORES
    rows, cols = states.shape[0] // CORES, out_ref.shape[0]
    for n in range(per_core):
        s = lax.axis_index("core") * per_core + n
        aligned = dot10(states[:, part_of(s, width)], weights_ref[s]).astype(BF16)
        total = sum(
            dot10(matrix[c * cols : (c + 1) * cols, :], aligned[c * rows : (c + 1) * rows])
            for c in range(CORES)
        )
        out_ref[:, n * width : (n + 1) * width] = total


def log_total(logits):
    highest = jnp.max(logits, axis=1, keepdims=True)
    raised = jnp.exp(logits - highest)
    summed = jnp.sum(raised, axis=1, keepdims=True)
    return raised, summed, highest + jnp.log(summed)


def target_column(ref, base):
    row = jnp.broadcast_to((ref[...] - base).astype(F32), (STATS, ref.shape[1]))
    return jnp.transpose(row)[:, 0:1].astype(jnp.int32)


def pick(logits, columns):
    lane = lax.broadcasted_iota(jnp.int32, logits.shape, 1)
    return jnp.sum(jnp.where(lane == columns, logits, 0.0), axis=1, keepdims=True)


def pack_columns(columns):
    lane = lax.broadcasted_iota(jnp.int32, (columns[0].shape[0], 128), 1)
    packed = jnp.zeros(lane.shape, F32)
    for k, column in enumerate(columns):
        packed = jnp.where(lane == k, column, packed)
    return packed


def own_student(targets, *refs):
    *blocks, head, out_ref, notes_ref, s_all = refs
    collect("x", *blocks, s_all)
    logits = dot00(s_all[...], head[...])
    out_ref[...] = logits
    columns = target_column(targets, vocab_base(head.shape[1]))
    _, _, total = log_total(logits)
    notes_ref[...] = pack_columns((total, pick(logits, columns)))


def own_teacher(weights_ref, *refs):
    *blocks, head, own_ref, t_all = refs
    sequences, width, _ = weights_ref.shape
    rows = blocks[0].shape[0]
    for n, block in enumerate(blocks):
        for s in range(sequences):
            tokens = slice(s * width, (s + 1) * width)
            aligned = dot10(block[:, tokens], weights_ref[s]).astype(BF16)
            t_all[part_of(behind("x", n), rows), tokens] = aligned
    own_ref[...] = dot00(t_all[...], head[...])


def mapped_teacher(targets, own_ref, *refs):
    *shares, head, mapped_ref, stats_ref, t_all = refs
    parts, blocks = len(shares), lax.axis_size("sv")
    width = shares[0].shape[1]
    rows = shares[0].shape[0] // (CORES * blocks)
    for n, share in enumerate(shares):
        part = behind("x", n) if parts > 1 else 0
        for c in range(CORES):
            tokens = slice(c * width, (c + 1) * width)
            for z in range(blocks):
                place = (c * blocks + z) * rows
                t_all[part_of(z * parts + part, rows), tokens] = share[place : place + rows, :]
    mapped = dot00(t_all[...], head[...])
    mapped_ref[...] = mapped
    own = own_ref[...]
    columns = target_column(targets, vocab_base(head.shape[1]))
    raised, summed, own_total = log_total(own)
    _, _, mapped_total = log_total(mapped)
    spread = jnp.sum(raised * (own - mapped), axis=1, keepdims=True) / summed
    zero = jnp.zeros_like(spread)
    columns = (zero, zero, own_total, mapped_total, zero, zero, spread, pick(mapped, columns))
    stats_ref[...] = jnp.transpose(pack_columns(columns))[:STATS]


def student_side(targets, t_stats, own_ref, notes_ref, halves, head, mapped_ref, stats_ref):
    rows = halves.shape[0] // CORES
    states = jnp.concatenate([halves[:rows], halves[rows:]], axis=1)
    mapped = dot00(states, head[...])
    mapped_ref[...] = mapped
    columns = target_column(targets, vocab_base(head.shape[1]))
    raised, summed, total = log_total(mapped)
    spread = jnp.sum(raised * (mapped - own_ref[...]), axis=1, keepdims=True) / summed
    zero = jnp.zeros_like(spread)
    picked = notes_ref[:, 1:2] + pick(mapped, columns)
    columns = (notes_ref[:, 0:1], total, zero, zero, spread, picked)
    stats_ref[...] = jnp.transpose(pack_columns(columns))[:STATS] + t_stats[...]


def merge_stats(parts):
    highest = parts[0]
    for part in parts[1:]:
        highest = jnp.maximum(highest, part)
    total = highest + jnp.log(sum(jnp.exp(part - highest) for part in parts))
    shares = [jnp.exp(part - total) for part in parts]
    s_spread = sum(share[1:2] * part[4:5] for share, part in zip(shares, parts))
    s_picked = sum(part[5:6] for part in parts)
    t_spread = sum(share[2:3] * part[6:7] for share, part in zip(shares, parts))
    t_picked = sum(part[7:8] for part in parts)
    return total, s_spread, s_picked, t_spread, t_picked


def merge_kernel(parts, in_ref, out_ref):
    total, *rest = merge_stats([in_ref[n * STATS : (n + 1) * STATS, :] for n in range(parts)])
    row = lax.broadcasted_iota(jnp.int32, total.shape, 0)
    for k, value in enumerate(rest):
        total = jnp.where(row == 4 + k, value, total)
    out_ref[...] = total


def finish(parts, lens_ref, s_targets, t_targets, so_ref, sm_ref, to_ref, tm_ref, *refs):
    s_loss, t_loss, s_grad, t_grad = refs[parts:]
    totals, s_spread, s_picked, t_spread, t_picked = merge_stats([ref[...] for ref in refs[:parts]])
    so, sm, to, tm = (totals[k : k + 1] for k in range(4))
    rows = s_loss.shape[1]
    sequences = lens_ref.shape[0]
    width = rows // sequences

    def live(dims, dim):
        place = lax.broadcasted_iota(jnp.int32, dims, dim)
        mask = jnp.zeros(dims, jnp.bool_)
        for s in range(sequences):
            mask |= (place >= s * width) & (place < s * width + lens_ref[s])
        return mask.astype(F32)

    live_row = live((1, rows), 1)
    s_loss[...] = live_row * (so + sm - s_picked + (s_spread - sm + so))
    t_loss[...] = live_row * ((t_spread - to + tm) + tm - t_picked)
    turned = jnp.transpose(totals)
    live_column = live((rows, 1), 0)
    base = vocab_base(so_ref.shape[1])
    lane = lax.broadcasted_iota(jnp.int32, so_ref.shape, 1)
    s_hot = (lane == target_column(s_targets, base)).astype(F32)
    t_hot = (lane == target_column(t_targets, base)).astype(F32)
    so_chance = jnp.exp(so_ref[...] - turned[:, 0:1])
    sm_chance = jnp.exp(sm_ref[...] - turned[:, 1:2])
    to_chance = jnp.exp(to_ref[...] - turned[:, 2:3])
    tm_chance = jnp.exp(tm_ref[...] - turned[:, 3:4])
    s_grad[...] = (live_column * (2.0 * so_chance - s_hot - sm_chance)).astype(BF16)
    t_grad[...] = (live_column * (2.0 * tm_chance - to_chance - t_hot)).astype(BF16)


def after(values, *needs):
    return lax.optimization_barrier((tuple(values), needs))[0]


def body(
    student_states,
    teacher_states,
    student_queries,
    teacher_keys,
    student_targets,
    teacher_targets,
    student_lengths,
    teacher_lengths,
    to_teacher,
    to_student,
    student_head,
    teacher_head,
):
    rows = student_states.shape[0]
    chips, sv_count = lax.axis_size("x"), lax.axis_size("sv")
    vocab = student_head.shape[1]
    tokens = rows // CORES
    sequences = teacher_lengths.shape[0]
    width = rows // sequences
    dma = pltpu.SemaphoreType.DMA

    def both(a):
        return lax.all_gather(a, "core", axis=0, tiled=True)

    def shift(a, axis, n):
        count = lax.axis_size(axis)
        return lax.ppermute(a, axis, [(i, (i + n) % count) for i in range(count)])

    def around(a, axis):
        return [shift(a, axis, n) for n in range(1, lax.axis_size(axis))]

    def cross(a, n):
        pairs = [(2 * i + c, (2 * (i + n) + 1 - c) % (CORES * chips)) for i in range(chips) for c in range(CORES)]
        return lax.ppermute(a, ("x", "core"), pairs)

    s_t, t_t = student_states.T, teacher_states.T
    w_t, w_s = to_teacher, to_student.T
    s_targets, t_targets = student_targets.reshape(1, rows), teacher_targets.reshape(1, rows)

    q_t, k_t = student_queries.T, teacher_keys.T
    qk = kernel_call(
        pack_kernel, shape((2 * q_t.shape[0], rows), BF16), [HBM] * 2, [dma((2,))], limit=60
    )(q_t, k_t)
    qk_blocks = [qk] + around(qk, "x") + [cross(qk, n) for n in range(chips)]
    chip_s, chip_w_t = (both(a) for a in after((s_t, w_t), qk))
    far_s, far_t = after((s_t, t_t), qk)
    far_s, far_t = around(far_s, "x"), around(far_t, "x")
    split = chips if w_t.shape[1] % (16 * chips) == 0 else 1
    share = shape((w_t.shape[1] // split, tokens))
    (chip_s, chip_w_t), qk_blocks = lax.optimization_barrier(((chip_s, chip_w_t), qk_blocks))
    *parts_t, _ = kernel_call(
        project, [share] * split + [shape((w_t.shape[1], tokens))], [VMEM] * 2
    )(chip_s, chip_w_t)

    t_out, w_out, *parts_t = lax.optimization_barrier((t_t, w_s, *parts_t))
    other_t = [shift(parts_t[n % split], "x", n) for n in range(1, chips)]
    chip_t, chip_w_s = both(t_out), both(w_out)
    features = q_t.shape[0] * chips * CORES
    part_s, weights = kernel_call(
        functools.partial(attend, len(qk_blocks)),
        (shape((w_s.shape[0], tokens)), shape((sequences, width, width), BF16)),
        [SMEM] + [VMEM] * (2 + len(qk_blocks)),
        [pltpu.VMEM((features, rows), BF16)] * 2,
    )(teacher_lengths, chip_t, chip_w_s, *qk_blocks)

    own_part, *other_t, part_s = lax.optimization_barrier((parts_t[0], *other_t, part_s))
    into_t = functools.reduce(jnp.add, other_t, own_part).astype(BF16)
    into_t = [into_t] + around(into_t, "sv")
    other_s = around(part_s, "x")

    far_s, far_t = [both(a) for a in far_s], [both(a) for a in far_t]

    *into_t, part_s = lax.optimization_barrier((*into_t, part_s))
    other_s = after(other_s, *into_t)
    into_s = functools.reduce(jnp.add, other_s, part_s).astype(BF16)
    into_s = [into_s] + around(into_s, "sv")
    into_t = kernel_call(
        functools.partial(collect, "sv"),
        shape((sv_count * into_t[0].shape[0], tokens), BF16),
        [VMEM] * sv_count,
    )(*into_t)
    t_shares = [into_t] + (around(into_t, "x") if split > 1 else [])
    t_shares = [both(a) for a in lax.optimization_barrier(tuple(t_shares))]
    s_blocks = [chip_s] + far_s
    t_blocks = [chip_t] + far_t
    logits = shape((rows, vocab))
    s_own, s_notes = kernel_call(
        own_student,
        (logits, shape((rows, 128))),
        [VMEM] * (2 + chips),
        [pltpu.VMEM((student_head.shape[0], rows), BF16)],
    )(s_targets, *s_blocks, student_head)
    t_own = kernel_call(
        own_teacher,
        logits,
        [VMEM] * (2 + chips),
        [pltpu.VMEM((teacher_head.shape[0], rows), BF16)],
    )(weights, *t_blocks, teacher_head)
    t_mapped, t_stats = kernel_call(
        mapped_teacher,
        (logits, shape((STATS, rows))),
        [VMEM] * (3 + len(t_shares)),
        [pltpu.VMEM((teacher_head.shape[0], rows), BF16)],
    )(t_targets, t_own, *t_shares, teacher_head)

    into_s = kernel_call(
        functools.partial(collect, "sv"),
        shape((sv_count * into_s[0].shape[0], tokens), BF16),
        [VMEM] * sv_count,
    )(*into_s)
    s_mapped, stats = kernel_call(
        student_side, (logits, shape((STATS, rows))), [VMEM] * 6
    )(s_targets, t_stats, s_own, s_notes, both(into_s), student_head)

    stats = lax.all_gather(stats, ("x", "core"), axis=0, tiled=True)
    stats = kernel_call(
        functools.partial(merge_kernel, chips * CORES), shape((STATS, rows)), [VMEM]
    )(stats)
    stats = [stats] + around(stats, "sv")
    s_loss, t_loss, s_grad, t_grad = kernel_call(
        functools.partial(finish, sv_count),
        (shape((1, rows)), shape((1, rows)), shape((rows, vocab), BF16), shape((rows, vocab), BF16)),
        [SMEM] + [VMEM] * (6 + sv_count),
    )(student_lengths, s_targets, t_targets, s_own, s_mapped, t_own, t_mapped, *stats)
    return s_loss.reshape(rows), t_loss.reshape(rows), s_grad, t_grad


def solution(mesh):
    grp, sv, tv = (mesh.shape[name] for name in ("grp", "sv", "tv"))
    devices = mesh.devices.reshape(grp, sv, tv // CORES, CORES)
    mesh = jax.sharding.Mesh(devices, ("grp", "sv", "x", "core"))
    tv = ("x", "core")
    columns = ("sv", "x", "core")
    in_specs = (P("grp", tv),) * 4 + (P("grp"),) * 4
    in_specs += (P(tv, "sv"),) * 2 + (P(None, columns),) * 2
    out_specs = (P("grp"), P("grp"), P("grp", columns), P("grp", columns))
    return jax.shard_map(body, mesh=mesh, in_specs=in_specs, out_specs=out_specs, check_vma=False)
```

time: 88.5 us -> 71.5 us (0.81)
  waiting for transfers between devices: 20.7 us -> 8.61 us
  local copies, waits for them, and re-layouts: 9.26 us -> 0.04 us
  blocking collectives: 20.5 us -> 26.2 us
  Pallas kernels: 13 us -> 11.4 us
    ppermute x27 -> x17, waiting for transfers between devices: 20.7 us -> 8.61 us  [the longest x15 8.61 us: shift(): return lax.ppermute(a, axis, [(i, (i + n) % count) for i in range(count)])]
    unnamed x48 -> x20, local copies, waits for them, and re-layouts: 8.67 us -> 0.04 us
    all_gather x3 -> x10, blocking collectives: 20.5 us -> 26.2 us  [the longest x9 21 us: both(): return lax.all_gather(a, 'core', axis=0, tiled=True)]
    pallas_call x6 -> x11, Pallas kernels: 13 us -> 11.4 us  [the longest x1 2.05 us: body(): kernel_call(functools.partial(finish, sv_count), (shape((1, rows)), shape...]
    ppermute x27 -> x17, starting transfers between devices: 23.5 us -> 24.2 us  [the longest x15 24 us: shift(): return lax.ppermute(a, axis, [(i, (i + n) % count) for i in range(count)])]
  transfers between devices with their start and end apart: 27 -> 17, of which waited for: 7 -> 6; matrix products, arithmetic and copies ran while one was open for 1% -> 0% of each run, Pallas kernels for 7% -> 7%
where the time goes in v2:
time: 71.5 us; the launch traced here: 71.2 us
  blocking collectives  26.2 us (37%)
  starting transfers between devices  24.2 us (34%)
  Pallas kernels  11.4 us (16%)
  waiting for transfers between devices  8.61 us (12%)
  between operations  0.76 us (1%)
    ppermute x15, starting transfers between devices, shift(): return lax.ppermute(a, axis, [(i, (i + n) % count) for i in range(count)])  24 us
    all_gather x9, blocking collectives, both(): return lax.all_gather(a, 'core', axis=0, tiled=True)  21 us
    ppermute x15, waiting for transfers between devices, shift(): return lax.ppermute(a, axis, [(i, (i + n) % count) for i in range(count)])  8.61 us
    all_gather x1, blocking collectives, body(): stats = lax.all_gather(stats, ('x', 'core'), axis=0, tiled=True)  5.18 us
    pallas_call x1, Pallas kernels, body(): kernel_call(functools.partial(finish, sv_count), (shape((1, rows)), shape...  2.05 us
    pallas_call x1, Pallas kernels, body(): kernel_call(functools.partial(attend, len(qk_blocks)), (shape((w_s.shape[...  1.48 us
    pallas_call x1, Pallas kernels, body(): kernel_call(pack_kernel, shape((2 * q_t.shape[0], rows), BF16), [HBM] * 2...  1.46 us
  transfers between devices with their start and end apart: 17, of which 6 were waited for; matrix products, arithmetic and copies ran while one was open for 0% of the time, Pallas kernels for 7%

profile of v2, /device:TPU:0, one launch (start us, length us, event | category | flops | bytes accessed | tf_op | source)
XLA Modules:
  0.0 71.2 jit_solution(13671021412336607134)
XLA Ops:
  0.6 0.0 copy-start.9
  0.6 1.5 %shard_map.147.refs_0_ = bf16[128,256]{1,0:T(8,128)(2,1)} custom-call(bf16[64,256]{1,0:T(8,128)(2,1)} %bitcast.19, bf16[64,256]{1,0:T(8,128)(2,1)} %bitcast.20), custom_call_target="tpu_custom_call" | custom-call | tf_op jit(solution)/shard_map/pallas_call | solution.py:300
  2.1 3.0 %collective-permute-start = (bf16[128,256]{1,0:T(8,128)(2,1)}, bf16[128,256]{1,0:T(8,128)(2,1)S(1)}, u32[]{:S(2)}, u32[]{:S(2)}) collective-permute-start(bf16[128,256]{1,0:T(8,128)(2,1)} %shard_map.147.refs_0_), channel_id=1, source_target_pairs={{0,2},{2,0},{1,3},{3,1},{4,6},{6,4},{5,7},{7,5},{8,10},{10,8},{9,1... | collective-permute-start | bytes 196616 | tf_op jit(solution)/shard_map/ppermute | solution.py:286
  5.1 0.0 collective-permute-start.1
  5.1 0.2 collective-permute-start.2
  5.3 1.9 %collective-permute-start.3 = (bf16[448,256]{1,0:T(8,128)(2,1)}, bf16[448,256]{1,0:T(8,128)(2,1)S(1)}, u32[]{:S(2)}, u32[]{:S(2)}) collective-permute-start(bf16[448,256]{1,0:T(8,128)(2,1)} %bitcast.17), channel_id=1, source_target_pairs={{0,2},{2,0},{1,3},{3,1},{4,6},{6,4},{5,7},{7,5},{8,10},{10,8},{9,1... | collective-permute-start | bytes 688136 | tf_op jit(solution)/shard_map/ppermute | solution.py:286
  7.3 0.1 collective-permute-start.4
  7.4 2.8 %all_gather.31.matrix = bf16[896,576]{1,0:T(8,128)(2,1)S(1)} all-gather(bf16[448,576]{1,0:T(8,128)(2,1)} %param.20), channel_id=1, replica_groups=mesh['grp'=2,'sv'=4,'x'=2,'core'=2] {'core'}, dimensions={0}, use_global_device_ids=true | all-gather | bytes 1548288 | tf_op jit(solution)/shard_map/all_gather | solution.py:282
  10.2 2.1 %all_gather.30.refs_0_.states = bf16[896,256]{1,0:T(8,128)(2,1)S(1)} all-gather(bf16[448,256]{1,0:T(8,128)(2,1)S(1)} %bitcast.18), channel_id=1, replica_groups=mesh['grp'=2,'sv'=4,'x'=2,'core'=2] {'core'}, dimensions={0}, use_global_device_ids=true | all-gather | bytes 688128 | tf_op jit(solution)/shard_map/all_gather | solution.py:282
  12.3 0.0 collective-permute-done.refs_1_
  12.3 0.0 collective-permute-done.2.refs_3_
  12.3 1.2 %shard_map.149 = (f32[288,128]{1,0:T(8,128)S(1)}, f32[288,128]{1,0:T(8,128)S(1)}, f32[576,128]{1,0:T(8,128)}) custom-call(bf16[896,256]{1,0:T(8,128)(2,1)S(1)} %all_gather.30.refs_0_.states, bf16[896,576]{1,0:T(8,128)(2,1)S(1)} %all_gather.31.matrix), custom_call_target="tpu_custom_call" | custom-call | tf_op jit(solution)/shard_map/pallas_call | solution.py:310
  13.6 2.6 %all_gather.34.matrix = bf16[896,576]{1,0:T(8,128)(2,1)S(1)} all-gather(bf16[448,576]{1,0:T(8,128)(2,1)S(1)} %bitcast.14), channel_id=1, replica_groups=mesh['grp'=2,'sv'=4,'x'=2,'core'=2] {'core'}, dimensions={0}, use_global_device_ids=true | all-gather | bytes 1548288 | tf_op jit(solution)/shard_map/all_gather | solution.py:282
  16.2 1.9 %collective-permute-start.5 = (f32[288,128]{1,0:T(8,128)S(1)}, f32[288,128]{1,0:T(8,128)S(1)}, u32[]{:S(2)}, u32[]{:S(2)}) collective-permute-start(f32[288,128]{1,0:T(8,128)S(1)} %get-tuple-element.60), channel_id=1, source_target_pairs={{0,2},{2,0},{1,3},{3,1},{4,6},{6,4},{5,7},{7,5},{8,10},{10,8},{9,1... | collective-permute-start | bytes 442376 | tf_op jit(solution)/shard_map/ppermute | solution.py:286
  18.1 2.2 %all_gather.33.states.refs_0_ = bf16[1152,256]{1,0:T(8,128)(2,1)S(1)} all-gather(bf16[576,256]{1,0:T(8,128)(2,1)S(1)} %bitcast.16), channel_id=1, replica_groups=mesh['grp'=2,'sv'=4,'x'=2,'core'=2] {'core'}, dimensions={0}, use_global_device_ids=true | all-gather | bytes 884736 | tf_op jit(solution)/shard_map/all_gather | solution.py:282
  20.4 1.5 %shard_map.150 = (f32[448,128]{1,0:T(8,128)S(1)}, bf16[2,128,128]{2,1,0:T(8,128)(2,1)S(1)}) custom-call(s32[2]{0:T(128)S(1)} %copy-done.5, bf16[1152,256]{1,0:T(8,128)(2,1)S(1)} %all_gather.33.states.refs_0_, bf16[896,576]{1,0:T(8,128)(2,1)S(1)} %all_gather.34.matrix, bf16[128,256]{1,0:T(8,128)(2,1)S(1)} %copy-done.2, ...), custom_call_target="tpu_custom_call" | custom-call | tf_op jit(solution)/shard_map/pallas_call | solution.py:318
  21.9 2.3 %collective-permute-done.5 = f32[288,128]{1,0:T(8,128)S(1)} collective-permute-done((f32[288,128]{1,0:T(8,128)S(1)}, f32[288,128]{1,0:T(8,128)S(1)}, u32[]{:S(2)}, u32[]{:S(2)}) %collective-permute-start.5) | collective-permute-done | bytes 147488 | tf_op jit(solution)/shard_map/ppermute | solution.py:286
  24.1 1.1 %collective-permute-start.10 = (f32[448,128]{1,0:T(8,128)S(1)}, f32[448,128]{1,0:T(8,128)S(1)}, u32[]{:S(2)}, u32[]{:S(2)}) collective-permute-start(f32[448,128]{1,0:T(8,128)S(1)} %get-tuple-element.73), channel_id=1, source_target_pairs={{0,2},{2,0},{1,3},{3,1},{4,6},{6,4},{5,7},{7,5},{8,10},{10,8},{9,1... | collective-permute-start | bytes 688136 | tf_op jit(solution)/shard_map/ppermute | solution.py:286
  25.2 1.8 %collective-permute-start.6 = (bf16[288,128]{1,0:T(8,128)(2,1)S(1)}, bf16[288,128]{1,0:T(8,128)(2,1)S(1)}, u32[]{:S(2)}, u32[]{:S(2)}) collective-permute-start(bf16[288,128]{1,0:T(8,128)(2,1)S(1)} %add_convert_fusion.1.refs_0_), channel_id=1, source_target_pairs={{0,4},{4,8},{8,12},{12,0},{1,5},{5,9},{9,13},{13,1},{2,6},{6,10},{... | collective-permute-start | bytes 221192 | tf_op jit(solution)/shard_map/ppermute | solution.py:286
  27.0 2.6 %collective-permute-start.7 = (bf16[288,128]{1,0:T(8,128)(2,1)S(1)}, bf16[288,128]{1,0:T(8,128)(2,1)S(1)}, u32[]{:S(2)}, u32[]{:S(2)}) collective-permute-start(bf16[288,128]{1,0:T(8,128)(2,1)S(1)} %add_convert_fusion.1.refs_0_), channel_id=1, source_target_pairs={{0,8},{4,12},{8,0},{12,4},{1,9},{5,13},{9,1},{13,5},{2,10},{6,14},... | collective-permute-start | bytes 221192 | tf_op jit(solution)/shard_map/ppermute | solution.py:286
  29.6 0.0 collective-permute-done.3
  29.6 1.3 %collective-permute-start.8 = (bf16[288,128]{1,0:T(8,128)(2,1)S(1)}, bf16[288,128]{1,0:T(8,128)(2,1)S(1)}, u32[]{:S(2)}, u32[]{:S(2)}) collective-permute-start(bf16[288,128]{1,0:T(8,128)(2,1)S(1)} %add_convert_fusion.1.refs_0_), channel_id=1, source_target_pairs={{0,12},{4,0},{8,4},{12,8},{1,13},{5,1},{9,5},{13,9},{2,14},{6,2},{... | collective-permute-start | bytes 221192 | tf_op jit(solution)/shard_map/ppermute | solution.py:286
  30.9 2.1 %all_gather.32.refs_1_ = bf16[896,256]{1,0:T(8,128)(2,1)S(1)} all-gather(bf16[448,256]{1,0:T(8,128)(2,1)S(1)} %collective-permute-done.3), channel_id=1, replica_groups=mesh['grp'=2,'sv'=4,'x'=2,'core'=2] {'core'}, dimensions={0}, use_global_device_ids=true | all-gather | bytes 688128 | tf_op jit(solution)/shard_map/all_gather | solution.py:282
  33.1 0.9 %shard_map.148 = (f32[256,512]{1,0:T(8,128)S(1)}, f32[256,128]{1,0:T(8,128)S(1)}) custom-call(s32[1,256]{1,0:T(1,128)S(1)} %bitcast.9, bf16[896,256]{1,0:T(8,128)(2,1)S(1)} %all_gather.30.refs_0_.states, bf16[896,256]{1,0:T(8,128)(2,1)S(1)} %all_gather.32.refs_1_, bf16[1792,512]{1,0:T(8,128)(2,1)S(1)} %copy-done.1), custom_call_target="tpu_custom_call" | custom-call | tf_op jit(solution)/shard_map/pallas_call | solution.py:346
  34.0 0.0 collective-permute-done.6.refs_1_
  34.0 0.4 collective-permute-done.7.refs_2_
  34.5 0.9 %collective-permute-start.9 = (bf16[1152,128]{1,0:T(8,128)(2,1)S(1)}, bf16[1152,128]{1,0:T(8,128)(2,1)S(1)}, u32[]{:S(2)}, u32[]{:S(2)}) collective-permute-start(bf16[1152,128]{1,0:T(8,128)(2,1)S(1)} %shard_map.152), channel_id=1, source_target_pairs={{0,2},{2,0},{1,3},{3,1},{4,6},{6,4},{5,7},{7,5},{8,10},{10,8},{9,1... | collective-permute-start | bytes 884744 | tf_op jit(solution)/shard_map/ppermute | solution.py:286
  35.5 1.5 %collective-permute-start.11 = (bf16[448,128]{1,0:T(8,128)(2,1)S(1)}, bf16[448,128]{1,0:T(8,128)(2,1)S(1)}, u32[]{:S(2)}, u32[]{:S(2)}) collective-permute-start(bf16[448,128]{1,0:T(8,128)(2,1)S(1)} %add_convert_fusion.refs_0_), channel_id=1, source_target_pairs={{0,4},{4,8},{8,12},{12,0},{1,5},{5,9},{9,13},{13,1},{2,6},{6,10},{... | collective-permute-start | bytes 344072 | tf_op jit(solution)/shard_map/ppermute | solution.py:286
  36.9 1.9 %collective-permute-start.12 = (bf16[448,128]{1,0:T(8,128)(2,1)S(1)}, bf16[448,128]{1,0:T(8,128)(2,1)S(1)}, u32[]{:S(2)}, u32[]{:S(2)}) collective-permute-start(bf16[448,128]{1,0:T(8,128)(2,1)S(1)} %add_convert_fusion.refs_0_), channel_id=1, source_target_pairs={{0,8},{4,12},{8,0},{12,4},{1,9},{5,13},{9,1},{13,5},{2,10},{6,14},... | collective-permute-start | bytes 344072 | tf_op jit(solution)/shard_map/ppermute | solution.py:286
  38.9 0.5 collective-permute-start.13
  39.4 0.0 collective-permute-done.4
  39.4 2.2 %all_gather.35.refs_1_ = bf16[1152,256]{1,0:T(8,128)(2,1)S(1)} all-gather(bf16[576,256]{1,0:T(8,128)(2,1)S(1)} %collective-permute-done.4), channel_id=1, replica_groups=mesh['grp'=2,'sv'=4,'x'=2,'core'=2] {'core'}, dimensions={0}, use_global_device_ids=true | all-gather | bytes 884736 | tf_op jit(solution)/shard_map/all_gather | solution.py:282
  41.6 1.3 %shard_map.151.own_ref.to_ref = f32[256,512]{1,0:T(8,128)S(1)} custom-call(bf16[2,128,128]{2,1,0:T(8,128)(2,1)S(1)} %get-tuple-element.57.weights_ref, bf16[1152,256]{1,0:T(8,128)(2,1)S(1)} %all_gather.33.states.refs_0_, bf16[1152,256]{1,0:T(8,128)(2,1)S(1)} %all_gather.35.refs_1_, bf16[2304,512]{1,0:T(8,128)(2,1)S(1)} %copy-done), custom_call_target="tpu_custom_call" | custom-call | tf_op jit(solution)/shard_map/pallas_call | solution.py:352
  42.9 0.0 copy-start.4
  43.0 0.5 collective-permute-done.11.refs_1_
  43.5 3.3 %collective-permute-done.12.refs_2_ = bf16[448,128]{1,0:T(8,128)(2,1)S(1)} collective-permute-done((bf16[448,128]{1,0:T(8,128)(2,1)S(1)}, bf16[448,128]{1,0:T(8,128)(2,1)S(1)}, u32[]{:S(2)}, u32[]{:S(2)}) %collective-permute-start.12) | collective-permute-done | bytes 114720 | tf_op jit(solution)/shard_map/ppermute | solution.py:286
  46.8 2.5 %all_gather.38.halves = bf16[3584,128]{1,0:T(8,128)(2,1)S(1)} all-gather(bf16[1792,128]{1,0:T(8,128)(2,1)S(1)} %shard_map.154), channel_id=1, replica_groups=mesh['grp'=2,'sv'=4,'x'=2,'core'=2] {'core'}, dimensions={0}, use_global_device_ids=true | all-gather | bytes 1376256 | tf_op jit(solution)/shard_map/all_gather | solution.py:282
  49.3 2.2 %all_gather.36.refs_0_ = bf16[2304,128]{1,0:T(8,128)(2,1)S(1)} all-gather(bf16[1152,128]{1,0:T(8,128)(2,1)S(1)} %shard_map.152), channel_id=1, replica_groups=mesh['grp'=2,'sv'=4,'x'=2,'core'=2] {'core'}, dimensions={0}, use_global_device_ids=true | all-gather | bytes 884736 | tf_op jit(solution)/shard_map/all_gather | solution.py:282
  51.5 2.2 %all_gather.37.refs_1_ = bf16[2304,128]{1,0:T(8,128)(2,1)S(1)} all-gather(bf16[1152,128]{1,0:T(8,128)(2,1)S(1)} %collective-permute-done.9), channel_id=1, replica_groups=mesh['grp'=2,'sv'=4,'x'=2,'core'=2] {'core'}, dimensions={0}, use_global_device_ids=true | all-gather | bytes 884736 | tf_op jit(solution)/shard_map/all_gather | solution.py:282
  53.7 1.3 %shard_map.153 = (f32[256,512]{1,0:T(8,128)S(1)}, f32[8,256]{1,0:T(8,128)S(1)}) custom-call(s32[1,256]{1,0:T(1,128)S(1)} %bitcast.12, f32[256,512]{1,0:T(8,128)S(1)} %shard_map.151.own_ref.to_ref, bf16[2304,128]{1,0:T(8,128)(2,1)S(1)} %all_gather.36.refs_0_, bf16[2304,128]{1,0:T(8,128)(2,1)S(1)} %all_gather.37.refs_1_, bf16[2304,512]{1,0:T(8,128)(2,1)S(1)} %copy-done), custom_call_target="tpu_custom_call" | custom-call | tf_op jit(solution)/shard_map/pallas_call | solution.py:358
  55.1 1.4 %shard_map.155 = (f32[256,512]{1,0:T(8,128)S(1)}, f32[8,256]{1,0:T(8,128)S(1)}) custom-call(s32[1,256]{1,0:T(1,128)S(1)} %bitcast.10, f32[8,256]{1,0:T(8,128)S(1)} %get-tuple-element.71.t_stats, f32[256,512]{1,0:T(8,128)S(1)} %get-tuple-element.47.own_ref.so_ref, f32[256,128]{1,0:T(8,128)S(1)} %get-tuple-element.72.notes_ref, ...), custom_call_target="tpu_custom_call" | custom-call | tf_op jit(solution)/shard_map/pallas_call | solution.py:370
  56.5 5.2 %all_gather.39.in_ref = f32[32,256]{1,0:T(8,128)S(1)} all-gather(f32[8,256]{1,0:T(8,128)S(1)} %get-tuple-element.77), channel_id=1, replica_groups=mesh['grp'=2,'sv'=4,'x'=2,'core'=2] {'x','core'}, dimensions={0}, use_global_device_ids=true | all-gather | bytes 40960 | tf_op jit(solution)/shard_map/all_gather | solution.py:374
  61.7 3.0 %collective-permute-start.14 = (f32[8,256]{1,0:T(8,128)S(1)}, f32[8,256]{1,0:T(8,128)S(1)}, u32[]{:S(2)}, u32[]{:S(2)}) collective-permute-start(f32[8,256]{1,0:T(8,128)S(1)} %shard_map.156.refs_0_), channel_id=1, source_target_pairs={{0,4},{4,8},{8,12},{12,0},{1,5},{5,9},{9,13},{13,1},{2,6},{6,10},{... | collective-permute-start | bytes 24584 | tf_op jit(solution)/shard_map/ppermute | solution.py:286
  64.6 0.4 collective-permute-start.15
  65.0 2.1 %collective-permute-start.16 = (f32[8,256]{1,0:T(8,128)S(1)}, f32[8,256]{1,0:T(8,128)S(1)}, u32[]{:S(2)}, u32[]{:S(2)}) collective-permute-start(f32[8,256]{1,0:T(8,128)S(1)} %shard_map.156.refs_0_), channel_id=1, source_target_pairs={{0,12},{4,0},{8,4},{12,8},{1,13},{5,1},{9,5},{13,9},{2,14},{6,2},{... | collective-permute-start | bytes 24584 | tf_op jit(solution)/shard_map/ppermute | solution.py:286
  67.1 0.1 collective-permute-done.14.refs_1_
  67.2 2.0 %collective-permute-done.15.refs_2_ = f32[8,256]{1,0:T(8,128)S(1)} collective-permute-done((f32[8,256]{1,0:T(8,128)S(1)}, f32[8,256]{1,0:T(8,128)S(1)}, u32[]{:S(2)}, u32[]{:S(2)}) %collective-permute-start.15) | collective-permute-done | bytes 8224 | tf_op jit(solution)/shard_map/ppermute | solution.py:286
  69.2 2.1 %shard_map.157 = (f32[1,256]{1,0:T(1,128)}, f32[1,256]{1,0:T(1,128)}, bf16[256,512]{1,0:T(8,128)(2,1)}, bf16[256,512]{1,0:T(8,128)(2,1)}) custom-call(s32[2]{0:T(128)S(1)} %copy-done.6, s32[1,256]{1,0:T(1,128)S(1)} %bitcast.11, s32[1,256]{1,0:T(1,128)S(1)} %bitcast.13, f32[256,512]{1,0:T(8,128)S(1)} %get-tuple-element.47.own_ref.so_ref, ...), custom_call_target="tpu_custom_call" | custom-call | tf_op jit(solution)/shard_map/pallas_call | solution.py:379
  (29 shorter events, 0.2 us)
Async XLA Ops:
  0.6 9.5 %copy-start.9 = (bf16[256,448]{0,1:T(8,128)(2,1)S(1)}, bf16[256,448]{0,1:T(8,128)(2,1)}, u32[]{:S(2)}) copy-start(bf16[256,448]{0,1:T(8,128)(2,1)} %param.12) | copy-start | bytes 688132
  2.1 10.2 %collective-permute-start = (bf16[128,256]{1,0:T(8,128)(2,1)}, bf16[128,256]{1,0:T(8,128)(2,1)S(1)}, u32[]{:S(2)}, u32[]{:S(2)}) collective-permute-start(bf16[128,256]{1,0:T(8,128)(2,1)} %shard_map.147.refs_0_), channel_id=1, source_target_pairs={{0,2},{2,0},{1,3},{3,1},{4,6},{6,4},{5,7},{7,5},{8,10},{10,8},{9,1... | collective-permute-start | bytes 196616 | tf_op jit(solution)/shard_map/ppermute | solution.py:286
  5.1 7.2 %collective-permute-start.1 = (bf16[128,256]{1,0:T(8,128)(2,1)}, bf16[128,256]{1,0:T(8,128)(2,1)S(1)}, u32[]{:S(2)}, u32[]{:S(2)}) collective-permute-start(bf16[128,256]{1,0:T(8,128)(2,1)} %shard_map.147.refs_0_), channel_id=1, source_target_pairs={{0,1},{1,0},{2,3},{3,2},{4,5},{5,4},{6,7},{7,6},{8,9},{9,8},{10,11... | collective-permute-start | bytes 196616 | tf_op jit(solution)/shard_map/ppermute | solution.py:293
  5.1 7.2 %collective-permute-start.2 = (bf16[128,256]{1,0:T(8,128)(2,1)}, bf16[128,256]{1,0:T(8,128)(2,1)S(1)}, u32[]{:S(2)}, u32[]{:S(2)}) collective-permute-start(bf16[128,256]{1,0:T(8,128)(2,1)} %shard_map.147.refs_0_), channel_id=1, source_target_pairs={{0,3},{1,2},{2,1},{3,0},{4,7},{5,6},{6,5},{7,4},{8,11},{9,10},{10,... | collective-permute-start | bytes 196616 | tf_op jit(solution)/shard_map/ppermute | solution.py:293
  5.3 8.3 %copy-start.7 = (bf16[576,448]{0,1:T(8,128)(2,1)S(1)}, bf16[576,448]{0,1:T(8,128)(2,1)}, u32[]{:S(2)}) copy-start(bf16[576,448]{0,1:T(8,128)(2,1)} %param.21) | copy-start | bytes 1548292
  5.3 24.3 %collective-permute-start.3 = (bf16[448,256]{1,0:T(8,128)(2,1)}, bf16[448,256]{1,0:T(8,128)(2,1)S(1)}, u32[]{:S(2)}, u32[]{:S(2)}) collective-permute-start(bf16[448,256]{1,0:T(8,128)(2,1)} %bitcast.17), channel_id=1, source_target_pairs={{0,2},{2,0},{1,3},{3,1},{4,6},{6,4},{5,7},{7,5},{8,10},{10,8},{9,1... | collective-permute-start | bytes 688136 | tf_op jit(solution)/shard_map/ppermute | solution.py:286
  7.3 32.1 %collective-permute-start.4 = (bf16[576,256]{1,0:T(8,128)(2,1)}, bf16[576,256]{1,0:T(8,128)(2,1)S(1)}, u32[]{:S(2)}, u32[]{:S(2)}) collective-permute-start(bf16[576,256]{1,0:T(8,128)(2,1)} %bitcast.15), channel_id=1, source_target_pairs={{0,2},{2,0},{1,3},{3,1},{4,6},{6,4},{5,7},{7,5},{8,10},{10,8},{9,1... | collective-permute-start | bytes 884744 | tf_op jit(solution)/shard_map/ppermute | solution.py:286
  12.3 5.8 %copy-start.8 = (bf16[256,576]{0,1:T(8,128)(2,1)S(1)}, bf16[256,576]{0,1:T(8,128)(2,1)}, u32[]{:S(2)}) copy-start(bf16[256,576]{0,1:T(8,128)(2,1)} %param.13) | copy-start | bytes 884740
  12.3 8.1 %copy-start.2 = (bf16[128,256]{1,0:T(8,128)(2,1)S(1)}, bf16[128,256]{1,0:T(8,128)(2,1)}, u32[]{:S(2)}) copy-start(bf16[128,256]{1,0:T(8,128)(2,1)} %shard_map.147.refs_0_) | copy-start | bytes 196612
  12.3 8.1 %copy-start.5 = (s32[2]{0:T(128)S(1)}, s32[2]{0:T(128)}, u32[]{:S(2)}) copy-start(s32[2]{0:T(128)} %lens_ref.2) | copy-start | bytes 28
  16.2 16.9 %copy-start.1 = (bf16[1792,512]{1,0:T(8,128)(2,1)S(1)}, bf16[1792,512]{1,0:T(8,128)(2,1)}, u32[]{:S(2)}) copy-start(bf16[1792,512]{1,0:T(8,128)(2,1)} %head.1) | copy-start | bytes 5505028
  16.2 16.9 %copy-start.3 = (s32[256]{0:T(256)S(1)}, s32[256]{0:T(256)}, u32[]{:S(2)}) copy-start(s32[256]{0:T(256)} %param.16) | copy-start | bytes 3076
  16.2 7.9 %collective-permute-start.5 = (f32[288,128]{1,0:T(8,128)S(1)}, f32[288,128]{1,0:T(8,128)S(1)}, u32[]{:S(2)}, u32[]{:S(2)}) collective-permute-start(f32[288,128]{1,0:T(8,128)S(1)} %get-tuple-element.60), channel_id=1, source_target_pairs={{0,2},{2,0},{1,3},{3,1},{4,6},{6,4},{5,7},{7,5},{8,10},{10,8},{9,1... | collective-permute-start | bytes 442376 | tf_op jit(solution)/shard_map/ppermute | solution.py:286
  24.1 11.3 %collective-permute-start.10 = (f32[448,128]{1,0:T(8,128)S(1)}, f32[448,128]{1,0:T(8,128)S(1)}, u32[]{:S(2)}, u32[]{:S(2)}) collective-permute-start(f32[448,128]{1,0:T(8,128)S(1)} %get-tuple-element.73), channel_id=1, source_target_pairs={{0,2},{2,0},{1,3},{3,1},{4,6},{6,4},{5,7},{7,5},{8,10},{10,8},{9,1... | collective-permute-start | bytes 688136 | tf_op jit(solution)/shard_map/ppermute | solution.py:286
  25.2 8.8 %collective-permute-start.6 = (bf16[288,128]{1,0:T(8,128)(2,1)S(1)}, bf16[288,128]{1,0:T(8,128)(2,1)S(1)}, u32[]{:S(2)}, u32[]{:S(2)}) collective-permute-start(bf16[288,128]{1,0:T(8,128)(2,1)S(1)} %add_convert_fusion.1.refs_0_), channel_id=1, source_target_pairs={{0,4},{4,8},{8,12},{12,0},{1,5},{5,9},{9,13},{13,1},{2,6},{6,10},{... | collective-permute-start | bytes 221192 | tf_op jit(solution)/shard_map/ppermute | solution.py:286
  27.0 7.4 %collective-permute-start.7 = (bf16[288,128]{1,0:T(8,128)(2,1)S(1)}, bf16[288,128]{1,0:T(8,128)(2,1)S(1)}, u32[]{:S(2)}, u32[]{:S(2)}) collective-permute-start(bf16[288,128]{1,0:T(8,128)(2,1)S(1)} %add_convert_fusion.1.refs_0_), channel_id=1, source_target_pairs={{0,8},{4,12},{8,0},{12,4},{1,9},{5,13},{9,1},{13,5},{2,10},{6,14},... | collective-permute-start | bytes 221192 | tf_op jit(solution)/shard_map/ppermute | solution.py:286
  29.6 4.8 %collective-permute-start.8 = (bf16[288,128]{1,0:T(8,128)(2,1)S(1)}, bf16[288,128]{1,0:T(8,128)(2,1)S(1)}, u32[]{:S(2)}, u32[]{:S(2)}) collective-permute-start(bf16[288,128]{1,0:T(8,128)(2,1)S(1)} %add_convert_fusion.1.refs_0_), channel_id=1, source_target_pairs={{0,12},{4,0},{8,4},{12,8},{1,13},{5,1},{9,5},{13,9},{2,14},{6,2},{... | collective-permute-start | bytes 221192 | tf_op jit(solution)/shard_map/ppermute | solution.py:286
  33.1 8.5 %copy-start = (bf16[2304,512]{1,0:T(8,128)(2,1)S(1)}, bf16[2304,512]{1,0:T(8,128)(2,1)}, u32[]{:S(2)}) copy-start(bf16[2304,512]{1,0:T(8,128)(2,1)} %refs_2_.5) | copy-start | bytes 7077892
  34.5 14.8 %collective-permute-start.9 = (bf16[1152,128]{1,0:T(8,128)(2,1)S(1)}, bf16[1152,128]{1,0:T(8,128)(2,1)S(1)}, u32[]{:S(2)}, u32[]{:S(2)}) collective-permute-start(bf16[1152,128]{1,0:T(8,128)(2,1)S(1)} %shard_map.152), channel_id=1, source_target_pairs={{0,2},{2,0},{1,3},{3,1},{4,6},{6,4},{5,7},{7,5},{8,10},{10,8},{9,1... | collective-permute-start | bytes 884744 | tf_op jit(solution)/shard_map/ppermute | solution.py:286
  35.5 8.0 %collective-permute-start.11 = (bf16[448,128]{1,0:T(8,128)(2,1)S(1)}, bf16[448,128]{1,0:T(8,128)(2,1)S(1)}, u32[]{:S(2)}, u32[]{:S(2)}) collective-permute-start(bf16[448,128]{1,0:T(8,128)(2,1)S(1)} %add_convert_fusion.refs_0_), channel_id=1, source_target_pairs={{0,4},{4,8},{8,12},{12,0},{1,5},{5,9},{9,13},{13,1},{2,6},{6,10},{... | collective-permute-start | bytes 344072 | tf_op jit(solution)/shard_map/ppermute | solution.py:286
  36.9 9.8 %collective-permute-start.12 = (bf16[448,128]{1,0:T(8,128)(2,1)S(1)}, bf16[448,128]{1,0:T(8,128)(2,1)S(1)}, u32[]{:S(2)}, u32[]{:S(2)}) collective-permute-start(bf16[448,128]{1,0:T(8,128)(2,1)S(1)} %add_convert_fusion.refs_0_), channel_id=1, source_target_pairs={{0,8},{4,12},{8,0},{12,4},{1,9},{5,13},{9,1},{13,5},{2,10},{6,14},... | collective-permute-start | bytes 344072 | tf_op jit(solution)/shard_map/ppermute | solution.py:286
  38.9 7.9 %collective-permute-start.13 = (bf16[448,128]{1,0:T(8,128)(2,1)S(1)}, bf16[448,128]{1,0:T(8,128)(2,1)S(1)}, u32[]{:S(2)}, u32[]{:S(2)}) collective-permute-start(bf16[448,128]{1,0:T(8,128)(2,1)S(1)} %add_convert_fusion.refs_0_), channel_id=1, source_target_pairs={{0,12},{4,0},{8,4},{12,8},{1,13},{5,1},{9,5},{13,9},{2,14},{6,2},{... | collective-permute-start | bytes 344072 | tf_op jit(solution)/shard_map/ppermute | solution.py:286
  42.9 10.8 %copy-start.4 = (s32[256]{0:T(256)S(1)}, s32[256]{0:T(256)}, u32[]{:S(2)}) copy-start(s32[256]{0:T(256)} %param.17) | copy-start | bytes 3076
  55.0 14.1 %copy-start.6 = (s32[2]{0:T(128)S(1)}, s32[2]{0:T(128)}, u32[]{:S(2)}) copy-start(s32[2]{0:T(128)} %lens_ref.3) | copy-start | bytes 28
  61.7 5.5 %collective-permute-start.14 = (f32[8,256]{1,0:T(8,128)S(1)}, f32[8,256]{1,0:T(8,128)S(1)}, u32[]{:S(2)}, u32[]{:S(2)}) collective-permute-start(f32[8,256]{1,0:T(8,128)S(1)} %shard_map.156.refs_0_), channel_id=1, source_target_pairs={{0,4},{4,8},{8,12},{12,0},{1,5},{5,9},{9,13},{13,1},{2,6},{6,10},{... | collective-permute-start | bytes 24584 | tf_op jit(solution)/shard_map/ppermute | solution.py:286
  64.6 4.5 %collective-permute-start.15 = (f32[8,256]{1,0:T(8,128)S(1)}, f32[8,256]{1,0:T(8,128)S(1)}, u32[]{:S(2)}, u32[]{:S(2)}) collective-permute-start(f32[8,256]{1,0:T(8,128)S(1)} %shard_map.156.refs_0_), channel_id=1, source_target_pairs={{0,8},{4,12},{8,0},{12,4},{1,9},{5,13},{9,1},{13,5},{2,10},{6,14},... | collective-permute-start | bytes 24584 | tf_op jit(solution)/shard_map/ppermute | solution.py:286
  65.0 4.2 %collective-permute-start.16 = (f32[8,256]{1,0:T(8,128)S(1)}, f32[8,256]{1,0:T(8,128)S(1)}, u32[]{:S(2)}, u32[]{:S(2)}) collective-permute-start(f32[8,256]{1,0:T(8,128)S(1)} %shard_map.156.refs_0_), channel_id=1, source_target_pairs={{0,12},{4,0},{8,4},{12,8},{1,13},{5,1},{9,5},{13,9},{2,14},{6,2},{... | collective-permute-start | bytes 24584 | tf_op jit(solution)/shard_map/ppermute | solution.py:286

commit v3 on v2

--- a/solution.py
+++ b/solution.py
@@ -53,6 +53,11 @@
     return lax.rem(lax.axis_index(axis) - offset + count, count)
 
 
+def block_place(n):
+    core = lax.axis_index("core")
+    return behind("x", n // CORES) * CORES + (core if n % CORES == 0 else 1 - core)
+
+
 def vocab_base(vocab):
     place = lax.axis_index("sv") * lax.axis_size("x") + lax.axis_index("x")
     return (place * CORES + lax.axis_index("core")) * vocab
@@ -86,9 +91,10 @@
         out_ref[part_of(behind(axis, n), rows), :] = block[...]
 
 
-def attend(blocks, lens_ref, states, matrix, *refs):
+def attend(blocks, lens_ref, own_t, own_w, mate_t, mate_w, *refs):
     qk_refs = refs[:blocks]
-    out_ref, weights_ref, q_all, k_all = refs[blocks:]
+    out_ref, weights_ref, q_all, k_all, t_v, w_v, sems = refs[blocks:]
+    copies = fetch(sems, (own_t, t_v), (own_w, w_v))
     rows = qk_refs[0].shape[0] // 2
     for n, ref in enumerate(qk_refs):
         q_all[n * rows : (n + 1) * rows, :] = ref[:rows]
@@ -102,16 +108,15 @@
         scores = jnp.where(position < lens_ref[s], scores, FLOOR)
         raised = jnp.exp(scores - jnp.max(scores, axis=0, keepdims=True))
         weights_ref[s] = (raised / jnp.sum(raised, axis=0, keepdims=True)).astype(BF16)
+    for copy in copies:
+        copy.wait()
     per_core = sequences // CORES
-    rows, cols = states.shape[0] // CORES, out_ref.shape[0]
     for n in range(per_core):
         s = lax.axis_index("core") * per_core + n
-        aligned = dot10(states[:, part_of(s, width)], weights_ref[s]).astype(BF16)
-        total = sum(
-            dot10(matrix[c * cols : (c + 1) * cols, :], aligned[c * rows : (c + 1) * rows])
-            for c in range(CORES)
-        )
-        out_ref[:, n * width : (n + 1) * width] = total
+        tokens = part_of(s, width)
+        own = dot10(t_v[:, tokens], weights_ref[s]).astype(BF16)
+        mate = dot10(mate_t[:, tokens], weights_ref[s]).astype(BF16)
+        out_ref[:, n * width : (n + 1) * width] = dot10(w_v[...], own) + dot10(mate_w[...], mate)
 
 
 def log_total(logits):
@@ -140,8 +145,10 @@
 
 
 def own_student(targets, *refs):
-    *blocks, head, out_ref, notes_ref, s_all = refs
-    collect("x", *blocks, s_all)
+    chip, *blocks, head, out_ref, notes_ref, s_all = refs
+    s_all[part_of(lax.axis_index("x"), chip.shape[0]), :] = chip[...]
+    for n, block in enumerate(blocks):
+        s_all[part_of(block_place(n + CORES), block.shape[0]), :] = block[...]
     logits = dot00(s_all[...], head[...])
     out_ref[...] = logits
     columns = target_column(targets, vocab_base(head.shape[1]))
@@ -149,15 +156,18 @@
     notes_ref[...] = pack_columns((total, pick(logits, columns)))
 
 
-def own_teacher(weights_ref, *refs):
-    *blocks, head, own_ref, t_all = refs
+def own_teacher(weights_ref, own_t, *refs):
+    *blocks, head, own_ref, t_v, t_all, sems = refs
+    copies = fetch(sems, (own_t, t_v))
     sequences, width, _ = weights_ref.shape
-    rows = blocks[0].shape[0]
-    for n, block in enumerate(blocks):
+    rows = own_t.shape[0]
+    for copy in copies:
+        copy.wait()
+    for n, block in enumerate([t_v] + blocks):
         for s in range(sequences):
             tokens = slice(s * width, (s + 1) * width)
             aligned = dot10(block[:, tokens], weights_ref[s]).astype(BF16)
-            t_all[part_of(behind("x", n), rows), tokens] = aligned
+            t_all[part_of(block_place(n), rows), tokens] = aligned
     own_ref[...] = dot00(t_all[...], head[...])
 
 
@@ -281,6 +291,9 @@
     def both(a):
         return lax.all_gather(a, "core", axis=0, tiled=True)
 
+    def swap(a):
+        return lax.ppermute(a, "core", [(0, 1), (1, 0)])
+
     def shift(a, axis, n):
         count = lax.axis_size(axis)
         return lax.ppermute(a, axis, [(i, (i + n) % count) for i in range(count)])
@@ -301,36 +314,36 @@
         pack_kernel, shape((2 * q_t.shape[0], rows), BF16), [HBM] * 2, [dma((2,))], limit=60
     )(q_t, k_t)
     qk_blocks = [qk] + around(qk, "x") + [cross(qk, n) for n in range(chips)]
-    chip_s, chip_w_t = (both(a) for a in after((s_t, w_t), qk))
-    far_s, far_t = after((s_t, t_t), qk)
-    far_s, far_t = around(far_s, "x"), around(far_t, "x")
+    mate_w_s, mate_t = swap(w_s), swap(t_t)
+    chip_w_t, chip_s = (both(a) for a in after((w_t, s_t), qk))
+    far_s = around(after((s_t,), qk)[0], "x")
     split = chips if w_t.shape[1] % (16 * chips) == 0 else 1
     share = shape((w_t.shape[1] // split, tokens))
-    (chip_s, chip_w_t), qk_blocks = lax.optimization_barrier(((chip_s, chip_w_t), qk_blocks))
     *parts_t, _ = kernel_call(
         project, [share] * split + [shape((w_t.shape[1], tokens))], [VMEM] * 2
     )(chip_s, chip_w_t)
 
-    t_out, w_out, *parts_t = lax.optimization_barrier((t_t, w_s, *parts_t))
+    *qk_blocks, mate_w_s, mate_t, parts_t = lax.optimization_barrier(
+        (*qk_blocks, mate_w_s, mate_t, parts_t)
+    )
     other_t = [shift(parts_t[n % split], "x", n) for n in range(1, chips)]
-    chip_t, chip_w_s = both(t_out), both(w_out)
     features = q_t.shape[0] * chips * CORES
     part_s, weights = kernel_call(
         functools.partial(attend, len(qk_blocks)),
         (shape((w_s.shape[0], tokens)), shape((sequences, width, width), BF16)),
-        [SMEM] + [VMEM] * (2 + len(qk_blocks)),
-        [pltpu.VMEM((features, rows), BF16)] * 2,
-    )(teacher_lengths, chip_t, chip_w_s, *qk_blocks)
+        [SMEM] + [HBM] * 2 + [VMEM] * (2 + len(qk_blocks)),
+        [pltpu.VMEM((features, rows), BF16)] * 2
+        + [pltpu.VMEM(a.shape, BF16) for a in (t_t, w_s)]
+        + [dma((2,))],
+    )(teacher_lengths, t_t, w_s, mate_t, mate_w_s, *qk_blocks)
 
     own_part, *other_t, part_s = lax.optimization_barrier((parts_t[0], *other_t, part_s))
+    far_t = around(after((t_t,), *other_t)[0], "x")
     into_t = functools.reduce(jnp.add, other_t, own_part).astype(BF16)
     into_t = [into_t] + around(into_t, "sv")
     other_s = around(part_s, "x")
 
-    far_s, far_t = [both(a) for a in far_s], [both(a) for a in far_t]
-
-    *into_t, part_s = lax.optimization_barrier((*into_t, part_s))
-    other_s = after(other_s, *into_t)
+    *into_t, part_s, other_s = lax.optimization_barrier((*into_t, part_s, other_s))
     into_s = functools.reduce(jnp.add, other_s, part_s).astype(BF16)
     into_s = [into_s] + around(into_s, "sv")
     into_t = kernel_call(
@@ -339,22 +352,26 @@
         [VMEM] * sv_count,
     )(*into_t)
     t_shares = [into_t] + (around(into_t, "x") if split > 1 else [])
-    t_shares = [both(a) for a in lax.optimization_barrier(tuple(t_shares))]
-    s_blocks = [chip_s] + far_s
-    t_blocks = [chip_t] + far_t
+    t_shares = [both(a) for a in t_shares]
+    s_blocks = [chip_s] + [p for a in far_s for p in (a, swap(a))]
+    t_blocks = [mate_t] + [p for a in far_t for p in (a, swap(a))]
     logits = shape((rows, vocab))
     s_own, s_notes = kernel_call(
         own_student,
         (logits, shape((rows, 128))),
-        [VMEM] * (2 + chips),
+        [VMEM] * (2 + len(s_blocks)),
         [pltpu.VMEM((student_head.shape[0], rows), BF16)],
     )(s_targets, *s_blocks, student_head)
     t_own = kernel_call(
         own_teacher,
         logits,
-        [VMEM] * (2 + chips),
-        [pltpu.VMEM((teacher_head.shape[0], rows), BF16)],
-    )(weights, *t_blocks, teacher_head)
+        [VMEM, HBM] + [VMEM] * (1 + len(t_blocks)),
+        [
+            pltpu.VMEM(t_t.shape, BF16),
+            pltpu.VMEM((teacher_head.shape[0], rows), BF16),
+            dma((1,)),
+        ],
+    )(weights, t_t, *t_blocks, teacher_head)
     t_mapped, t_stats = kernel_call(
         mapped_teacher,
         (logits, shape((STATS, rows))),
@@ -366,7 +383,7 @@
         functools.partial(collect, "sv"),
         shape((sv_count * into_s[0].shape[0], tokens), BF16),
         [VMEM] * sv_count,
-    )(*into_s)
+    )(*after(into_s, t_stats))
     s_mapped, stats = kernel_call(
         student_side, (logits, shape((STATS, rows))), [VMEM] * 6
     )(s_targets, t_stats, s_own, s_notes, both(into_s), student_head)

time: 71.5 us -> 63.9 us (0.89)
  blocking collectives: 26.2 us -> 17.3 us
  waiting for transfers between devices: 8.61 us -> 11.3 us
  starting transfers between devices: 24.2 us -> 22.6 us
    all_gather x9 -> x5, blocking collectives: 21 us -> 12.1 us  [both(): return lax.all_gather(a, 'core', axis=0, tiled=True)]
    ppermute x15, waiting for transfers between devices: 8.61 us -> 11.3 us  [shift(): return lax.ppermute(a, axis, [(i, (i + n) % count) for i in range(count)])]
    ppermute x15, starting transfers between devices: 24 us -> 21.5 us  [shift(): return lax.ppermute(a, axis, [(i, (i + n) % count) for i in range(count)])]
    ppermute x0 -> x4, starting transfers between devices: none -> 0.96 us  [swap(): return lax.ppermute(a, 'core', [(0, 1), (1, 0)])]
  transfers between devices with their start and end apart: 17 -> 21, of which waited for: 6 -> 8; matrix products, arithmetic and copies ran while one was open for 0% -> 0% of each run, Pallas kernels for 7% -> 13%
where the time goes in v3:
time: 63.9 us; the launch traced here: 63.7 us
  starting transfers between devices  22.6 us (35%)
  blocking collectives  17.3 us (27%)
  Pallas kernels  11.5 us (18%)
  waiting for transfers between devices  11.3 us (18%)
  between operations  0.79 us (1%)
    ppermute x15, starting transfers between devices, shift(): return lax.ppermute(a, axis, [(i, (i + n) % count) for i in range(count)])  21.5 us
    all_gather x5, blocking collectives, both(): return lax.all_gather(a, 'core', axis=0, tiled=True)  12.1 us
    ppermute x15, waiting for transfers between devices, shift(): return lax.ppermute(a, axis, [(i, (i + n) % count) for i in range(count)])  11.3 us
    all_gather x1, blocking collectives, body(): stats = lax.all_gather(stats, ('x', 'core'), axis=0, tiled=True)  5.18 us
    pallas_call x1, Pallas kernels, body(): kernel_call(functools.partial(finish, sv_count), (shape((1, rows)), shape...  2.05 us
    pallas_call x1, Pallas kernels, body(): kernel_call(functools.partial(attend, len(qk_blocks)), (shape((w_s.shape[...  1.66 us
    pallas_call x1, Pallas kernels, body(): kernel_call(pack_kernel, shape((2 * q_t.shape[0], rows), BF16), [HBM] * 2...  1.42 us
    pallas_call x1, Pallas kernels, body(): kernel_call(student_side, (logits, shape((STATS, rows))), [VMEM] * 6)  1.4 us
  transfers between devices with their start and end apart: 21, of which 8 were waited for; matrix products, arithmetic and copies ran while one was open for 0% of the time, Pallas kernels for 13%

profile of v3, /device:TPU:0, one launch (start us, length us, event | category | flops | bytes accessed | tf_op | source)
XLA Modules:
  0.0 63.7 jit_solution(4600444917171667471)
XLA Ops:
  0.6 0.5 collective-permute-start.5
  1.2 1.4 %shard_map.147.refs_0_ = bf16[128,256]{1,0:T(8,128)(2,1)} custom-call(bf16[64,256]{1,0:T(8,128)(2,1)} %bitcast.22, bf16[64,256]{1,0:T(8,128)(2,1)} %bitcast.23), custom_call_target="tpu_custom_call" | custom-call | tf_op jit(solution)/shard_map/pallas_call | solution.py:313
  2.6 2.6 %collective-permute-start.2 = (bf16[128,256]{1,0:T(8,128)(2,1)}, bf16[128,256]{1,0:T(8,128)(2,1)S(1)}, u32[]{:S(2)}, u32[]{:S(2)}) collective-permute-start(bf16[128,256]{1,0:T(8,128)(2,1)} %shard_map.147.refs_0_), channel_id=1, source_target_pairs={{0,2},{2,0},{1,3},{3,1},{4,6},{6,4},{5,7},{7,5},{8,10},{10,8},{9,1... | collective-permute-start | bytes 196616 | tf_op jit(solution)/shard_map/ppermute | solution.py:299
  5.2 0.2 collective-permute-start.3
  5.4 0.0 collective-permute-start.4
  5.4 0.4 collective-permute-start.6
  5.9 3.0 %all_gather.19.matrix = bf16[896,576]{1,0:T(8,128)(2,1)S(1)} all-gather(bf16[448,576]{1,0:T(8,128)(2,1)} %param.20), channel_id=1, replica_groups=mesh['grp'=2,'sv'=4,'x'=2,'core'=2] {'core'}, dimensions={0}, use_global_device_ids=true | all-gather | bytes 1548288 | tf_op jit(solution)/shard_map/all_gather | solution.py:292
  8.8 1.7 %collective-permute-start = (bf16[448,256]{1,0:T(8,128)(2,1)S(1)}, bf16[448,256]{1,0:T(8,128)(2,1)S(1)}, u32[]{:S(2)}, u32[]{:S(2)}) collective-permute-start(bf16[448,256]{1,0:T(8,128)(2,1)S(1)} %bitcast.20), channel_id=1, source_target_pairs={{0,2},{2,0},{1,3},{3,1},{4,6},{6,4},{5,7},{7,5},{8,10},{10,8},{9,1... | collective-permute-start | bytes 688136 | tf_op jit(solution)/shard_map/ppermute | solution.py:299
  10.5 2.1 %all_gather.18.refs_0_.states = bf16[896,256]{1,0:T(8,128)(2,1)S(1)} all-gather(bf16[448,256]{1,0:T(8,128)(2,1)S(1)} %bitcast.21), channel_id=1, replica_groups=mesh['grp'=2,'sv'=4,'x'=2,'core'=2] {'core'}, dimensions={0}, use_global_device_ids=true | all-gather | bytes 688128 | tf_op jit(solution)/shard_map/all_gather | solution.py:292
  12.7 1.3 %shard_map.149 = (f32[288,128]{1,0:T(8,128)S(1)}, f32[288,128]{1,0:T(8,128)S(1)}, f32[576,128]{1,0:T(8,128)}) custom-call(bf16[896,256]{1,0:T(8,128)(2,1)S(1)} %all_gather.18.refs_0_.states, bf16[896,576]{1,0:T(8,128)(2,1)S(1)} %all_gather.19.matrix), custom_call_target="tpu_custom_call" | custom-call | tf_op jit(solution)/shard_map/pallas_call | solution.py:322
  13.9 0.0 collective-permute-done.3.refs_2_
  13.9 0.0 collective-permute-done.4.refs_3_
  13.9 0.0 collective-permute-done.6.mate_t.refs_0_
  13.9 0.4 collective-permute-start.7
  14.4 2.3 %collective-permute-done.refs_1_ = bf16[448,256]{1,0:T(8,128)(2,1)S(1)} collective-permute-done((bf16[448,256]{1,0:T(8,128)(2,1)S(1)}, bf16[448,256]{1,0:T(8,128)(2,1)S(1)}, u32[]{:S(2)}, u32[]{:S(2)}) %collective-permute-start) | collective-permute-done | bytes 229408 | tf_op jit(solution)/shard_map/ppermute | solution.py:299
  16.6 0.0 collective-permute-start.1
  16.7 1.7 %shard_map.150 = (f32[448,128]{1,0:T(8,128)S(1)}, bf16[2,128,128]{2,1,0:T(8,128)(2,1)S(1)}) custom-call(s32[2]{0:T(128)S(1)} %copy-done.7, bf16[576,256]{1,0:T(8,128)(2,1)S(1)} %bitcast.10, bf16[448,576]{1,0:T(8,128)(2,1)S(1)} %bitcast.14, bf16[576,256]{1,0:T(8,128)(2,1)S(1)} %collective-permute-done.6.mate_t.refs_0_, ...), custom_call_target="tpu_custom_call" | custom-call | tf_op jit(solution)/shard_map/pallas_call | solution.py:331
  18.3 1.6 %collective-permute-done.7 = f32[288,128]{1,0:T(8,128)S(1)} collective-permute-done((f32[288,128]{1,0:T(8,128)S(1)}, f32[288,128]{1,0:T(8,128)S(1)}, u32[]{:S(2)}, u32[]{:S(2)}) %collective-permute-start.7) | collective-permute-done | bytes 147488 | tf_op jit(solution)/shard_map/ppermute | solution.py:299
  19.9 1.6 %collective-permute-start.13 = (f32[448,128]{1,0:T(8,128)S(1)}, f32[448,128]{1,0:T(8,128)S(1)}, u32[]{:S(2)}, u32[]{:S(2)}) collective-permute-start(f32[448,128]{1,0:T(8,128)S(1)} %get-tuple-element.69), channel_id=1, source_target_pairs={{0,2},{2,0},{1,3},{3,1},{4,6},{6,4},{5,7},{7,5},{8,10},{10,8},{9,1... | collective-permute-start | bytes 688136 | tf_op jit(solution)/shard_map/ppermute | solution.py:299
  21.6 1.6 %collective-permute-start.10 = (bf16[288,128]{1,0:T(8,128)(2,1)S(1)}, bf16[288,128]{1,0:T(8,128)(2,1)S(1)}, u32[]{:S(2)}, u32[]{:S(2)}) collective-permute-start(bf16[288,128]{1,0:T(8,128)(2,1)S(1)} %add_convert_fusion.1.refs_0_), channel_id=1, source_target_pairs={{0,4},{4,8},{8,12},{12,0},{1,5},{5,9},{9,13},{13,1},{2,6},{6,10},{... | collective-permute-start | bytes 221192 | tf_op jit(solution)/shard_map/ppermute | solution.py:299
  23.2 2.6 %collective-permute-start.11 = (bf16[288,128]{1,0:T(8,128)(2,1)S(1)}, bf16[288,128]{1,0:T(8,128)(2,1)S(1)}, u32[]{:S(2)}, u32[]{:S(2)}) collective-permute-start(bf16[288,128]{1,0:T(8,128)(2,1)S(1)} %add_convert_fusion.1.refs_0_), channel_id=1, source_target_pairs={{0,8},{4,12},{8,0},{12,4},{1,9},{5,13},{9,1},{13,5},{2,10},{6,14},... | collective-permute-start | bytes 221192 | tf_op jit(solution)/shard_map/ppermute | solution.py:299
  25.8 1.3 %collective-permute-start.12 = (bf16[288,128]{1,0:T(8,128)(2,1)S(1)}, bf16[288,128]{1,0:T(8,128)(2,1)S(1)}, u32[]{:S(2)}, u32[]{:S(2)}) collective-permute-start(bf16[288,128]{1,0:T(8,128)(2,1)S(1)} %add_convert_fusion.1.refs_0_), channel_id=1, source_target_pairs={{0,12},{4,0},{8,4},{12,8},{1,13},{5,1},{9,5},{13,9},{2,14},{6,2},{... | collective-permute-start | bytes 221192 | tf_op jit(solution)/shard_map/ppermute | solution.py:299
  27.1 0.5 collective-permute-start.8
  27.7 0.9 %shard_map.148 = (f32[256,512]{1,0:T(8,128)S(1)}, f32[256,128]{1,0:T(8,128)S(1)}) custom-call(s32[1,256]{1,0:T(1,128)S(1)} %bitcast.15, bf16[896,256]{1,0:T(8,128)(2,1)S(1)} %all_gather.18.refs_0_.states, bf16[448,256]{1,0:T(8,128)(2,1)S(1)} %collective-permute-done.refs_1_, bf16[448,256]{1,0:T(8,128)(2,1)S(1)} %collective-permute-done.1.refs_2_, ...), custom_call_target="tpu_custom_call" | custom-call | tf_op jit(solution)/shard_map/pallas_call | solution.py:359
  28.6 0.0 copy-start
  28.6 0.1 collective-permute-done.10.refs_1_
  28.7 2.2 %collective-permute-done.11.refs_2_ = bf16[288,128]{1,0:T(8,128)(2,1)S(1)} collective-permute-done((bf16[288,128]{1,0:T(8,128)(2,1)S(1)}, bf16[288,128]{1,0:T(8,128)(2,1)S(1)}, u32[]{:S(2)}, u32[]{:S(2)}) %collective-permute-start.11) | collective-permute-done | bytes 73760 | tf_op jit(solution)/shard_map/ppermute | solution.py:299
  30.9 0.0 collective-permute-done.12.refs_3_
  31.0 0.4 collective-permute-start.14
  31.4 1.5 %collective-permute-start.15 = (bf16[448,128]{1,0:T(8,128)(2,1)S(1)}, bf16[448,128]{1,0:T(8,128)(2,1)S(1)}, u32[]{:S(2)}, u32[]{:S(2)}) collective-permute-start(bf16[448,128]{1,0:T(8,128)(2,1)S(1)} %add_convert_fusion.refs_0_), channel_id=1, source_target_pairs={{0,4},{4,8},{8,12},{12,0},{1,5},{5,9},{9,13},{13,1},{2,6},{6,10},{... | collective-permute-start | bytes 344072 | tf_op jit(solution)/shard_map/ppermute | solution.py:299
  32.8 1.9 %collective-permute-start.16 = (bf16[448,128]{1,0:T(8,128)(2,1)S(1)}, bf16[448,128]{1,0:T(8,128)(2,1)S(1)}, u32[]{:S(2)}, u32[]{:S(2)}) collective-permute-start(bf16[448,128]{1,0:T(8,128)(2,1)S(1)} %add_convert_fusion.refs_0_), channel_id=1, source_target_pairs={{0,8},{4,12},{8,0},{12,4},{1,9},{5,13},{9,1},{13,5},{2,10},{6,14},... | collective-permute-start | bytes 344072 | tf_op jit(solution)/shard_map/ppermute | solution.py:299
  34.8 1.0 %collective-permute-start.17 = (bf16[448,128]{1,0:T(8,128)(2,1)S(1)}, bf16[448,128]{1,0:T(8,128)(2,1)S(1)}, u32[]{:S(2)}, u32[]{:S(2)}) collective-permute-start(bf16[448,128]{1,0:T(8,128)(2,1)S(1)} %add_convert_fusion.refs_0_), channel_id=1, source_target_pairs={{0,12},{4,0},{8,4},{12,8},{1,13},{5,1},{9,5},{13,9},{2,14},{6,2},{... | collective-permute-start | bytes 344072 | tf_op jit(solution)/shard_map/ppermute | solution.py:299
  35.7 1.3 %collective-permute-done.8.refs_1_ = bf16[576,256]{1,0:T(8,128)(2,1)S(1)} collective-permute-done((bf16[576,256]{1,0:T(8,128)(2,1)S(1)}, bf16[576,256]{1,0:T(8,128)(2,1)S(1)}, u32[]{:S(2)}, u32[]{:S(2)}) %collective-permute-start.8) | collective-permute-done | bytes 294944 | tf_op jit(solution)/shard_map/ppermute | solution.py:299
  37.1 2.3 %all_gather.20.refs_0_ = bf16[2304,128]{1,0:T(8,128)(2,1)S(1)} all-gather(bf16[1152,128]{1,0:T(8,128)(2,1)S(1)} %shard_map.152), channel_id=1, replica_groups=mesh['grp'=2,'sv'=4,'x'=2,'core'=2] {'core'}, dimensions={0}, use_global_device_ids=true | all-gather | bytes 884736 | tf_op jit(solution)/shard_map/all_gather | solution.py:292
  39.4 1.5 %collective-permute-done.14 = bf16[1152,128]{1,0:T(8,128)(2,1)S(1)} collective-permute-done((bf16[1152,128]{1,0:T(8,128)(2,1)S(1)}, bf16[1152,128]{1,0:T(8,128)(2,1)S(1)}, u32[]{:S(2)}, u32[]{:S(2)}) %collective-permute-start.14) | collective-permute-done | bytes 294944 | tf_op jit(solution)/shard_map/ppermute | solution.py:299
  40.9 2.2 %all_gather.21.refs_1_ = bf16[2304,128]{1,0:T(8,128)(2,1)S(1)} all-gather(bf16[1152,128]{1,0:T(8,128)(2,1)S(1)} %collective-permute-done.14), channel_id=1, replica_groups=mesh['grp'=2,'sv'=4,'x'=2,'core'=2] {'core'}, dimensions={0}, use_global_device_ids=true | all-gather | bytes 884736 | tf_op jit(solution)/shard_map/all_gather | solution.py:292
  43.2 1.3 %shard_map.151.own_ref.to_ref = f32[256,512]{1,0:T(8,128)S(1)} custom-call(bf16[2,128,128]{2,1,0:T(8,128)(2,1)S(1)} %get-tuple-element.55.weights_ref, bf16[576,256]{1,0:T(8,128)(2,1)S(1)} %bitcast.12, bf16[576,256]{1,0:T(8,128)(2,1)S(1)} %collective-permute-done.6.mate_t.refs_0_, bf16[576,256]{1,0:T(8,128)(2,1)S(1)} %collective-permute-done.8.refs_1_, ...), custom_call_target="tpu_custom_call" | custom-call | tf_op jit(solution)/shard_map/pallas_call | solution.py:365
  44.5 1.4 %shard_map.153 = (f32[256,512]{1,0:T(8,128)S(1)}, f32[8,256]{1,0:T(8,128)S(1)}) custom-call(s32[1,256]{1,0:T(1,128)S(1)} %bitcast.18, f32[256,512]{1,0:T(8,128)S(1)} %shard_map.151.own_ref.to_ref, bf16[2304,128]{1,0:T(8,128)(2,1)S(1)} %all_gather.20.refs_0_, bf16[2304,128]{1,0:T(8,128)(2,1)S(1)} %all_gather.21.refs_1_, bf16[2304,512]{1,0:T(8,128)(2,1)S(1)} %copy-done), custom_call_target="tpu_custom_call" | custom-call | tf_op jit(solution)/shard_map/pallas_call | solution.py:375
  45.9 0.0 collective-permute-done.17.refs_3_
  46.0 2.5 %all_gather.22.halves = bf16[3584,128]{1,0:T(8,128)(2,1)S(1)} all-gather(bf16[1792,128]{1,0:T(8,128)(2,1)S(1)} %shard_map.154), channel_id=1, replica_groups=mesh['grp'=2,'sv'=4,'x'=2,'core'=2] {'core'}, dimensions={0}, use_global_device_ids=true | all-gather | bytes 1376256 | tf_op jit(solution)/shard_map/all_gather | solution.py:292
  48.4 1.4 %shard_map.155 = (f32[256,512]{1,0:T(8,128)S(1)}, f32[8,256]{1,0:T(8,128)S(1)}) custom-call(s32[1,256]{1,0:T(1,128)S(1)} %bitcast.16, f32[8,256]{1,0:T(8,128)S(1)} %get-tuple-element.67.t_stats, f32[256,512]{1,0:T(8,128)S(1)} %get-tuple-element.45.own_ref.so_ref, f32[256,128]{1,0:T(8,128)S(1)} %get-tuple-element.68.notes_ref, ...), custom_call_target="tpu_custom_call" | custom-call | tf_op jit(solution)/shard_map/pallas_call | solution.py:387
  49.8 5.2 %all_gather.23.in_ref = f32[32,256]{1,0:T(8,128)S(1)} all-gather(f32[8,256]{1,0:T(8,128)S(1)} %get-tuple-element.77), channel_id=1, replica_groups=mesh['grp'=2,'sv'=4,'x'=2,'core'=2] {'x','core'}, dimensions={0}, use_global_device_ids=true | all-gather | bytes 40960 | tf_op jit(solution)/shard_map/all_gather | solution.py:391
  55.0 0.7 %collective-permute-start.18 = (f32[8,256]{1,0:T(8,128)S(1)}, f32[8,256]{1,0:T(8,128)S(1)}, u32[]{:S(2)}, u32[]{:S(2)}) collective-permute-start(f32[8,256]{1,0:T(8,128)S(1)} %shard_map.156.refs_0_), channel_id=1, source_target_pairs={{0,4},{4,8},{8,12},{12,0},{1,5},{5,9},{9,13},{13,1},{2,6},{6,10},{... | collective-permute-start | bytes 24584 | tf_op jit(solution)/shard_map/ppermute | solution.py:299
  55.8 2.2 %collective-permute-start.19 = (f32[8,256]{1,0:T(8,128)S(1)}, f32[8,256]{1,0:T(8,128)S(1)}, u32[]{:S(2)}, u32[]{:S(2)}) collective-permute-start(f32[8,256]{1,0:T(8,128)S(1)} %shard_map.156.refs_0_), channel_id=1, source_target_pairs={{0,8},{4,12},{8,0},{12,4},{1,9},{5,13},{9,1},{13,5},{2,10},{6,14},... | collective-permute-start | bytes 24584 | tf_op jit(solution)/shard_map/ppermute | solution.py:299
  58.0 1.4 %collective-permute-start.20 = (f32[8,256]{1,0:T(8,128)S(1)}, f32[8,256]{1,0:T(8,128)S(1)}, u32[]{:S(2)}, u32[]{:S(2)}) collective-permute-start(f32[8,256]{1,0:T(8,128)S(1)} %shard_map.156.refs_0_), channel_id=1, source_target_pairs={{0,12},{4,0},{8,4},{12,8},{1,13},{5,1},{9,5},{13,9},{2,14},{6,2},{... | collective-permute-start | bytes 24584 | tf_op jit(solution)/shard_map/ppermute | solution.py:299
  59.3 1.3 %collective-permute-done.18.refs_1_ = f32[8,256]{1,0:T(8,128)S(1)} collective-permute-done((f32[8,256]{1,0:T(8,128)S(1)}, f32[8,256]{1,0:T(8,128)S(1)}, u32[]{:S(2)}, u32[]{:S(2)}) %collective-permute-start.18) | collective-permute-done | bytes 8224 | tf_op jit(solution)/shard_map/ppermute | solution.py:299
  60.6 1.0 %collective-permute-done.20.refs_3_ = f32[8,256]{1,0:T(8,128)S(1)} collective-permute-done((f32[8,256]{1,0:T(8,128)S(1)}, f32[8,256]{1,0:T(8,128)S(1)}, u32[]{:S(2)}, u32[]{:S(2)}) %collective-permute-start.20) | collective-permute-done | bytes 8224 | tf_op jit(solution)/shard_map/ppermute | solution.py:299
  61.6 2.0 %shard_map.157 = (f32[1,256]{1,0:T(1,128)}, f32[1,256]{1,0:T(1,128)}, bf16[256,512]{1,0:T(8,128)(2,1)}, bf16[256,512]{1,0:T(8,128)(2,1)}) custom-call(s32[2]{0:T(128)S(1)} %copy-done.8, s32[1,256]{1,0:T(1,128)S(1)} %bitcast.17, s32[1,256]{1,0:T(1,128)S(1)} %bitcast.19, f32[256,512]{1,0:T(8,128)S(1)} %get-tuple-element.45.own_ref.so_ref, ...), custom_call_target="tpu_custom_call" | custom-call | tf_op jit(solution)/shard_map/pallas_call | solution.py:396
  (33 shorter events, 0.2 us)
Async XLA Ops:
  0.6 8.2 %copy-start.9 = (bf16[256,448]{0,1:T(8,128)(2,1)S(1)}, bf16[256,448]{0,1:T(8,128)(2,1)}, u32[]{:S(2)}) copy-start(bf16[256,448]{0,1:T(8,128)(2,1)} %param.12) | copy-start | bytes 688132
  0.6 13.3 %collective-permute-start.5 = (bf16[448,576]{1,0:T(8,128)(2,1)}, bf16[448,576]{1,0:T(8,128)(2,1)S(1)}, u32[]{:S(2)}, u32[]{:S(2)}) collective-permute-start(bf16[448,576]{1,0:T(8,128)(2,1)} %bitcast.13), channel_id=1, source_target_pairs={{0,1},{1,0},{2,3},{3,2},{4,5},{5,4},{6,7},{7,6},{8,9},{9,8},{10,11... | collective-permute-start | bytes 1548296 | tf_op jit(solution)/shard_map/ppermute | solution.py:295
  2.6 6.2 %collective-permute-start.2 = (bf16[128,256]{1,0:T(8,128)(2,1)}, bf16[128,256]{1,0:T(8,128)(2,1)S(1)}, u32[]{:S(2)}, u32[]{:S(2)}) collective-permute-start(bf16[128,256]{1,0:T(8,128)(2,1)} %shard_map.147.refs_0_), channel_id=1, source_target_pairs={{0,2},{2,0},{1,3},{3,1},{4,6},{6,4},{5,7},{7,5},{8,10},{10,8},{9,1... | collective-permute-start | bytes 196616 | tf_op jit(solution)/shard_map/ppermute | solution.py:299
  5.2 8.7 %collective-permute-start.3 = (bf16[128,256]{1,0:T(8,128)(2,1)}, bf16[128,256]{1,0:T(8,128)(2,1)S(1)}, u32[]{:S(2)}, u32[]{:S(2)}) collective-permute-start(bf16[128,256]{1,0:T(8,128)(2,1)} %shard_map.147.refs_0_), channel_id=1, source_target_pairs={{0,1},{1,0},{2,3},{3,2},{4,5},{5,4},{6,7},{7,6},{8,9},{9,8},{10,11... | collective-permute-start | bytes 196616 | tf_op jit(solution)/shard_map/ppermute | solution.py:306
  5.4 8.6 %collective-permute-start.4 = (bf16[128,256]{1,0:T(8,128)(2,1)}, bf16[128,256]{1,0:T(8,128)(2,1)S(1)}, u32[]{:S(2)}, u32[]{:S(2)}) collective-permute-start(bf16[128,256]{1,0:T(8,128)(2,1)} %shard_map.147.refs_0_), channel_id=1, source_target_pairs={{0,3},{1,2},{2,1},{3,0},{4,7},{5,6},{6,5},{7,4},{8,11},{9,10},{10,... | collective-permute-start | bytes 196616 | tf_op jit(solution)/shard_map/ppermute | solution.py:306
  5.4 8.5 %collective-permute-start.6 = (bf16[576,256]{1,0:T(8,128)(2,1)}, bf16[576,256]{1,0:T(8,128)(2,1)S(1)}, u32[]{:S(2)}, u32[]{:S(2)}) collective-permute-start(bf16[576,256]{1,0:T(8,128)(2,1)} %bitcast.9), channel_id=1, source_target_pairs={{0,1},{1,0},{2,3},{3,2},{4,5},{5,4},{6,7},{7,6},{8,9},{9,8},{10,11... | collective-permute-start | bytes 884744 | tf_op jit(solution)/shard_map/ppermute | solution.py:295
  5.8 10.8 %copy-start.2 = (bf16[256,576]{0,1:T(8,128)(2,1)S(1)}, bf16[256,576]{0,1:T(8,128)(2,1)}, u32[]{:S(2)}) copy-start(bf16[256,576]{0,1:T(8,128)(2,1)} %param.13) | copy-start | bytes 884740
  5.8 10.8 %copy-start.3 = (bf16[576,448]{0,1:T(8,128)(2,1)S(1)}, bf16[576,448]{0,1:T(8,128)(2,1)}, u32[]{:S(2)}) copy-start(bf16[576,448]{0,1:T(8,128)(2,1)} %param.21) | copy-start | bytes 1548292
  5.8 10.8 %copy-start.4 = (bf16[128,256]{1,0:T(8,128)(2,1)S(1)}, bf16[128,256]{1,0:T(8,128)(2,1)}, u32[]{:S(2)}) copy-start(bf16[128,256]{1,0:T(8,128)(2,1)} %shard_map.147.refs_0_) | copy-start | bytes 196612
  5.8 10.8 %copy-start.7 = (s32[2]{0:T(128)S(1)}, s32[2]{0:T(128)}, u32[]{:S(2)}) copy-start(s32[2]{0:T(128)} %lens_ref.2) | copy-start | bytes 28
  8.8 7.8 %collective-permute-start = (bf16[448,256]{1,0:T(8,128)(2,1)S(1)}, bf16[448,256]{1,0:T(8,128)(2,1)S(1)}, u32[]{:S(2)}, u32[]{:S(2)}) collective-permute-start(bf16[448,256]{1,0:T(8,128)(2,1)S(1)} %bitcast.20), channel_id=1, source_target_pairs={{0,2},{2,0},{1,3},{3,1},{4,6},{6,4},{5,7},{7,5},{8,10},{10,8},{9,1... | collective-permute-start | bytes 688136 | tf_op jit(solution)/shard_map/ppermute | solution.py:299
  12.7 15.0 %copy-start.1 = (bf16[1792,512]{1,0:T(8,128)(2,1)S(1)}, bf16[1792,512]{1,0:T(8,128)(2,1)}, u32[]{:S(2)}) copy-start(bf16[1792,512]{1,0:T(8,128)(2,1)} %head.1) | copy-start | bytes 5505028
  12.7 15.0 %copy-start.5 = (s32[256]{0:T(256)S(1)}, s32[256]{0:T(256)}, u32[]{:S(2)}) copy-start(s32[256]{0:T(256)} %param.16) | copy-start | bytes 3076
  13.9 6.0 %collective-permute-start.7 = (f32[288,128]{1,0:T(8,128)S(1)}, f32[288,128]{1,0:T(8,128)S(1)}, u32[]{:S(2)}, u32[]{:S(2)}) collective-permute-start(f32[288,128]{1,0:T(8,128)S(1)} %get-tuple-element.57), channel_id=1, source_target_pairs={{0,2},{2,0},{1,3},{3,1},{4,6},{6,4},{5,7},{7,5},{8,10},{10,8},{9,1... | collective-permute-start | bytes 442376 | tf_op jit(solution)/shard_map/ppermute | solution.py:299
  16.6 10.5 %collective-permute-start.1 = (bf16[448,256]{1,0:T(8,128)(2,1)S(1)}, bf16[448,256]{1,0:T(8,128)(2,1)S(1)}, u32[]{:S(2)}, u32[]{:S(2)}) collective-permute-start(bf16[448,256]{1,0:T(8,128)(2,1)S(1)} %collective-permute-done.refs_1_), channel_id=1, source_target_pairs={{0,1},{1,0},{2,3},{3,2},{4,5},{5,4},{6,7},{7,6},{8,9},{9,8},{10,11... | collective-permute-start | bytes 688136 | tf_op jit(solution)/shard_map/ppermute | solution.py:295
  19.9 11.0 %collective-permute-start.13 = (f32[448,128]{1,0:T(8,128)S(1)}, f32[448,128]{1,0:T(8,128)S(1)}, u32[]{:S(2)}, u32[]{:S(2)}) collective-permute-start(f32[448,128]{1,0:T(8,128)S(1)} %get-tuple-element.69), channel_id=1, source_target_pairs={{0,2},{2,0},{1,3},{3,1},{4,6},{6,4},{5,7},{7,5},{8,10},{10,8},{9,1... | collective-permute-start | bytes 688136 | tf_op jit(solution)/shard_map/ppermute | solution.py:299
  21.6 7.1 %collective-permute-start.10 = (bf16[288,128]{1,0:T(8,128)(2,1)S(1)}, bf16[288,128]{1,0:T(8,128)(2,1)S(1)}, u32[]{:S(2)}, u32[]{:S(2)}) collective-permute-start(bf16[288,128]{1,0:T(8,128)(2,1)S(1)} %add_convert_fusion.1.refs_0_), channel_id=1, source_target_pairs={{0,4},{4,8},{8,12},{12,0},{1,5},{5,9},{9,13},{13,1},{2,6},{6,10},{... | collective-permute-start | bytes 221192 | tf_op jit(solution)/shard_map/ppermute | solution.py:299
  23.2 7.8 %collective-permute-start.11 = (bf16[288,128]{1,0:T(8,128)(2,1)S(1)}, bf16[288,128]{1,0:T(8,128)(2,1)S(1)}, u32[]{:S(2)}, u32[]{:S(2)}) collective-permute-start(bf16[288,128]{1,0:T(8,128)(2,1)S(1)} %add_convert_fusion.1.refs_0_), channel_id=1, source_target_pairs={{0,8},{4,12},{8,0},{12,4},{1,9},{5,13},{9,1},{13,5},{2,10},{6,14},... | collective-permute-start | bytes 221192 | tf_op jit(solution)/shard_map/ppermute | solution.py:299
  25.8 5.2 %collective-permute-start.12 = (bf16[288,128]{1,0:T(8,128)(2,1)S(1)}, bf16[288,128]{1,0:T(8,128)(2,1)S(1)}, u32[]{:S(2)}, u32[]{:S(2)}) collective-permute-start(bf16[288,128]{1,0:T(8,128)(2,1)S(1)} %add_convert_fusion.1.refs_0_), channel_id=1, source_target_pairs={{0,12},{4,0},{8,4},{12,8},{1,13},{5,1},{9,5},{13,9},{2,14},{6,2},{... | collective-permute-start | bytes 221192 | tf_op jit(solution)/shard_map/ppermute | solution.py:299
  27.1 9.9 %collective-permute-start.8 = (bf16[576,256]{1,0:T(8,128)(2,1)S(1)}, bf16[576,256]{1,0:T(8,128)(2,1)S(1)}, u32[]{:S(2)}, u32[]{:S(2)}) collective-permute-start(bf16[576,256]{1,0:T(8,128)(2,1)S(1)} %bitcast.11), channel_id=1, source_target_pairs={{0,2},{2,0},{1,3},{3,1},{4,6},{6,4},{5,7},{7,5},{8,10},{10,8},{9,1... | collective-permute-start | bytes 884744 | tf_op jit(solution)/shard_map/ppermute | solution.py:299
  28.6 14.6 %copy-start = (bf16[2304,512]{1,0:T(8,128)(2,1)S(1)}, bf16[2304,512]{1,0:T(8,128)(2,1)}, u32[]{:S(2)}) copy-start(bf16[2304,512]{1,0:T(8,128)(2,1)} %refs_2_.1) | copy-start | bytes 7077892
  31.0 10.0 %collective-permute-start.14 = (bf16[1152,128]{1,0:T(8,128)(2,1)S(1)}, bf16[1152,128]{1,0:T(8,128)(2,1)S(1)}, u32[]{:S(2)}, u32[]{:S(2)}) collective-permute-start(bf16[1152,128]{1,0:T(8,128)(2,1)S(1)} %shard_map.152), channel_id=1, source_target_pairs={{0,2},{2,0},{1,3},{3,1},{4,6},{6,4},{5,7},{7,5},{8,10},{10,8},{9,1... | collective-permute-start | bytes 884744 | tf_op jit(solution)/shard_map/ppermute | solution.py:299
  31.4 14.5 %collective-permute-start.15 = (bf16[448,128]{1,0:T(8,128)(2,1)S(1)}, bf16[448,128]{1,0:T(8,128)(2,1)S(1)}, u32[]{:S(2)}, u32[]{:S(2)}) collective-permute-start(bf16[448,128]{1,0:T(8,128)(2,1)S(1)} %add_convert_fusion.refs_0_), channel_id=1, source_target_pairs={{0,4},{4,8},{8,12},{12,0},{1,5},{5,9},{9,13},{13,1},{2,6},{6,10},{... | collective-permute-start | bytes 344072 | tf_op jit(solution)/shard_map/ppermute | solution.py:299
  32.8 13.0 %collective-permute-start.16 = (bf16[448,128]{1,0:T(8,128)(2,1)S(1)}, bf16[448,128]{1,0:T(8,128)(2,1)S(1)}, u32[]{:S(2)}, u32[]{:S(2)}) collective-permute-start(bf16[448,128]{1,0:T(8,128)(2,1)S(1)} %add_convert_fusion.refs_0_), channel_id=1, source_target_pairs={{0,8},{4,12},{8,0},{12,4},{1,9},{5,13},{9,1},{13,5},{2,10},{6,14},... | collective-permute-start | bytes 344072 | tf_op jit(solution)/shard_map/ppermute | solution.py:299
  34.8 11.1 %collective-permute-start.17 = (bf16[448,128]{1,0:T(8,128)(2,1)S(1)}, bf16[448,128]{1,0:T(8,128)(2,1)S(1)}, u32[]{:S(2)}, u32[]{:S(2)}) collective-permute-start(bf16[448,128]{1,0:T(8,128)(2,1)S(1)} %add_convert_fusion.refs_0_), channel_id=1, source_target_pairs={{0,12},{4,0},{8,4},{12,8},{1,13},{5,1},{9,5},{13,9},{2,14},{6,2},{... | collective-permute-start | bytes 344072 | tf_op jit(solution)/shard_map/ppermute | solution.py:299
  37.1 6.1 %collective-permute-start.9 = (bf16[576,256]{1,0:T(8,128)(2,1)S(1)}, bf16[576,256]{1,0:T(8,128)(2,1)S(1)}, u32[]{:S(2)}, u32[]{:S(2)}) collective-permute-start(bf16[576,256]{1,0:T(8,128)(2,1)S(1)} %collective-permute-done.8.refs_1_), channel_id=1, source_target_pairs={{0,1},{1,0},{2,3},{3,2},{4,5},{5,4},{6,7},{7,6},{8,9},{9,8},{10,11... | collective-permute-start | bytes 884744 | tf_op jit(solution)/shard_map/ppermute | solution.py:295
  43.2 1.4 %copy-start.6 = (s32[256]{0:T(256)S(1)}, s32[256]{0:T(256)}, u32[]{:S(2)}) copy-start(s32[256]{0:T(256)} %param.17) | copy-start | bytes 3076
  48.4 13.2 %copy-start.8 = (s32[2]{0:T(128)S(1)}, s32[2]{0:T(128)}, u32[]{:S(2)}) copy-start(s32[2]{0:T(128)} %lens_ref.3) | copy-start | bytes 28
  55.0 5.6 %collective-permute-start.18 = (f32[8,256]{1,0:T(8,128)S(1)}, f32[8,256]{1,0:T(8,128)S(1)}, u32[]{:S(2)}, u32[]{:S(2)}) collective-permute-start(f32[8,256]{1,0:T(8,128)S(1)} %shard_map.156.refs_0_), channel_id=1, source_target_pairs={{0,4},{4,8},{8,12},{12,0},{1,5},{5,9},{9,13},{13,1},{2,6},{6,10},{... | collective-permute-start | bytes 24584 | tf_op jit(solution)/shard_map/ppermute | solution.py:299
  55.8 4.8 %collective-permute-start.19 = (f32[8,256]{1,0:T(8,128)S(1)}, f32[8,256]{1,0:T(8,128)S(1)}, u32[]{:S(2)}, u32[]{:S(2)}) collective-permute-start(f32[8,256]{1,0:T(8,128)S(1)} %shard_map.156.refs_0_), channel_id=1, source_target_pairs={{0,8},{4,12},{8,0},{12,4},{1,9},{5,13},{9,1},{13,5},{2,10},{6,14},... | collective-permute-start | bytes 24584 | tf_op jit(solution)/shard_map/ppermute | solution.py:299
  58.0 3.7 %collective-permute-start.20 = (f32[8,256]{1,0:T(8,128)S(1)}, f32[8,256]{1,0:T(8,128)S(1)}, u32[]{:S(2)}, u32[]{:S(2)}) collective-permute-start(f32[8,256]{1,0:T(8,128)S(1)} %shard_map.156.refs_0_), channel_id=1, source_target_pairs={{0,12},{4,0},{8,4},{12,8},{1,13},{5,1},{9,5},{13,9},{2,14},{6,2},{... | collective-permute-start | bytes 24584 | tf_op jit(solution)/shard_map/ppermute | solution.py:299

commit v4 on v2

--- a/solution.py
+++ b/solution.py
@@ -53,6 +53,11 @@
     return lax.rem(lax.axis_index(axis) - offset + count, count)
 
 
+def block_place(n):
+    core = lax.axis_index("core")
+    return behind("x", n // CORES) * CORES + (core if n % CORES == 0 else 1 - core)
+
+
 def vocab_base(vocab):
     place = lax.axis_index("sv") * lax.axis_size("x") + lax.axis_index("x")
     return (place * CORES + lax.axis_index("core")) * vocab
@@ -65,18 +70,23 @@
     return copies
 
 
-def pack_kernel(q_ref, k_ref, out_ref, sems):
+def prepare(q_ref, k_ref, own_s, own_w, qk_ref, keep_ref, give_ref, s_v, w_v, sems):
     rows = q_ref.shape[0]
-    for copy in fetch(sems, (q_ref, out_ref.at[:rows]), (k_ref, out_ref.at[rows:])):
+    qk_pairs = (q_ref, qk_ref.at[:rows]), (k_ref, qk_ref.at[rows:])
+    copies = fetch(sems, (own_s, s_v), (own_w, w_v), *qk_pairs)
+    for copy in copies:
         copy.wait()
-
-
-def project(states, matrix, *out_refs):
-    *shares, total = out_refs
-    total[...] = dot00(matrix[...], states[:, part_of(lax.axis_index("core"), total.shape[1])])
+    core = lax.axis_index("core")
+    tokens = keep_ref.shape[1]
+    give_ref[...] = dot00(w_v[...], s_v[:, part_of(1 - core, tokens)])
+    keep_ref[...] = dot00(w_v[...], s_v[:, part_of(core, tokens)])
+
+
+def share_out(keep_ref, got_ref, *shares):
     rows = shares[0].shape[0]
     for n, share in enumerate(shares):
-        share[...] = total[part_of(behind("x", lax.axis_size("x") - n), rows), :]
+        place = part_of(behind("x", lax.axis_size("x") - n), rows) if len(shares) > 1 else slice(None)
+        share[...] = keep_ref[place, :] + got_ref[place, :]
 
 
 def collect(axis, *refs):
@@ -139,9 +149,15 @@
     return packed
 
 
-def own_student(targets, *refs):
-    *blocks, head, out_ref, notes_ref, s_all = refs
-    collect("x", *blocks, s_all)
+def own_student(targets, own_s, mate_s, *refs):
+    *chips, head, out_ref, notes_ref, s_all, sems = refs
+    rows = own_s.shape[0]
+    copies = fetch(sems, (own_s, s_all.at[part_of(block_place(0), rows), :]))
+    s_all[part_of(block_place(1), rows), :] = mate_s[...]
+    for n, chip in enumerate(chips):
+        s_all[part_of(behind("x", n + 1), CORES * rows), :] = chip[...]
+    for copy in copies:
+        copy.wait()
     logits = dot00(s_all[...], head[...])
     out_ref[...] = logits
     columns = target_column(targets, vocab_base(head.shape[1]))
@@ -150,13 +166,13 @@
 
 
 def own_teacher(weights_ref, *refs):
-    *blocks, head, own_ref, t_all = refs
+    *chips, head, own_ref, t_all = refs
     sequences, width, _ = weights_ref.shape
-    rows = blocks[0].shape[0]
-    for n, block in enumerate(blocks):
+    rows = chips[0].shape[0]
+    for n, chip in enumerate(chips):
         for s in range(sequences):
             tokens = slice(s * width, (s + 1) * width)
-            aligned = dot10(block[:, tokens], weights_ref[s]).astype(BF16)
+            aligned = dot10(chip[:, tokens], weights_ref[s]).astype(BF16)
             t_all[part_of(behind("x", n), rows), tokens] = aligned
     own_ref[...] = dot00(t_all[...], head[...])
 
@@ -212,8 +228,9 @@
     return total, s_spread, s_picked, t_spread, t_picked
 
 
-def merge_kernel(parts, in_ref, out_ref):
-    total, *rest = merge_stats([in_ref[n * STATS : (n + 1) * STATS, :] for n in range(parts)])
+def merge_kernel(*refs):
+    *parts, out_ref = refs
+    total, *rest = merge_stats([part[...] for part in parts])
     row = lax.broadcasted_iota(jnp.int32, total.shape, 0)
     for k, value in enumerate(rest):
         total = jnp.where(row == 4 + k, value, total)
@@ -281,6 +298,9 @@
     def both(a):
         return lax.all_gather(a, "core", axis=0, tiled=True)
 
+    def swap(a):
+        return lax.ppermute(a, "core", [(0, 1), (1, 0)])
+
     def shift(a, axis, n):
         count = lax.axis_size(axis)
         return lax.ppermute(a, axis, [(i, (i + n) % count) for i in range(count)])
@@ -296,25 +316,26 @@
     w_t, w_s = to_teacher, to_student.T
     s_targets, t_targets = student_targets.reshape(1, rows), teacher_targets.reshape(1, rows)
 
-    q_t, k_t = student_queries.T, teacher_keys.T
-    qk = kernel_call(
-        pack_kernel, shape((2 * q_t.shape[0], rows), BF16), [HBM] * 2, [dma((2,))], limit=60
-    )(q_t, k_t)
+    qk, keep, give = kernel_call(
+        prepare,
+        [shape((2 * student_queries.shape[1], rows), BF16)] + [shape((w_t.shape[1], tokens))] * 2,
+        [HBM] * 4,
+        [pltpu.VMEM(a.shape, BF16) for a in (s_t, w_t)] + [dma((4,))],
+        limit=60,
+    )(student_queries.T, teacher_keys.T, s_t, w_t)
+    got = swap(give)
     qk_blocks = [qk] + around(qk, "x") + [cross(qk, n) for n in range(chips)]
-    chip_s, chip_w_t = (both(a) for a in after((s_t, w_t), qk))
-    far_s, far_t = after((s_t, t_t), qk)
-    far_s, far_t = around(far_s, "x"), around(far_t, "x")
     split = chips if w_t.shape[1] % (16 * chips) == 0 else 1
-    share = shape((w_t.shape[1] // split, tokens))
-    (chip_s, chip_w_t), qk_blocks = lax.optimization_barrier(((chip_s, chip_w_t), qk_blocks))
-    *parts_t, _ = kernel_call(
-        project, [share] * split + [shape((w_t.shape[1], tokens))], [VMEM] * 2
-    )(chip_s, chip_w_t)
-
-    t_out, w_out, *parts_t = lax.optimization_barrier((t_t, w_s, *parts_t))
+    parts_t = kernel_call(
+        share_out, [shape((w_t.shape[1] // split, tokens))] * split, [VMEM] * 2
+    )(keep, got)
+
+    s_out, t_out, w_out, *parts_t = lax.optimization_barrier((s_t, t_t, w_s, *parts_t))
     other_t = [shift(parts_t[n % split], "x", n) for n in range(1, chips)]
-    chip_t, chip_w_s = both(t_out), both(w_out)
-    features = q_t.shape[0] * chips * CORES
+    chip_w_s, chip_t = both(w_out), both(t_out)
+    mate_s = swap(s_out)
+    far_s = around(after((s_t,), chip_t, chip_w_s)[0], "x")
+    features = student_queries.shape[1] * chips * CORES
     part_s, weights = kernel_call(
         functools.partial(attend, len(qk_blocks)),
         (shape((w_s.shape[0], tokens)), shape((sequences, width, width), BF16)),
@@ -322,37 +343,39 @@
         [pltpu.VMEM((features, rows), BF16)] * 2,
     )(teacher_lengths, chip_t, chip_w_s, *qk_blocks)
 
-    own_part, *other_t, part_s = lax.optimization_barrier((parts_t[0], *other_t, part_s))
+    own_part, *other_t, part_s, mate_s = lax.optimization_barrier(
+        (parts_t[0], *other_t, part_s, mate_s)
+    )
     into_t = functools.reduce(jnp.add, other_t, own_part).astype(BF16)
     into_t = [into_t] + around(into_t, "sv")
     other_s = around(part_s, "x")
-
-    far_s, far_t = [both(a) for a in far_s], [both(a) for a in far_t]
-
-    *into_t, part_s = lax.optimization_barrier((*into_t, part_s))
-    other_s = after(other_s, *into_t)
-    into_s = functools.reduce(jnp.add, other_s, part_s).astype(BF16)
-    into_s = [into_s] + around(into_s, "sv")
+    far_t = around(after((t_t,), *other_t)[0], "x")
+    s_blocks = [both(a) for a in after(far_s, *other_t)]
+
+    logits = shape((rows, vocab))
+    s_own, s_notes = kernel_call(
+        own_student,
+        (logits, shape((rows, 128))),
+        [VMEM, HBM] + [VMEM] * (2 + len(s_blocks)),
+        [pltpu.VMEM((student_head.shape[0], rows), BF16), dma((1,))],
+    )(s_targets, s_t, mate_s, *s_blocks, student_head)
+
+    *into_t, part_s, other_s, s_own = lax.optimization_barrier((*into_t, part_s, other_s, s_own))
     into_t = kernel_call(
         functools.partial(collect, "sv"),
         shape((sv_count * into_t[0].shape[0], tokens), BF16),
         [VMEM] * sv_count,
     )(*into_t)
+    into_t, part_s = lax.optimization_barrier((into_t, part_s))
+    into_s = functools.reduce(jnp.add, other_s, part_s).astype(BF16)
+    into_s = [into_s] + around(into_s, "sv")
     t_shares = [into_t] + (around(into_t, "x") if split > 1 else [])
-    t_shares = [both(a) for a in lax.optimization_barrier(tuple(t_shares))]
-    s_blocks = [chip_s] + far_s
-    t_blocks = [chip_t] + far_t
-    logits = shape((rows, vocab))
-    s_own, s_notes = kernel_call(
-        own_student,
-        (logits, shape((rows, 128))),
-        [VMEM] * (2 + chips),
-        [pltpu.VMEM((student_head.shape[0], rows), BF16)],
-    )(s_targets, *s_blocks, student_head)
+    t_shares = [both(a) for a in t_shares]
+    t_blocks = [chip_t] + [both(a) for a in far_t]
     t_own = kernel_call(
         own_teacher,
         logits,
-        [VMEM] * (2 + chips),
+        [VMEM] * (2 + len(t_blocks)),
         [pltpu.VMEM((teacher_head.shape[0], rows), BF16)],
     )(weights, *t_blocks, teacher_head)
     t_mapped, t_stats = kernel_call(
@@ -366,15 +389,13 @@
         functools.partial(collect, "sv"),
         shape((sv_count * into_s[0].shape[0], tokens), BF16),
         [VMEM] * sv_count,
-    )(*into_s)
+    )(*after(into_s, t_stats))
     s_mapped, stats = kernel_call(
         student_side, (logits, shape((STATS, rows))), [VMEM] * 6
     )(s_targets, t_stats, s_own, s_notes, both(into_s), student_head)
 
-    stats = lax.all_gather(stats, ("x", "core"), axis=0, tiled=True)
-    stats = kernel_call(
-        functools.partial(merge_kernel, chips * CORES), shape((STATS, rows)), [VMEM]
-    )(stats)
+    stats = [stats] + around(stats, "x") + [cross(stats, n) for n in range(chips)]
+    stats = kernel_call(merge_kernel, shape((STATS, rows)), [VMEM] * len(stats))(*stats)
     stats = [stats] + around(stats, "sv")
     s_loss, t_loss, s_grad, t_grad = kernel_call(
         functools.partial(finish, sv_count),

time: 71.5 us -> 61.7 us (0.86)
  blocking collectives: 26.2 us -> 16.3 us
  waiting for transfers between devices: 8.61 us -> 5.7 us
  starting transfers between devices: 24.2 us -> 25.9 us
  local copies, waits for them, and re-layouts: 0.04 us -> 1.01 us
    all_gather x1 -> x0, blocking collectives: 5.18 us -> none  [body(): stats = lax.all_gather(stats, ('x', 'core'), axis=0, tiled=True)]
    all_gather x9 -> x7, blocking collectives: 21 us -> 16.3 us  [both(): return lax.all_gather(a, 'core', axis=0, tiled=True)]
    ppermute x15 -> x16, waiting for transfers between devices: 8.61 us -> 4.76 us  [shift(): return lax.ppermute(a, axis, [(i, (i + n) % count) for i in range(count)])]
    unnamed x20 -> x22, local copies, waits for them, and re-layouts: 0.04 us -> 1.01 us
    ppermute x2 -> x4, waiting for transfers between devices: 0.01 us -> 0.93 us  [cross(): return lax.ppermute(a, ('x', 'core'), pairs)]
    ppermute x15 -> x16, starting transfers between devices: 24 us -> 24.5 us  [shift(): return lax.ppermute(a, axis, [(i, (i + n) % count) for i in range(count)])]
  transfers between devices with their start and end apart: 17 -> 22, of which waited for: 6 -> 6; matrix products, arithmetic and copies ran while one was open for 0% -> 0% of each run, Pallas kernels for 7% -> 9%
where the time goes in v4:
time: 61.7 us; the launch traced here: 61.5 us
  starting transfers between devices  25.9 us (42%)
  blocking collectives  16.3 us (26%)
  Pallas kernels  11.7 us (19%)
  waiting for transfers between devices  5.7 us (9%)
  local copies, waits for them, and re-layouts  1.01 us (2%)
  between operations  0.81 us (1%)
    ppermute x16, starting transfers between devices, shift(): return lax.ppermute(a, axis, [(i, (i + n) % count) for i in range(count)])  24.5 us
    all_gather x7, blocking collectives, both(): return lax.all_gather(a, 'core', axis=0, tiled=True)  16.3 us
    ppermute x16, waiting for transfers between devices, shift(): return lax.ppermute(a, axis, [(i, (i + n) % count) for i in range(count)])  4.76 us
    pallas_call x1, Pallas kernels, body(): kernel_call(prepare, [shape((2 * student_queries.shape[1], rows), BF16)]...  2.64 us
    pallas_call x1, Pallas kernels, body(): kernel_call(functools.partial(finish, sv_count), (shape((1, rows)), shape...  2.1 us
    pallas_call x1, Pallas kernels, body(): kernel_call(functools.partial(attend, len(qk_blocks)), (shape((w_s.shape[...  1.48 us
    pallas_call x1, Pallas kernels, body(): kernel_call(student_side, (logits, shape((STATS, rows))), [VMEM] * 6)  1.42 us
    pallas_call x1, Pallas kernels, body(): kernel_call(mapped_teacher, (logits, shape((STATS, rows))), [VMEM] * (3 +...  1.36 us
  transfers between devices with their start and end apart: 22, of which 6 were waited for; matrix products, arithmetic and copies ran while one was open for 0% of the time, Pallas kernels for 9%

profile of v4, /device:TPU:0, one launch (start us, length us, event | category | flops | bytes accessed | tf_op | source)
XLA Modules:
  0.0 61.5 jit_solution(12734510620877197985)
XLA Ops:
  0.6 0.0 copy-start.2
  0.7 2.6 %shard_map.147 = (bf16[128,256]{1,0:T(8,128)(2,1)}, f32[576,128]{1,0:T(8,128)}, f32[576,128]{1,0:T(8,128)}) custom-call(bf16[64,256]{1,0:T(8,128)(2,1)} %bitcast.21, bf16[64,256]{1,0:T(8,128)(2,1)} %bitcast.22, bf16[448,256]{1,0:T(8,128)(2,1)} %bitcast.9, bf16[448,576]{1,0:T(8,128)(2,1)} %own_w.1), custom_call_target="tpu_custom_call" | custom-call | tf_op jit(solution)/shard_map/pallas_call | solution.py:319
  3.3 0.5 collective-permute-start
  3.8 2.6 %collective-permute-start.2 = (bf16[128,256]{1,0:T(8,128)(2,1)}, bf16[128,256]{1,0:T(8,128)(2,1)S(1)}, u32[]{:S(2)}, u32[]{:S(2)}) collective-permute-start(bf16[128,256]{1,0:T(8,128)(2,1)} %get-tuple-element.54.refs_0_), channel_id=1, source_target_pairs={{0,2},{2,0},{1,3},{3,1},{4,6},{6,4},{5,7},{7,5},{8,10},{10,8},{9,1... | collective-permute-start | bytes 196616 | tf_op jit(solution)/shard_map/ppermute | solution.py:306
  6.4 0.2 collective-permute-start.3
  6.6 0.0 collective-permute-start.4
  6.6 0.0 collective-permute-done.got_ref
  6.6 1.0 %copy-done.3 = f32[576,128]{1,0:T(8,128)S(1)} copy-done((f32[576,128]{1,0:T(8,128)S(1)}, f32[576,128]{1,0:T(8,128)}, u32[]{:S(2)}) %copy-start.3) | copy-done | bytes 294936
  7.6 2.0 %collective-permute-start.1 = (f32[288,128]{1,0:T(8,128)S(1)}, f32[288,128]{1,0:T(8,128)S(1)}, u32[]{:S(2)}, u32[]{:S(2)}) collective-permute-start(f32[288,128]{1,0:T(8,128)S(1)} %get-tuple-element.51), channel_id=1, source_target_pairs={{0,2},{2,0},{1,3},{3,1},{4,6},{6,4},{5,7},{7,5},{8,10},{10,8},{9,1... | collective-permute-start | bytes 442376 | tf_op jit(solution)/shard_map/ppermute | solution.py:306
  9.6 2.7 %all_gather.22.matrix = bf16[896,576]{1,0:T(8,128)(2,1)S(1)} all-gather(bf16[448,576]{1,0:T(8,128)(2,1)S(1)} %bitcast.18), channel_id=1, replica_groups=mesh['grp'=2,'sv'=4,'x'=2,'core'=2] {'core'}, dimensions={0}, use_global_device_ids=true | all-gather | bytes 1548288 | tf_op jit(solution)/shard_map/all_gather | solution.py:299
  12.4 2.3 %all_gather.21.states.refs_0_ = bf16[1152,256]{1,0:T(8,128)(2,1)S(1)} all-gather(bf16[576,256]{1,0:T(8,128)(2,1)S(1)} %bitcast.19), channel_id=1, replica_groups=mesh['grp'=2,'sv'=4,'x'=2,'core'=2] {'core'}, dimensions={0}, use_global_device_ids=true | all-gather | bytes 884736 | tf_op jit(solution)/shard_map/all_gather | solution.py:299
  14.7 0.1 collective-permute-start.10
  14.9 0.0 collective-permute-done.4.refs_3_
  14.9 1.5 %shard_map.149 = (f32[448,128]{1,0:T(8,128)S(1)}, bf16[2,128,128]{2,1,0:T(8,128)(2,1)S(1)}) custom-call(s32[2]{0:T(128)S(1)} %copy-done.7, bf16[1152,256]{1,0:T(8,128)(2,1)S(1)} %all_gather.21.states.refs_0_, bf16[896,576]{1,0:T(8,128)(2,1)S(1)} %all_gather.22.matrix, bf16[128,256]{1,0:T(8,128)(2,1)S(1)} %copy-done.4, ...), custom_call_target="tpu_custom_call" | custom-call | tf_op jit(solution)/shard_map/pallas_call | solution.py:339
  16.4 0.0 collective-permute-done.1
  16.4 0.0 collective-permute-done.5.mate_s
  16.4 2.0 %collective-permute-start.9 = (f32[448,128]{1,0:T(8,128)S(1)}, f32[448,128]{1,0:T(8,128)S(1)}, u32[]{:S(2)}, u32[]{:S(2)}) collective-permute-start(f32[448,128]{1,0:T(8,128)S(1)} %get-tuple-element.75), channel_id=1, source_target_pairs={{0,2},{2,0},{1,3},{3,1},{4,6},{6,4},{5,7},{7,5},{8,10},{10,8},{9,1... | collective-permute-start | bytes 688136 | tf_op jit(solution)/shard_map/ppermute | solution.py:306
  18.4 1.6 %collective-permute-start.6 = (bf16[288,128]{1,0:T(8,128)(2,1)S(1)}, bf16[288,128]{1,0:T(8,128)(2,1)S(1)}, u32[]{:S(2)}, u32[]{:S(2)}) collective-permute-start(bf16[288,128]{1,0:T(8,128)(2,1)S(1)} %add_convert_fusion.1.refs_0_), channel_id=1, source_target_pairs={{0,4},{4,8},{8,12},{12,0},{1,5},{5,9},{9,13},{13,1},{2,6},{6,10},{... | collective-permute-start | bytes 221192 | tf_op jit(solution)/shard_map/ppermute | solution.py:306
  20.0 2.6 %collective-permute-start.7 = (bf16[288,128]{1,0:T(8,128)(2,1)S(1)}, bf16[288,128]{1,0:T(8,128)(2,1)S(1)}, u32[]{:S(2)}, u32[]{:S(2)}) collective-permute-start(bf16[288,128]{1,0:T(8,128)(2,1)S(1)} %add_convert_fusion.1.refs_0_), channel_id=1, source_target_pairs={{0,8},{4,12},{8,0},{12,4},{1,9},{5,13},{9,1},{13,5},{2,10},{6,14},... | collective-permute-start | bytes 221192 | tf_op jit(solution)/shard_map/ppermute | solution.py:306
  22.6 1.4 %collective-permute-start.8 = (bf16[288,128]{1,0:T(8,128)(2,1)S(1)}, bf16[288,128]{1,0:T(8,128)(2,1)S(1)}, u32[]{:S(2)}, u32[]{:S(2)}) collective-permute-start(bf16[288,128]{1,0:T(8,128)(2,1)S(1)} %add_convert_fusion.1.refs_0_), channel_id=1, source_target_pairs={{0,12},{4,0},{8,4},{12,8},{1,13},{5,1},{9,5},{13,9},{2,14},{6,2},{... | collective-permute-start | bytes 221192 | tf_op jit(solution)/shard_map/ppermute | solution.py:306
  24.0 0.5 collective-permute-start.11
  24.5 2.1 %all_gather.23.refs_0_ = bf16[896,256]{1,0:T(8,128)(2,1)S(1)} all-gather(bf16[448,256]{1,0:T(8,128)(2,1)S(1)} %collective-permute-done.10), channel_id=1, replica_groups=mesh['grp'=2,'sv'=4,'x'=2,'core'=2] {'core'}, dimensions={0}, use_global_device_ids=true | all-gather | bytes 688128 | tf_op jit(solution)/shard_map/all_gather | solution.py:299
  26.6 1.2 %shard_map.150 = (f32[256,512]{1,0:T(8,128)S(1)}, f32[256,128]{1,0:T(8,128)S(1)}) custom-call(s32[1,256]{1,0:T(1,128)S(1)} %bitcast.13, bf16[448,256]{1,0:T(8,128)(2,1)S(1)} %bitcast.12, bf16[448,256]{1,0:T(8,128)(2,1)S(1)} %collective-permute-done.5.mate_s, bf16[896,256]{1,0:T(8,128)(2,1)S(1)} %all_gather.23.refs_0_, bf16[1792,512]{1,0:T(8,128)(2,1)S(1)} %copy-done.1), custom_call_target="tpu_custom_call" | custom-call | tf_op jit(solution)/shard_map/pallas_call | solution.py:356
  27.8 0.0 copy-start
  27.9 0.2 collective-permute-done.9
  28.2 1.6 %collective-permute-start.13 = (bf16[448,128]{1,0:T(8,128)(2,1)S(1)}, bf16[448,128]{1,0:T(8,128)(2,1)S(1)}, u32[]{:S(2)}, u32[]{:S(2)}) collective-permute-start(bf16[448,128]{1,0:T(8,128)(2,1)S(1)} %add_convert_fusion.refs_0_), channel_id=1, source_target_pairs={{0,4},{4,8},{8,12},{12,0},{1,5},{5,9},{9,13},{13,1},{2,6},{6,10},{... | collective-permute-start | bytes 344072 | tf_op jit(solution)/shard_map/ppermute | solution.py:306
  29.8 2.6 %collective-permute-start.14 = (bf16[448,128]{1,0:T(8,128)(2,1)S(1)}, bf16[448,128]{1,0:T(8,128)(2,1)S(1)}, u32[]{:S(2)}, u32[]{:S(2)}) collective-permute-start(bf16[448,128]{1,0:T(8,128)(2,1)S(1)} %add_convert_fusion.refs_0_), channel_id=1, source_target_pairs={{0,8},{4,12},{8,0},{12,4},{1,9},{5,13},{9,1},{13,5},{2,10},{6,14},... | collective-permute-start | bytes 344072 | tf_op jit(solution)/shard_map/ppermute | solution.py:306
  32.4 1.4 %collective-permute-start.15 = (bf16[448,128]{1,0:T(8,128)(2,1)S(1)}, bf16[448,128]{1,0:T(8,128)(2,1)S(1)}, u32[]{:S(2)}, u32[]{:S(2)}) collective-permute-start(bf16[448,128]{1,0:T(8,128)(2,1)S(1)} %add_convert_fusion.refs_0_), channel_id=1, source_target_pairs={{0,12},{4,0},{8,4},{12,8},{1,13},{5,1},{9,5},{13,9},{2,14},{6,2},{... | collective-permute-start | bytes 344072 | tf_op jit(solution)/shard_map/ppermute | solution.py:306
  33.7 0.5 collective-permute-start.12
  34.3 2.2 %all_gather.25.refs_0_ = bf16[2304,128]{1,0:T(8,128)(2,1)S(1)} all-gather(bf16[1152,128]{1,0:T(8,128)(2,1)S(1)} %shard_map.152), channel_id=1, replica_groups=mesh['grp'=2,'sv'=4,'x'=2,'core'=2] {'core'}, dimensions={0}, use_global_device_ids=true | all-gather | bytes 884736 | tf_op jit(solution)/shard_map/all_gather | solution.py:299
  36.5 2.2 %all_gather.24.refs_1_ = bf16[1152,256]{1,0:T(8,128)(2,1)S(1)} all-gather(bf16[576,256]{1,0:T(8,128)(2,1)S(1)} %collective-permute-done.11), channel_id=1, replica_groups=mesh['grp'=2,'sv'=4,'x'=2,'core'=2] {'core'}, dimensions={0}, use_global_device_ids=true | all-gather | bytes 884736 | tf_op jit(solution)/shard_map/all_gather | solution.py:299
  38.7 1.3 %shard_map.151.own_ref.to_ref = f32[256,512]{1,0:T(8,128)S(1)} custom-call(bf16[2,128,128]{2,1,0:T(8,128)(2,1)S(1)} %get-tuple-element.65.weights_ref, bf16[1152,256]{1,0:T(8,128)(2,1)S(1)} %all_gather.21.states.refs_0_, bf16[1152,256]{1,0:T(8,128)(2,1)S(1)} %all_gather.24.refs_1_, bf16[2304,512]{1,0:T(8,128)(2,1)S(1)} %copy-done), custom_call_target="tpu_custom_call" | custom-call | tf_op jit(solution)/shard_map/pallas_call | solution.py:375
  40.1 0.9 %collective-permute-done.12 = bf16[1152,128]{1,0:T(8,128)(2,1)S(1)} collective-permute-done((bf16[1152,128]{1,0:T(8,128)(2,1)S(1)}, bf16[1152,128]{1,0:T(8,128)(2,1)S(1)}, u32[]{:S(2)}, u32[]{:S(2)}) %collective-permute-start.12) | collective-permute-done | bytes 294944 | tf_op jit(solution)/shard_map/ppermute | solution.py:306
  40.9 2.2 %all_gather.26.refs_1_ = bf16[2304,128]{1,0:T(8,128)(2,1)S(1)} all-gather(bf16[1152,128]{1,0:T(8,128)(2,1)S(1)} %collective-permute-done.12), channel_id=1, replica_groups=mesh['grp'=2,'sv'=4,'x'=2,'core'=2] {'core'}, dimensions={0}, use_global_device_ids=true | all-gather | bytes 884736 | tf_op jit(solution)/shard_map/all_gather | solution.py:299
  43.2 1.4 %shard_map.153 = (f32[256,512]{1,0:T(8,128)S(1)}, f32[8,256]{1,0:T(8,128)S(1)}) custom-call(s32[1,256]{1,0:T(1,128)S(1)} %bitcast.16, f32[256,512]{1,0:T(8,128)S(1)} %shard_map.151.own_ref.to_ref, bf16[2304,128]{1,0:T(8,128)(2,1)S(1)} %all_gather.25.refs_0_, bf16[2304,128]{1,0:T(8,128)(2,1)S(1)} %all_gather.26.refs_1_, bf16[2304,512]{1,0:T(8,128)(2,1)S(1)} %copy-done), custom_call_target="tpu_custom_call" | custom-call | tf_op jit(solution)/shard_map/pallas_call | solution.py:381
  44.5 0.0 collective-permute-done.15.refs_3_
  44.6 2.5 %all_gather.27.halves = bf16[3584,128]{1,0:T(8,128)(2,1)S(1)} all-gather(bf16[1792,128]{1,0:T(8,128)(2,1)S(1)} %shard_map.154), channel_id=1, replica_groups=mesh['grp'=2,'sv'=4,'x'=2,'core'=2] {'core'}, dimensions={0}, use_global_device_ids=true | all-gather | bytes 1376256 | tf_op jit(solution)/shard_map/all_gather | solution.py:299
  47.0 1.4 %shard_map.155 = (f32[256,512]{1,0:T(8,128)S(1)}, f32[8,256]{1,0:T(8,128)S(1)}) custom-call(s32[1,256]{1,0:T(1,128)S(1)} %bitcast.14, f32[8,256]{1,0:T(8,128)S(1)} %get-tuple-element.73.t_stats, f32[256,512]{1,0:T(8,128)S(1)} %get-tuple-element.64.own_ref.so_ref, f32[256,128]{1,0:T(8,128)S(1)} %get-tuple-element.74.notes_ref, ...), custom_call_target="tpu_custom_call" | custom-call | tf_op jit(solution)/shard_map/pallas_call | solution.py:393
  48.5 1.5 %collective-permute-start.16 = (f32[8,256]{1,0:T(8,128)S(1)}, f32[8,256]{1,0:T(8,128)S(1)}, u32[]{:S(2)}, u32[]{:S(2)}) collective-permute-start(f32[8,256]{1,0:T(8,128)S(1)} %get-tuple-element.83.refs_0_), channel_id=1, source_target_pairs={{0,2},{2,0},{1,3},{3,1},{4,6},{6,4},{5,7},{7,5},{8,10},{10,8},{9,1... | collective-permute-start | bytes 24584 | tf_op jit(solution)/shard_map/ppermute | solution.py:306
  50.0 0.6 %collective-permute-start.18 = (f32[8,256]{1,0:T(8,128)S(1)}, f32[8,256]{1,0:T(8,128)S(1)}, u32[]{:S(2)}, u32[]{:S(2)}) collective-permute-start(f32[8,256]{1,0:T(8,128)S(1)} %get-tuple-element.83.refs_0_), channel_id=1, source_target_pairs={{0,3},{1,2},{2,1},{3,0},{4,7},{5,6},{6,5},{7,4},{8,11},{9,10},{10,... | collective-permute-start | bytes 24584 | tf_op jit(solution)/shard_map/ppermute | solution.py:313
  50.6 1.5 %collective-permute-done.16.refs_1_ = f32[8,256]{1,0:T(8,128)S(1)} collective-permute-done((f32[8,256]{1,0:T(8,128)S(1)}, f32[8,256]{1,0:T(8,128)S(1)}, u32[]{:S(2)}, u32[]{:S(2)}) %collective-permute-start.16) | collective-permute-done | bytes 8224 | tf_op jit(solution)/shard_map/ppermute | solution.py:306
  52.2 0.9 %collective-permute-done.18.refs_3_ = f32[8,256]{1,0:T(8,128)S(1)} collective-permute-done((f32[8,256]{1,0:T(8,128)S(1)}, f32[8,256]{1,0:T(8,128)S(1)}, u32[]{:S(2)}, u32[]{:S(2)}) %collective-permute-start.18) | collective-permute-done | bytes 8224 | tf_op jit(solution)/shard_map/ppermute | solution.py:313
  53.1 0.7 %collective-permute-start.19 = (f32[8,256]{1,0:T(8,128)S(1)}, f32[8,256]{1,0:T(8,128)S(1)}, u32[]{:S(2)}, u32[]{:S(2)}) collective-permute-start(f32[8,256]{1,0:T(8,128)S(1)} %shard_map.156.refs_0_), channel_id=1, source_target_pairs={{0,4},{4,8},{8,12},{12,0},{1,5},{5,9},{9,13},{13,1},{2,6},{6,10},{... | collective-permute-start | bytes 24584 | tf_op jit(solution)/shard_map/ppermute | solution.py:306
  53.9 1.9 %collective-permute-start.20 = (f32[8,256]{1,0:T(8,128)S(1)}, f32[8,256]{1,0:T(8,128)S(1)}, u32[]{:S(2)}, u32[]{:S(2)}) collective-permute-start(f32[8,256]{1,0:T(8,128)S(1)} %shard_map.156.refs_0_), channel_id=1, source_target_pairs={{0,8},{4,12},{8,0},{12,4},{1,9},{5,13},{9,1},{13,5},{2,10},{6,14},... | collective-permute-start | bytes 24584 | tf_op jit(solution)/shard_map/ppermute | solution.py:306
  55.7 1.5 %collective-permute-start.21 = (f32[8,256]{1,0:T(8,128)S(1)}, f32[8,256]{1,0:T(8,128)S(1)}, u32[]{:S(2)}, u32[]{:S(2)}) collective-permute-start(f32[8,256]{1,0:T(8,128)S(1)} %shard_map.156.refs_0_), channel_id=1, source_target_pairs={{0,12},{4,0},{8,4},{12,8},{1,13},{5,1},{9,5},{13,9},{2,14},{6,2},{... | collective-permute-start | bytes 24584 | tf_op jit(solution)/shard_map/ppermute | solution.py:306
  57.2 1.4 %collective-permute-done.19.refs_1_ = f32[8,256]{1,0:T(8,128)S(1)} collective-permute-done((f32[8,256]{1,0:T(8,128)S(1)}, f32[8,256]{1,0:T(8,128)S(1)}, u32[]{:S(2)}, u32[]{:S(2)}) %collective-permute-start.19) | collective-permute-done | bytes 8224 | tf_op jit(solution)/shard_map/ppermute | solution.py:306
  58.6 0.7 %collective-permute-done.21.refs_3_ = f32[8,256]{1,0:T(8,128)S(1)} collective-permute-done((f32[8,256]{1,0:T(8,128)S(1)}, f32[8,256]{1,0:T(8,128)S(1)}, u32[]{:S(2)}, u32[]{:S(2)}) %collective-permute-start.21) | collective-permute-done | bytes 8224 | tf_op jit(solution)/shard_map/ppermute | solution.py:306
  59.4 2.1 %shard_map.157 = (f32[1,256]{1,0:T(1,128)}, f32[1,256]{1,0:T(1,128)}, bf16[256,512]{1,0:T(8,128)(2,1)}, bf16[256,512]{1,0:T(8,128)(2,1)}) custom-call(s32[2]{0:T(128)S(1)} %copy-done.8, s32[1,256]{1,0:T(1,128)S(1)} %bitcast.15, s32[1,256]{1,0:T(1,128)S(1)} %bitcast.17, f32[256,512]{1,0:T(8,128)S(1)} %get-tuple-element.64.own_ref.so_ref, ...), custom_call_target="tpu_custom_call" | custom-call | tf_op jit(solution)/shard_map/pallas_call | solution.py:400
  (38 shorter events, 0.3 us)
Async XLA Ops:
  0.6 9.0 %copy-start.9 = (bf16[576,448]{0,1:T(8,128)(2,1)S(1)}, bf16[576,448]{0,1:T(8,128)(2,1)}, u32[]{:S(2)}) copy-start(bf16[576,448]{0,1:T(8,128)(2,1)} %param.21) | copy-start | bytes 1548292
  0.6 14.1 %copy-start.2 = (bf16[256,448]{0,1:T(8,128)(2,1)S(1)}, bf16[256,448]{0,1:T(8,128)(2,1)}, u32[]{:S(2)}) copy-start(bf16[256,448]{0,1:T(8,128)(2,1)} %param.12) | copy-start | bytes 688132
  0.7 14.2 %copy-start.7 = (s32[2]{0:T(128)S(1)}, s32[2]{0:T(128)}, u32[]{:S(2)}) copy-start(s32[2]{0:T(128)} %lens_ref.2) | copy-start | bytes 28
  3.3 3.3 %collective-permute-start = (f32[576,128]{1,0:T(8,128)}, f32[576,128]{1,0:T(8,128)S(1)}, u32[]{:S(2)}, u32[]{:S(2)}) collective-permute-start(f32[576,128]{1,0:T(8,128)} %get-tuple-element.47), channel_id=1, source_target_pairs={{0,1},{1,0},{2,3},{3,2},{4,5},{5,4},{6,7},{7,6},{8,9},{9,8},{10,11... | collective-permute-start | bytes 884744 | tf_op jit(solution)/shard_map/ppermute | solution.py:302
  3.8 10.9 %collective-permute-start.2 = (bf16[128,256]{1,0:T(8,128)(2,1)}, bf16[128,256]{1,0:T(8,128)(2,1)S(1)}, u32[]{:S(2)}, u32[]{:S(2)}) collective-permute-start(bf16[128,256]{1,0:T(8,128)(2,1)} %get-tuple-element.54.refs_0_), channel_id=1, source_target_pairs={{0,2},{2,0},{1,3},{3,1},{4,6},{6,4},{5,7},{7,5},{8,10},{10,8},{9,1... | collective-permute-start | bytes 196616 | tf_op jit(solution)/shard_map/ppermute | solution.py:306
  6.4 8.5 %collective-permute-start.3 = (bf16[128,256]{1,0:T(8,128)(2,1)}, bf16[128,256]{1,0:T(8,128)(2,1)S(1)}, u32[]{:S(2)}, u32[]{:S(2)}) collective-permute-start(bf16[128,256]{1,0:T(8,128)(2,1)} %get-tuple-element.54.refs_0_), channel_id=1, source_target_pairs={{0,1},{1,0},{2,3},{3,2},{4,5},{5,4},{6,7},{7,6},{8,9},{9,8},{10,11... | collective-permute-start | bytes 196616 | tf_op jit(solution)/shard_map/ppermute | solution.py:313
  6.6 8.3 %collective-permute-start.4 = (bf16[128,256]{1,0:T(8,128)(2,1)}, bf16[128,256]{1,0:T(8,128)(2,1)S(1)}, u32[]{:S(2)}, u32[]{:S(2)}) collective-permute-start(bf16[128,256]{1,0:T(8,128)(2,1)} %get-tuple-element.54.refs_0_), channel_id=1, source_target_pairs={{0,3},{1,2},{2,1},{3,0},{4,7},{5,6},{6,5},{7,4},{8,11},{9,10},{10,... | collective-permute-start | bytes 196616 | tf_op jit(solution)/shard_map/ppermute | solution.py:313
  6.6 1.0 %copy-start.3 = (f32[576,128]{1,0:T(8,128)S(1)}, f32[576,128]{1,0:T(8,128)}, u32[]{:S(2)}) copy-start(f32[576,128]{1,0:T(8,128)} %get-tuple-element.46.keep_ref) | copy-start | bytes 884740
  7.6 4.8 %copy-start.10 = (bf16[256,576]{0,1:T(8,128)(2,1)S(1)}, bf16[256,576]{0,1:T(8,128)(2,1)}, u32[]{:S(2)}) copy-start(bf16[256,576]{0,1:T(8,128)(2,1)} %param.13) | copy-start | bytes 884740
  7.6 7.3 %copy-start.4 = (bf16[128,256]{1,0:T(8,128)(2,1)S(1)}, bf16[128,256]{1,0:T(8,128)(2,1)}, u32[]{:S(2)}) copy-start(bf16[128,256]{1,0:T(8,128)(2,1)} %get-tuple-element.54.refs_0_) | copy-start | bytes 196612
  7.6 8.8 %collective-permute-start.1 = (f32[288,128]{1,0:T(8,128)S(1)}, f32[288,128]{1,0:T(8,128)S(1)}, u32[]{:S(2)}, u32[]{:S(2)}) collective-permute-start(f32[288,128]{1,0:T(8,128)S(1)} %get-tuple-element.51), channel_id=1, source_target_pairs={{0,2},{2,0},{1,3},{3,1},{4,6},{6,4},{5,7},{7,5},{8,10},{10,8},{9,1... | collective-permute-start | bytes 442376 | tf_op jit(solution)/shard_map/ppermute | solution.py:306
  9.6 6.8 %collective-permute-start.5 = (bf16[448,256]{1,0:T(8,128)(2,1)}, bf16[448,256]{1,0:T(8,128)(2,1)S(1)}, u32[]{:S(2)}, u32[]{:S(2)}) collective-permute-start(bf16[448,256]{1,0:T(8,128)(2,1)} %bitcast.10), channel_id=1, source_target_pairs={{0,1},{1,0},{2,3},{3,2},{4,5},{5,4},{6,7},{7,6},{8,9},{9,8},{10,11... | collective-permute-start | bytes 688136 | tf_op jit(solution)/shard_map/ppermute | solution.py:302
  12.4 14.3 %copy-start.1 = (bf16[1792,512]{1,0:T(8,128)(2,1)S(1)}, bf16[1792,512]{1,0:T(8,128)(2,1)}, u32[]{:S(2)}) copy-start(bf16[1792,512]{1,0:T(8,128)(2,1)} %head.1) | copy-start | bytes 5505028
  12.4 14.3 %copy-start.5 = (s32[256]{0:T(256)S(1)}, s32[256]{0:T(256)}, u32[]{:S(2)}) copy-start(s32[256]{0:T(256)} %param.16) | copy-start | bytes 3076
  14.7 9.2 %collective-permute-start.10 = (bf16[448,256]{1,0:T(8,128)(2,1)S(1)}, bf16[448,256]{1,0:T(8,128)(2,1)S(1)}, u32[]{:S(2)}, u32[]{:S(2)}) collective-permute-start(bf16[448,256]{1,0:T(8,128)(2,1)S(1)} %bitcast.11), channel_id=1, source_target_pairs={{0,2},{2,0},{1,3},{3,1},{4,6},{6,4},{5,7},{7,5},{8,10},{10,8},{9,1... | collective-permute-start | bytes 688136 | tf_op jit(solution)/shard_map/ppermute | solution.py:306
  16.4 11.7 %collective-permute-start.9 = (f32[448,128]{1,0:T(8,128)S(1)}, f32[448,128]{1,0:T(8,128)S(1)}, u32[]{:S(2)}, u32[]{:S(2)}) collective-permute-start(f32[448,128]{1,0:T(8,128)S(1)} %get-tuple-element.75), channel_id=1, source_target_pairs={{0,2},{2,0},{1,3},{3,1},{4,6},{6,4},{5,7},{7,5},{8,10},{10,8},{9,1... | collective-permute-start | bytes 688136 | tf_op jit(solution)/shard_map/ppermute | solution.py:306
  18.4 9.4 %collective-permute-start.6 = (bf16[288,128]{1,0:T(8,128)(2,1)S(1)}, bf16[288,128]{1,0:T(8,128)(2,1)S(1)}, u32[]{:S(2)}, u32[]{:S(2)}) collective-permute-start(bf16[288,128]{1,0:T(8,128)(2,1)S(1)} %add_convert_fusion.1.refs_0_), channel_id=1, source_target_pairs={{0,4},{4,8},{8,12},{12,0},{1,5},{5,9},{9,13},{13,1},{2,6},{6,10},{... | collective-permute-start | bytes 221192 | tf_op jit(solution)/shard_map/ppermute | solution.py:306
  20.0 7.8 %collective-permute-start.7 = (bf16[288,128]{1,0:T(8,128)(2,1)S(1)}, bf16[288,128]{1,0:T(8,128)(2,1)S(1)}, u32[]{:S(2)}, u32[]{:S(2)}) collective-permute-start(bf16[288,128]{1,0:T(8,128)(2,1)S(1)} %add_convert_fusion.1.refs_0_), channel_id=1, source_target_pairs={{0,8},{4,12},{8,0},{12,4},{1,9},{5,13},{9,1},{13,5},{2,10},{6,14},... | collective-permute-start | bytes 221192 | tf_op jit(solution)/shard_map/ppermute | solution.py:306
  22.6 5.2 %collective-permute-start.8 = (bf16[288,128]{1,0:T(8,128)(2,1)S(1)}, bf16[288,128]{1,0:T(8,128)(2,1)S(1)}, u32[]{:S(2)}, u32[]{:S(2)}) collective-permute-start(bf16[288,128]{1,0:T(8,128)(2,1)S(1)} %add_convert_fusion.1.refs_0_), channel_id=1, source_target_pairs={{0,12},{4,0},{8,4},{12,8},{1,13},{5,1},{9,5},{13,9},{2,14},{6,2},{... | collective-permute-start | bytes 221192 | tf_op jit(solution)/shard_map/ppermute | solution.py:306
  24.0 12.5 %collective-permute-start.11 = (bf16[576,256]{1,0:T(8,128)(2,1)S(1)}, bf16[576,256]{1,0:T(8,128)(2,1)S(1)}, u32[]{:S(2)}, u32[]{:S(2)}) collective-permute-start(bf16[576,256]{1,0:T(8,128)(2,1)S(1)} %bitcast.20), channel_id=1, source_target_pairs={{0,2},{2,0},{1,3},{3,1},{4,6},{6,4},{5,7},{7,5},{8,10},{10,8},{9,1... | collective-permute-start | bytes 884744 | tf_op jit(solution)/shard_map/ppermute | solution.py:306
  27.8 10.9 %copy-start = (bf16[2304,512]{1,0:T(8,128)(2,1)S(1)}, bf16[2304,512]{1,0:T(8,128)(2,1)}, u32[]{:S(2)}) copy-start(bf16[2304,512]{1,0:T(8,128)(2,1)} %refs_2_.3) | copy-start | bytes 7077892
  28.2 16.4 %collective-permute-start.13 = (bf16[448,128]{1,0:T(8,128)(2,1)S(1)}, bf16[448,128]{1,0:T(8,128)(2,1)S(1)}, u32[]{:S(2)}, u32[]{:S(2)}) collective-permute-start(bf16[448,128]{1,0:T(8,128)(2,1)S(1)} %add_convert_fusion.refs_0_), channel_id=1, source_target_pairs={{0,4},{4,8},{8,12},{12,0},{1,5},{5,9},{9,13},{13,1},{2,6},{6,10},{... | collective-permute-start | bytes 344072 | tf_op jit(solution)/shard_map/ppermute | solution.py:306
  29.8 14.7 %collective-permute-start.14 = (bf16[448,128]{1,0:T(8,128)(2,1)S(1)}, bf16[448,128]{1,0:T(8,128)(2,1)S(1)}, u32[]{:S(2)}, u32[]{:S(2)}) collective-permute-start(bf16[448,128]{1,0:T(8,128)(2,1)S(1)} %add_convert_fusion.refs_0_), channel_id=1, source_target_pairs={{0,8},{4,12},{8,0},{12,4},{1,9},{5,13},{9,1},{13,5},{2,10},{6,14},... | collective-permute-start | bytes 344072 | tf_op jit(solution)/shard_map/ppermute | solution.py:306
  32.4 12.1 %collective-permute-start.15 = (bf16[448,128]{1,0:T(8,128)(2,1)S(1)}, bf16[448,128]{1,0:T(8,128)(2,1)S(1)}, u32[]{:S(2)}, u32[]{:S(2)}) collective-permute-start(bf16[448,128]{1,0:T(8,128)(2,1)S(1)} %add_convert_fusion.refs_0_), channel_id=1, source_target_pairs={{0,12},{4,0},{8,4},{12,8},{1,13},{5,1},{9,5},{13,9},{2,14},{6,2},{... | collective-permute-start | bytes 344072 | tf_op jit(solution)/shard_map/ppermute | solution.py:306
  33.7 7.2 %collective-permute-start.12 = (bf16[1152,128]{1,0:T(8,128)(2,1)S(1)}, bf16[1152,128]{1,0:T(8,128)(2,1)S(1)}, u32[]{:S(2)}, u32[]{:S(2)}) collective-permute-start(bf16[1152,128]{1,0:T(8,128)(2,1)S(1)} %shard_map.152), channel_id=1, source_target_pairs={{0,2},{2,0},{1,3},{3,1},{4,6},{6,4},{5,7},{7,5},{8,10},{10,8},{9,1... | collective-permute-start | bytes 884744 | tf_op jit(solution)/shard_map/ppermute | solution.py:306
  38.7 4.5 %copy-start.6 = (s32[256]{0:T(256)S(1)}, s32[256]{0:T(256)}, u32[]{:S(2)}) copy-start(s32[256]{0:T(256)} %param.17) | copy-start | bytes 3076
  47.0 12.3 %copy-start.8 = (s32[2]{0:T(128)S(1)}, s32[2]{0:T(128)}, u32[]{:S(2)}) copy-start(s32[2]{0:T(128)} %lens_ref.3) | copy-start | bytes 28
  48.5 3.7 %collective-permute-start.16 = (f32[8,256]{1,0:T(8,128)S(1)}, f32[8,256]{1,0:T(8,128)S(1)}, u32[]{:S(2)}, u32[]{:S(2)}) collective-permute-start(f32[8,256]{1,0:T(8,128)S(1)} %get-tuple-element.83.refs_0_), channel_id=1, source_target_pairs={{0,2},{2,0},{1,3},{3,1},{4,6},{6,4},{5,7},{7,5},{8,10},{10,8},{9,1... | collective-permute-start | bytes 24584 | tf_op jit(solution)/shard_map/ppermute | solution.py:306
  50.0 2.2 %collective-permute-start.17 = (f32[8,256]{1,0:T(8,128)S(1)}, f32[8,256]{1,0:T(8,128)S(1)}, u32[]{:S(2)}, u32[]{:S(2)}) collective-permute-start(f32[8,256]{1,0:T(8,128)S(1)} %get-tuple-element.83.refs_0_), channel_id=1, source_target_pairs={{0,1},{1,0},{2,3},{3,2},{4,5},{5,4},{6,7},{7,6},{8,9},{9,8},{10,11... | collective-permute-start | bytes 24584 | tf_op jit(solution)/shard_map/ppermute | solution.py:313
  50.0 3.1 %collective-permute-start.18 = (f32[8,256]{1,0:T(8,128)S(1)}, f32[8,256]{1,0:T(8,128)S(1)}, u32[]{:S(2)}, u32[]{:S(2)}) collective-permute-start(f32[8,256]{1,0:T(8,128)S(1)} %get-tuple-element.83.refs_0_), channel_id=1, source_target_pairs={{0,3},{1,2},{2,1},{3,0},{4,7},{5,6},{6,5},{7,4},{8,11},{9,10},{10,... | collective-permute-start | bytes 24584 | tf_op jit(solution)/shard_map/ppermute | solution.py:313
  53.1 5.5 %collective-permute-start.19 = (f32[8,256]{1,0:T(8,128)S(1)}, f32[8,256]{1,0:T(8,128)S(1)}, u32[]{:S(2)}, u32[]{:S(2)}) collective-permute-start(f32[8,256]{1,0:T(8,128)S(1)} %shard_map.156.refs_0_), channel_id=1, source_target_pairs={{0,4},{4,8},{8,12},{12,0},{1,5},{5,9},{9,13},{13,1},{2,6},{6,10},{... | collective-permute-start | bytes 24584 | tf_op jit(solution)/shard_map/ppermute | solution.py:306
  53.9 4.8 %collective-permute-start.20 = (f32[8,256]{1,0:T(8,128)S(1)}, f32[8,256]{1,0:T(8,128)S(1)}, u32[]{:S(2)}, u32[]{:S(2)}) collective-permute-start(f32[8,256]{1,0:T(8,128)S(1)} %shard_map.156.refs_0_), channel_id=1, source_target_pairs={{0,8},{4,12},{8,0},{12,4},{1,9},{5,13},{9,1},{13,5},{2,10},{6,14},... | collective-permute-start | bytes 24584 | tf_op jit(solution)/shard_map/ppermute | solution.py:306
  55.7 3.7 %collective-permute-start.21 = (f32[8,256]{1,0:T(8,128)S(1)}, f32[8,256]{1,0:T(8,128)S(1)}, u32[]{:S(2)}, u32[]{:S(2)}) collective-permute-start(f32[8,256]{1,0:T(8,128)S(1)} %shard_map.156.refs_0_), channel_id=1, source_target_pairs={{0,12},{4,0},{8,4},{12,8},{1,13},{5,1},{9,5},{13,9},{2,14},{6,2},{... | collective-permute-start | bytes 24584 | tf_op jit(solution)/shard_map/ppermute | solution.py:306

commit v5 on v4

--- a/solution.py
+++ b/solution.py
@@ -23,13 +23,13 @@
     return jax.ShapeDtypeStruct(dims, dtype)
 
 
-def kernel_call(body, out_shape, in_specs, scratch=(), limit=32):
+def kernel_call(body, out_shape, in_specs, scratch=(), limit=32, outs=VMEM):
     single = not isinstance(out_shape, (tuple, list))
     return pl.pallas_call(
         body,
         out_shape=out_shape,
         in_specs=in_specs,
-        out_specs=VMEM if single else [VMEM] * len(out_shape),
+        out_specs=outs if single else [outs] * len(out_shape),
         scratch_shapes=list(scratch),
         compiler_params=pltpu.CompilerParams(vmem_limit_bytes=limit * 2**20),
 
@@ -70,7 +70,7 @@
     return copies
 
 
-def prepare(q_ref, k_ref, own_s, own_w, qk_ref, keep_ref, give_ref, s_v, w_v, sems):
+def prepare(q_ref, k_ref, own_s, own_w, qk_ref, keep_ref, give_ref, s_v, w_v, total, sems):
     rows = q_ref.shape[0]
     qk_pairs = (q_ref, qk_ref.at[:rows]), (k_ref, qk_ref.at[rows:])
     copies = fetch(sems, (own_s, s_v), (own_w, w_v), *qk_pairs)
@@ -78,8 +78,9 @@
         copy.wait()
     core = lax.axis_index("core")
     tokens = keep_ref.shape[1]
-    give_ref[...] = dot00(w_v[...], s_v[:, part_of(1 - core, tokens)])
-    keep_ref[...] = dot00(w_v[...], s_v[:, part_of(core, tokens)])
+    total[...] = dot00(w_v[...], s_v[...])
+    give_ref[...] = total[:, part_of(1 - core, tokens)]
+    keep_ref[...] = total[:, part_of(core, tokens)]
 
 
 def share_out(keep_ref, got_ref, *shares):
@@ -238,35 +239,39 @@
 
 
 def finish(parts, lens_ref, s_targets, t_targets, so_ref, sm_ref, to_ref, tm_ref, *refs):
-    s_loss, t_loss, s_grad, t_grad = refs[parts:]
+    outs, (s_loss, t_loss, s_grad, t_grad), sems = refs[parts : parts + 4], refs[parts + 4 : parts + 8], refs[-1]
     totals, s_spread, s_picked, t_spread, t_picked = merge_stats([ref[...] for ref in refs[:parts]])
     so, sm, to, tm = (totals[k : k + 1] for k in range(4))
     rows = s_loss.shape[1]
     sequences = lens_ref.shape[0]
     width = rows // sequences
 
-    def live(dims, dim):
-        place = lax.broadcasted_iota(jnp.int32, dims, dim)
-        mask = jnp.zeros(dims, jnp.bool_)
-        for s in range(sequences):
-            mask |= (place >= s * width) & (place < s * width + lens_ref[s])
-        return mask.astype(F32)
-
-    live_row = live((1, rows), 1)
-    s_loss[...] = live_row * (so + sm - s_picked + (s_spread - sm + so))
-    t_loss[...] = live_row * ((t_spread - to + tm) + tm - t_picked)
-    turned = jnp.transpose(totals)
-    live_column = live((rows, 1), 0)
+    place = lax.broadcasted_iota(jnp.int32, (1, rows), 1)
+    live = jnp.zeros((1, rows), jnp.bool_)
+    for s in range(sequences):
+        live |= (place >= s * width) & (place < s * width + lens_ref[s])
+    live = live.astype(F32)
+    s_loss[...] = live * (so + sm - s_picked + (s_spread - sm + so))
+    t_loss[...] = live * ((t_spread - to + tm) + tm - t_picked)
+    copies = fetch(sems, (s_loss, outs[0]), (t_loss, outs[1]))
     base = vocab_base(so_ref.shape[1])
+    row = lax.broadcasted_iota(jnp.int32, totals.shape, 0)
+    wanted = totals
+    for k, value in ((4, live), (5, s_targets[...] - base), (6, t_targets[...] - base)):
+        wanted = jnp.where(row == k, value.astype(F32), wanted)
+    turned = jnp.transpose(wanted)
+    live = turned[:, 4:5]
     lane = lax.broadcasted_iota(jnp.int32, so_ref.shape, 1)
-    s_hot = (lane == target_column(s_targets, base)).astype(F32)
-    t_hot = (lane == target_column(t_targets, base)).astype(F32)
-    so_chance = jnp.exp(so_ref[...] - turned[:, 0:1])
-    sm_chance = jnp.exp(sm_ref[...] - turned[:, 1:2])
-    to_chance = jnp.exp(to_ref[...] - turned[:, 2:3])
-    tm_chance = jnp.exp(tm_ref[...] - turned[:, 3:4])
-    s_grad[...] = (live_column * (2.0 * so_chance - s_hot - sm_chance)).astype(BF16)
-    t_grad[...] = (live_column * (2.0 * tm_chance - to_chance - t_hot)).astype(BF16)
+    hot = jnp.where(lane == turned[:, 5:6].astype(jnp.int32), 1.0, 0.0)
+    own, mapped = jnp.exp(so_ref[...] - turned[:, 0:1]), jnp.exp(sm_ref[...] - turned[:, 1:2])
+    s_grad[...] = (live * (2.0 * own - hot - mapped)).astype(BF16)
+    copies += fetch(sems.at[pl.ds(2, 1)], (s_grad, outs[2]))
+    hot = jnp.where(lane == turned[:, 6:7].astype(jnp.int32), 1.0, 0.0)
+    own, mapped = jnp.exp(to_ref[...] - turned[:, 2:3]), jnp.exp(tm_ref[...] - turned[:, 3:4])
+    t_grad[...] = (live * (2.0 * mapped - own - hot)).astype(BF16)
+    copies += fetch(sems.at[pl.ds(3, 1)], (t_grad, outs[3]))
+    for copy in copies:
+        copy.wait()
 
 
 def after(values, *needs):
@@ -320,7 +325,8 @@
         prepare,
         [shape((2 * student_queries.shape[1], rows), BF16)] + [shape((w_t.shape[1], tokens))] * 2,
         [HBM] * 4,
-        [pltpu.VMEM(a.shape, BF16) for a in (s_t, w_t)] + [dma((4,))],
+        [pltpu.VMEM(a.shape, BF16) for a in (s_t, w_t)]
+        + [pltpu.VMEM((w_t.shape[1], rows), F32), dma((4,))],
         limit=60,
     )(student_queries.T, teacher_keys.T, s_t, w_t)
     got = swap(give)
@@ -401,6 +407,8 @@
         functools.partial(finish, sv_count),
         (shape((1, rows)), shape((1, rows)), shape((rows, vocab), BF16), shape((rows, vocab), BF16)),
         [SMEM] + [VMEM] * (6 + sv_count),
+        [pltpu.VMEM((1, rows), F32)] * 2 + [pltpu.VMEM((rows, vocab), BF16)] * 2 + [dma((4,))],
+        outs=HBM,
     )(student_lengths, s_targets, t_targets, s_own, s_mapped, t_own, t_mapped, *stats)
     return s_loss.reshape(rows), t_loss.reshape(rows), s_grad, t_grad
 

time: 61.7 us -> 61.6 us (level)
  no operation moved by 1% of the time
where the time goes in v5:
time: 61.6 us; the launch traced here: 61.4 us
  starting transfers between devices  25.9 us (42%)
  blocking collectives  16.3 us (26%)
  Pallas kernels  11.6 us (19%)
  waiting for transfers between devices  5.71 us (9%)
  local copies, waits for them, and re-layouts  1.01 us (2%)
  between operations  0.81 us (1%)
    ppermute x16, starting transfers between devices, shift(): return lax.ppermute(a, axis, [(i, (i + n) % count) for i in range(count)])  24.5 us
    all_gather x7, blocking collectives, both(): return lax.all_gather(a, 'core', axis=0, tiled=True)  16.3 us
    ppermute x16, waiting for transfers between devices, shift(): return lax.ppermute(a, axis, [(i, (i + n) % count) for i in range(count)])  4.78 us
    pallas_call x1, Pallas kernels, body(): kernel_call(prepare, [shape((2 * student_queries.shape[1], rows), BF16)]...  2.54 us
    pallas_call x1, Pallas kernels, body(): kernel_call(functools.partial(finish, sv_count), (shape((1, rows)), shape...  2.12 us
    pallas_call x1, Pallas kernels, body(): kernel_call(functools.partial(attend, len(qk_blocks)), (shape((w_s.shape[...  1.48 us
    pallas_call x1, Pallas kernels, body(): kernel_call(student_side, (logits, shape((STATS, rows))), [VMEM] * 6)  1.42 us
    pallas_call x1, Pallas kernels, body(): kernel_call(mapped_teacher, (logits, shape((STATS, rows))), [VMEM] * (3 +...  1.36 us
  transfers between devices with their start and end apart: 22, of which 6 were waited for; matrix products, arithmetic and copies ran while one was open for 0% of the time, Pallas kernels for 9%

profile of v5, /device:TPU:0, one launch (start us, length us, event | category | flops | bytes accessed | tf_op | source)
XLA Modules:
  0.0 61.4 jit_solution(2703379753357257612)
XLA Ops:
  0.6 0.0 copy-start.2
  0.7 2.5 %shard_map.147 = (bf16[128,256]{1,0:T(8,128)(2,1)}, f32[576,128]{1,0:T(8,128)}, f32[576,128]{1,0:T(8,128)}) custom-call(bf16[64,256]{1,0:T(8,128)(2,1)} %bitcast.21, bf16[64,256]{1,0:T(8,128)(2,1)} %bitcast.22, bf16[448,256]{1,0:T(8,128)(2,1)} %bitcast.9, bf16[448,576]{1,0:T(8,128)(2,1)} %own_w.1), custom_call_target="tpu_custom_call" | custom-call | tf_op jit(solution)/shard_map/pallas_call | solution.py:324
  3.2 0.6 collective-permute-start
  3.8 2.5 %collective-permute-start.2 = (bf16[128,256]{1,0:T(8,128)(2,1)}, bf16[128,256]{1,0:T(8,128)(2,1)S(1)}, u32[]{:S(2)}, u32[]{:S(2)}) collective-permute-start(bf16[128,256]{1,0:T(8,128)(2,1)} %get-tuple-element.54.refs_0_), channel_id=1, source_target_pairs={{0,2},{2,0},{1,3},{3,1},{4,6},{6,4},{5,7},{7,5},{8,10},{10,8},{9,1... | collective-permute-start | bytes 196616 | tf_op jit(solution)/shard_map/ppermute | solution.py:311
  6.3 0.2 collective-permute-start.3
  6.5 0.0 collective-permute-start.4
  6.5 1.0 %copy-done.3 = f32[576,128]{1,0:T(8,128)S(1)} copy-done((f32[576,128]{1,0:T(8,128)S(1)}, f32[576,128]{1,0:T(8,128)}, u32[]{:S(2)}) %copy-start.3) | copy-done | bytes 294936
  7.5 2.0 %collective-permute-start.1 = (f32[288,128]{1,0:T(8,128)S(1)}, f32[288,128]{1,0:T(8,128)S(1)}, u32[]{:S(2)}, u32[]{:S(2)}) collective-permute-start(f32[288,128]{1,0:T(8,128)S(1)} %get-tuple-element.51), channel_id=1, source_target_pairs={{0,2},{2,0},{1,3},{3,1},{4,6},{6,4},{5,7},{7,5},{8,10},{10,8},{9,1... | collective-permute-start | bytes 442376 | tf_op jit(solution)/shard_map/ppermute | solution.py:311
  9.5 0.0 collective-permute-start.5
  9.5 2.7 %all_gather.22.matrix = bf16[896,576]{1,0:T(8,128)(2,1)S(1)} all-gather(bf16[448,576]{1,0:T(8,128)(2,1)S(1)} %bitcast.18), channel_id=1, replica_groups=mesh['grp'=2,'sv'=4,'x'=2,'core'=2] {'core'}, dimensions={0}, use_global_device_ids=true | all-gather | bytes 1548288 | tf_op jit(solution)/shard_map/all_gather | solution.py:304
  12.3 2.3 %all_gather.21.states.refs_0_ = bf16[1152,256]{1,0:T(8,128)(2,1)S(1)} all-gather(bf16[576,256]{1,0:T(8,128)(2,1)S(1)} %bitcast.19), channel_id=1, replica_groups=mesh['grp'=2,'sv'=4,'x'=2,'core'=2] {'core'}, dimensions={0}, use_global_device_ids=true | all-gather | bytes 884736 | tf_op jit(solution)/shard_map/all_gather | solution.py:304
  14.6 0.0 collective-permute-done.2.refs_1_
  14.6 0.1 collective-permute-start.10
  14.8 0.0 collective-permute-done.3.refs_2_
  14.8 1.5 %shard_map.149 = (f32[448,128]{1,0:T(8,128)S(1)}, bf16[2,128,128]{2,1,0:T(8,128)(2,1)S(1)}) custom-call(s32[2]{0:T(128)S(1)} %copy-done.7, bf16[1152,256]{1,0:T(8,128)(2,1)S(1)} %all_gather.21.states.refs_0_, bf16[896,576]{1,0:T(8,128)(2,1)S(1)} %all_gather.22.matrix, bf16[128,256]{1,0:T(8,128)(2,1)S(1)} %copy-done.4, ...), custom_call_target="tpu_custom_call" | custom-call | tf_op jit(solution)/shard_map/pallas_call | solution.py:345
  16.3 0.0 collective-permute-done.1
  16.3 2.0 %collective-permute-start.9 = (f32[448,128]{1,0:T(8,128)S(1)}, f32[448,128]{1,0:T(8,128)S(1)}, u32[]{:S(2)}, u32[]{:S(2)}) collective-permute-start(f32[448,128]{1,0:T(8,128)S(1)} %get-tuple-element.75), channel_id=1, source_target_pairs={{0,2},{2,0},{1,3},{3,1},{4,6},{6,4},{5,7},{7,5},{8,10},{10,8},{9,1... | collective-permute-start | bytes 688136 | tf_op jit(solution)/shard_map/ppermute | solution.py:311
  18.3 1.6 %collective-permute-start.6 = (bf16[288,128]{1,0:T(8,128)(2,1)S(1)}, bf16[288,128]{1,0:T(8,128)(2,1)S(1)}, u32[]{:S(2)}, u32[]{:S(2)}) collective-permute-start(bf16[288,128]{1,0:T(8,128)(2,1)S(1)} %add_convert_fusion.1.refs_0_), channel_id=1, source_target_pairs={{0,4},{4,8},{8,12},{12,0},{1,5},{5,9},{9,13},{13,1},{2,6},{6,10},{... | collective-permute-start | bytes 221192 | tf_op jit(solution)/shard_map/ppermute | solution.py:311
  19.9 2.6 %collective-permute-start.7 = (bf16[288,128]{1,0:T(8,128)(2,1)S(1)}, bf16[288,128]{1,0:T(8,128)(2,1)S(1)}, u32[]{:S(2)}, u32[]{:S(2)}) collective-permute-start(bf16[288,128]{1,0:T(8,128)(2,1)S(1)} %add_convert_fusion.1.refs_0_), channel_id=1, source_target_pairs={{0,8},{4,12},{8,0},{12,4},{1,9},{5,13},{9,1},{13,5},{2,10},{6,14},... | collective-permute-start | bytes 221192 | tf_op jit(solution)/shard_map/ppermute | solution.py:311
  22.5 1.4 %collective-permute-start.8 = (bf16[288,128]{1,0:T(8,128)(2,1)S(1)}, bf16[288,128]{1,0:T(8,128)(2,1)S(1)}, u32[]{:S(2)}, u32[]{:S(2)}) collective-permute-start(bf16[288,128]{1,0:T(8,128)(2,1)S(1)} %add_convert_fusion.1.refs_0_), channel_id=1, source_target_pairs={{0,12},{4,0},{8,4},{12,8},{1,13},{5,1},{9,5},{13,9},{2,14},{6,2},{... | collective-permute-start | bytes 221192 | tf_op jit(solution)/shard_map/ppermute | solution.py:311
  23.9 0.5 collective-permute-start.11
  24.4 2.1 %all_gather.23.refs_0_ = bf16[896,256]{1,0:T(8,128)(2,1)S(1)} all-gather(bf16[448,256]{1,0:T(8,128)(2,1)S(1)} %collective-permute-done.10), channel_id=1, replica_groups=mesh['grp'=2,'sv'=4,'x'=2,'core'=2] {'core'}, dimensions={0}, use_global_device_ids=true | all-gather | bytes 688128 | tf_op jit(solution)/shard_map/all_gather | solution.py:304
  26.5 1.2 %shard_map.150 = (f32[256,512]{1,0:T(8,128)S(1)}, f32[256,128]{1,0:T(8,128)S(1)}) custom-call(s32[1,256]{1,0:T(1,128)S(1)} %bitcast.13, bf16[448,256]{1,0:T(8,128)(2,1)S(1)} %bitcast.12, bf16[448,256]{1,0:T(8,128)(2,1)S(1)} %collective-permute-done.5.mate_s, bf16[896,256]{1,0:T(8,128)(2,1)S(1)} %all_gather.23.refs_0_, bf16[1792,512]{1,0:T(8,128)(2,1)S(1)} %copy-done.1), custom_call_target="tpu_custom_call" | custom-call | tf_op jit(solution)/shard_map/pallas_call | solution.py:362
  27.7 0.0 copy-start
  27.8 0.2 collective-permute-done.9
  28.1 1.6 %collective-permute-start.13 = (bf16[448,128]{1,0:T(8,128)(2,1)S(1)}, bf16[448,128]{1,0:T(8,128)(2,1)S(1)}, u32[]{:S(2)}, u32[]{:S(2)}) collective-permute-start(bf16[448,128]{1,0:T(8,128)(2,1)S(1)} %add_convert_fusion.refs_0_), channel_id=1, source_target_pairs={{0,4},{4,8},{8,12},{12,0},{1,5},{5,9},{9,13},{13,1},{2,6},{6,10},{... | collective-permute-start | bytes 344072 | tf_op jit(solution)/shard_map/ppermute | solution.py:311
  29.7 2.6 %collective-permute-start.14 = (bf16[448,128]{1,0:T(8,128)(2,1)S(1)}, bf16[448,128]{1,0:T(8,128)(2,1)S(1)}, u32[]{:S(2)}, u32[]{:S(2)}) collective-permute-start(bf16[448,128]{1,0:T(8,128)(2,1)S(1)} %add_convert_fusion.refs_0_), channel_id=1, source_target_pairs={{0,8},{4,12},{8,0},{12,4},{1,9},{5,13},{9,1},{13,5},{2,10},{6,14},... | collective-permute-start | bytes 344072 | tf_op jit(solution)/shard_map/ppermute | solution.py:311
  32.3 1.4 %collective-permute-start.15 = (bf16[448,128]{1,0:T(8,128)(2,1)S(1)}, bf16[448,128]{1,0:T(8,128)(2,1)S(1)}, u32[]{:S(2)}, u32[]{:S(2)}) collective-permute-start(bf16[448,128]{1,0:T(8,128)(2,1)S(1)} %add_convert_fusion.refs_0_), channel_id=1, source_target_pairs={{0,12},{4,0},{8,4},{12,8},{1,13},{5,1},{9,5},{13,9},{2,14},{6,2},{... | collective-permute-start | bytes 344072 | tf_op jit(solution)/shard_map/ppermute | solution.py:311
  33.6 0.5 collective-permute-start.12
  34.2 2.2 %all_gather.25.refs_0_ = bf16[2304,128]{1,0:T(8,128)(2,1)S(1)} all-gather(bf16[1152,128]{1,0:T(8,128)(2,1)S(1)} %shard_map.152), channel_id=1, replica_groups=mesh['grp'=2,'sv'=4,'x'=2,'core'=2] {'core'}, dimensions={0}, use_global_device_ids=true | all-gather | bytes 884736 | tf_op jit(solution)/shard_map/all_gather | solution.py:304
  36.4 2.2 %all_gather.24.refs_1_ = bf16[1152,256]{1,0:T(8,128)(2,1)S(1)} all-gather(bf16[576,256]{1,0:T(8,128)(2,1)S(1)} %collective-permute-done.11), channel_id=1, replica_groups=mesh['grp'=2,'sv'=4,'x'=2,'core'=2] {'core'}, dimensions={0}, use_global_device_ids=true | all-gather | bytes 884736 | tf_op jit(solution)/shard_map/all_gather | solution.py:304
  38.6 1.3 %shard_map.151.own_ref.to_ref = f32[256,512]{1,0:T(8,128)S(1)} custom-call(bf16[2,128,128]{2,1,0:T(8,128)(2,1)S(1)} %get-tuple-element.65.weights_ref, bf16[1152,256]{1,0:T(8,128)(2,1)S(1)} %all_gather.21.states.refs_0_, bf16[1152,256]{1,0:T(8,128)(2,1)S(1)} %all_gather.24.refs_1_, bf16[2304,512]{1,0:T(8,128)(2,1)S(1)} %copy-done), custom_call_target="tpu_custom_call" | custom-call | tf_op jit(solution)/shard_map/pallas_call | solution.py:381
  40.0 0.9 %collective-permute-done.12 = bf16[1152,128]{1,0:T(8,128)(2,1)S(1)} collective-permute-done((bf16[1152,128]{1,0:T(8,128)(2,1)S(1)}, bf16[1152,128]{1,0:T(8,128)(2,1)S(1)}, u32[]{:S(2)}, u32[]{:S(2)}) %collective-permute-start.12) | collective-permute-done | bytes 294944 | tf_op jit(solution)/shard_map/ppermute | solution.py:311
  40.8 2.2 %all_gather.26.refs_1_ = bf16[2304,128]{1,0:T(8,128)(2,1)S(1)} all-gather(bf16[1152,128]{1,0:T(8,128)(2,1)S(1)} %collective-permute-done.12), channel_id=1, replica_groups=mesh['grp'=2,'sv'=4,'x'=2,'core'=2] {'core'}, dimensions={0}, use_global_device_ids=true | all-gather | bytes 884736 | tf_op jit(solution)/shard_map/all_gather | solution.py:304
  43.1 1.4 %shard_map.153 = (f32[256,512]{1,0:T(8,128)S(1)}, f32[8,256]{1,0:T(8,128)S(1)}) custom-call(s32[1,256]{1,0:T(1,128)S(1)} %bitcast.16, f32[256,512]{1,0:T(8,128)S(1)} %shard_map.151.own_ref.to_ref, bf16[2304,128]{1,0:T(8,128)(2,1)S(1)} %all_gather.25.refs_0_, bf16[2304,128]{1,0:T(8,128)(2,1)S(1)} %all_gather.26.refs_1_, bf16[2304,512]{1,0:T(8,128)(2,1)S(1)} %copy-done), custom_call_target="tpu_custom_call" | custom-call | tf_op jit(solution)/shard_map/pallas_call | solution.py:387
  44.4 0.0 collective-permute-done.15.refs_3_
  44.5 2.5 %all_gather.27.halves = bf16[3584,128]{1,0:T(8,128)(2,1)S(1)} all-gather(bf16[1792,128]{1,0:T(8,128)(2,1)S(1)} %shard_map.154), channel_id=1, replica_groups=mesh['grp'=2,'sv'=4,'x'=2,'core'=2] {'core'}, dimensions={0}, use_global_device_ids=true | all-gather | bytes 1376256 | tf_op jit(solution)/shard_map/all_gather | solution.py:304
  47.0 1.4 %shard_map.155 = (f32[256,512]{1,0:T(8,128)S(1)}, f32[8,256]{1,0:T(8,128)S(1)}) custom-call(s32[1,256]{1,0:T(1,128)S(1)} %bitcast.14, f32[8,256]{1,0:T(8,128)S(1)} %get-tuple-element.73.t_stats, f32[256,512]{1,0:T(8,128)S(1)} %get-tuple-element.64.own_ref.so_ref, f32[256,128]{1,0:T(8,128)S(1)} %get-tuple-element.74.notes_ref, ...), custom_call_target="tpu_custom_call" | custom-call | tf_op jit(solution)/shard_map/pallas_call | solution.py:399
  48.4 1.5 %collective-permute-start.16 = (f32[8,256]{1,0:T(8,128)S(1)}, f32[8,256]{1,0:T(8,128)S(1)}, u32[]{:S(2)}, u32[]{:S(2)}) collective-permute-start(f32[8,256]{1,0:T(8,128)S(1)} %get-tuple-element.83.refs_0_), channel_id=1, source_target_pairs={{0,2},{2,0},{1,3},{3,1},{4,6},{6,4},{5,7},{7,5},{8,10},{10,8},{9,1... | collective-permute-start | bytes 24584 | tf_op jit(solution)/shard_map/ppermute | solution.py:311
  49.9 0.6 %collective-permute-start.18 = (f32[8,256]{1,0:T(8,128)S(1)}, f32[8,256]{1,0:T(8,128)S(1)}, u32[]{:S(2)}, u32[]{:S(2)}) collective-permute-start(f32[8,256]{1,0:T(8,128)S(1)} %get-tuple-element.83.refs_0_), channel_id=1, source_target_pairs={{0,3},{1,2},{2,1},{3,0},{4,7},{5,6},{6,5},{7,4},{8,11},{9,10},{10,... | collective-permute-start | bytes 24584 | tf_op jit(solution)/shard_map/ppermute | solution.py:318
  50.6 1.5 %collective-permute-done.16.refs_1_ = f32[8,256]{1,0:T(8,128)S(1)} collective-permute-done((f32[8,256]{1,0:T(8,128)S(1)}, f32[8,256]{1,0:T(8,128)S(1)}, u32[]{:S(2)}, u32[]{:S(2)}) %collective-permute-start.16) | collective-permute-done | bytes 8224 | tf_op jit(solution)/shard_map/ppermute | solution.py:311
  52.1 0.9 %collective-permute-done.18.refs_3_ = f32[8,256]{1,0:T(8,128)S(1)} collective-permute-done((f32[8,256]{1,0:T(8,128)S(1)}, f32[8,256]{1,0:T(8,128)S(1)}, u32[]{:S(2)}, u32[]{:S(2)}) %collective-permute-start.18) | collective-permute-done | bytes 8224 | tf_op jit(solution)/shard_map/ppermute | solution.py:318
  53.0 0.7 %collective-permute-start.19 = (f32[8,256]{1,0:T(8,128)S(1)}, f32[8,256]{1,0:T(8,128)S(1)}, u32[]{:S(2)}, u32[]{:S(2)}) collective-permute-start(f32[8,256]{1,0:T(8,128)S(1)} %shard_map.156.refs_0_), channel_id=1, source_target_pairs={{0,4},{4,8},{8,12},{12,0},{1,5},{5,9},{9,13},{13,1},{2,6},{6,10},{... | collective-permute-start | bytes 24584 | tf_op jit(solution)/shard_map/ppermute | solution.py:311
  53.8 1.9 %collective-permute-start.20 = (f32[8,256]{1,0:T(8,128)S(1)}, f32[8,256]{1,0:T(8,128)S(1)}, u32[]{:S(2)}, u32[]{:S(2)}) collective-permute-start(f32[8,256]{1,0:T(8,128)S(1)} %shard_map.156.refs_0_), channel_id=1, source_target_pairs={{0,8},{4,12},{8,0},{12,4},{1,9},{5,13},{9,1},{13,5},{2,10},{6,14},... | collective-permute-start | bytes 24584 | tf_op jit(solution)/shard_map/ppermute | solution.py:311
  55.6 1.5 %collective-permute-start.21 = (f32[8,256]{1,0:T(8,128)S(1)}, f32[8,256]{1,0:T(8,128)S(1)}, u32[]{:S(2)}, u32[]{:S(2)}) collective-permute-start(f32[8,256]{1,0:T(8,128)S(1)} %shard_map.156.refs_0_), channel_id=1, source_target_pairs={{0,12},{4,0},{8,4},{12,8},{1,13},{5,1},{9,5},{13,9},{2,14},{6,2},{... | collective-permute-start | bytes 24584 | tf_op jit(solution)/shard_map/ppermute | solution.py:311
  57.1 1.4 %collective-permute-done.19.refs_1_ = f32[8,256]{1,0:T(8,128)S(1)} collective-permute-done((f32[8,256]{1,0:T(8,128)S(1)}, f32[8,256]{1,0:T(8,128)S(1)}, u32[]{:S(2)}, u32[]{:S(2)}) %collective-permute-start.19) | collective-permute-done | bytes 8224 | tf_op jit(solution)/shard_map/ppermute | solution.py:311
  58.5 0.7 %collective-permute-done.21.refs_3_ = f32[8,256]{1,0:T(8,128)S(1)} collective-permute-done((f32[8,256]{1,0:T(8,128)S(1)}, f32[8,256]{1,0:T(8,128)S(1)}, u32[]{:S(2)}, u32[]{:S(2)}) %collective-permute-start.21) | collective-permute-done | bytes 8224 | tf_op jit(solution)/shard_map/ppermute | solution.py:311
  59.3 2.1 %shard_map.157 = (f32[1,256]{1,0:T(1,128)}, f32[1,256]{1,0:T(1,128)}, bf16[256,512]{1,0:T(8,128)(2,1)}, bf16[256,512]{1,0:T(8,128)(2,1)}) custom-call(s32[2]{0:T(128)S(1)} %copy-done.8, s32[1,256]{1,0:T(1,128)S(1)} %bitcast.15, s32[1,256]{1,0:T(1,128)S(1)} %bitcast.17, f32[256,512]{1,0:T(8,128)S(1)} %get-tuple-element.64.own_ref.so_ref, ...), custom_call_target="tpu_custom_call" | custom-call | tf_op jit(solution)/shard_map/pallas_call | solution.py:406
  (38 shorter events, 0.3 us)
Async XLA Ops:
  0.6 8.9 %copy-start.9 = (bf16[576,448]{0,1:T(8,128)(2,1)S(1)}, bf16[576,448]{0,1:T(8,128)(2,1)}, u32[]{:S(2)}) copy-start(bf16[576,448]{0,1:T(8,128)(2,1)} %param.21) | copy-start | bytes 1548292
  0.6 14.0 %copy-start.2 = (bf16[256,448]{0,1:T(8,128)(2,1)S(1)}, bf16[256,448]{0,1:T(8,128)(2,1)}, u32[]{:S(2)}) copy-start(bf16[256,448]{0,1:T(8,128)(2,1)} %param.12) | copy-start | bytes 688132
  0.7 14.1 %copy-start.7 = (s32[2]{0:T(128)S(1)}, s32[2]{0:T(128)}, u32[]{:S(2)}) copy-start(s32[2]{0:T(128)} %lens_ref.2) | copy-start | bytes 28
  3.2 3.3 %collective-permute-start = (f32[576,128]{1,0:T(8,128)}, f32[576,128]{1,0:T(8,128)S(1)}, u32[]{:S(2)}, u32[]{:S(2)}) collective-permute-start(f32[576,128]{1,0:T(8,128)} %get-tuple-element.47), channel_id=1, source_target_pairs={{0,1},{1,0},{2,3},{3,2},{4,5},{5,4},{6,7},{7,6},{8,9},{9,8},{10,11... | collective-permute-start | bytes 884744 | tf_op jit(solution)/shard_map/ppermute | solution.py:307
  3.8 10.8 %collective-permute-start.2 = (bf16[128,256]{1,0:T(8,128)(2,1)}, bf16[128,256]{1,0:T(8,128)(2,1)S(1)}, u32[]{:S(2)}, u32[]{:S(2)}) collective-permute-start(bf16[128,256]{1,0:T(8,128)(2,1)} %get-tuple-element.54.refs_0_), channel_id=1, source_target_pairs={{0,2},{2,0},{1,3},{3,1},{4,6},{6,4},{5,7},{7,5},{8,10},{10,8},{9,1... | collective-permute-start | bytes 196616 | tf_op jit(solution)/shard_map/ppermute | solution.py:311
  6.3 8.5 %collective-permute-start.3 = (bf16[128,256]{1,0:T(8,128)(2,1)}, bf16[128,256]{1,0:T(8,128)(2,1)S(1)}, u32[]{:S(2)}, u32[]{:S(2)}) collective-permute-start(bf16[128,256]{1,0:T(8,128)(2,1)} %get-tuple-element.54.refs_0_), channel_id=1, source_target_pairs={{0,1},{1,0},{2,3},{3,2},{4,5},{5,4},{6,7},{7,6},{8,9},{9,8},{10,11... | collective-permute-start | bytes 196616 | tf_op jit(solution)/shard_map/ppermute | solution.py:318
  6.5 8.3 %collective-permute-start.4 = (bf16[128,256]{1,0:T(8,128)(2,1)}, bf16[128,256]{1,0:T(8,128)(2,1)S(1)}, u32[]{:S(2)}, u32[]{:S(2)}) collective-permute-start(bf16[128,256]{1,0:T(8,128)(2,1)} %get-tuple-element.54.refs_0_), channel_id=1, source_target_pairs={{0,3},{1,2},{2,1},{3,0},{4,7},{5,6},{6,5},{7,4},{8,11},{9,10},{10,... | collective-permute-start | bytes 196616 | tf_op jit(solution)/shard_map/ppermute | solution.py:318
  6.5 1.0 %copy-start.3 = (f32[576,128]{1,0:T(8,128)S(1)}, f32[576,128]{1,0:T(8,128)}, u32[]{:S(2)}) copy-start(f32[576,128]{1,0:T(8,128)} %get-tuple-element.46.keep_ref) | copy-start | bytes 884740
  7.5 4.8 %copy-start.10 = (bf16[256,576]{0,1:T(8,128)(2,1)S(1)}, bf16[256,576]{0,1:T(8,128)(2,1)}, u32[]{:S(2)}) copy-start(bf16[256,576]{0,1:T(8,128)(2,1)} %param.13) | copy-start | bytes 884740
  7.5 7.3 %copy-start.4 = (bf16[128,256]{1,0:T(8,128)(2,1)S(1)}, bf16[128,256]{1,0:T(8,128)(2,1)}, u32[]{:S(2)}) copy-start(bf16[128,256]{1,0:T(8,128)(2,1)} %get-tuple-element.54.refs_0_) | copy-start | bytes 196612
  7.5 8.8 %collective-permute-start.1 = (f32[288,128]{1,0:T(8,128)S(1)}, f32[288,128]{1,0:T(8,128)S(1)}, u32[]{:S(2)}, u32[]{:S(2)}) collective-permute-start(f32[288,128]{1,0:T(8,128)S(1)} %get-tuple-element.51), channel_id=1, source_target_pairs={{0,2},{2,0},{1,3},{3,1},{4,6},{6,4},{5,7},{7,5},{8,10},{10,8},{9,1... | collective-permute-start | bytes 442376 | tf_op jit(solution)/shard_map/ppermute | solution.py:311
  9.5 6.8 %collective-permute-start.5 = (bf16[448,256]{1,0:T(8,128)(2,1)}, bf16[448,256]{1,0:T(8,128)(2,1)S(1)}, u32[]{:S(2)}, u32[]{:S(2)}) collective-permute-start(bf16[448,256]{1,0:T(8,128)(2,1)} %bitcast.10), channel_id=1, source_target_pairs={{0,1},{1,0},{2,3},{3,2},{4,5},{5,4},{6,7},{7,6},{8,9},{9,8},{10,11... | collective-permute-start | bytes 688136 | tf_op jit(solution)/shard_map/ppermute | solution.py:307
  12.3 14.3 %copy-start.1 = (bf16[1792,512]{1,0:T(8,128)(2,1)S(1)}, bf16[1792,512]{1,0:T(8,128)(2,1)}, u32[]{:S(2)}) copy-start(bf16[1792,512]{1,0:T(8,128)(2,1)} %head.1) | copy-start | bytes 5505028
  12.3 14.3 %copy-start.5 = (s32[256]{0:T(256)S(1)}, s32[256]{0:T(256)}, u32[]{:S(2)}) copy-start(s32[256]{0:T(256)} %param.16) | copy-start | bytes 3076
  14.6 9.2 %collective-permute-start.10 = (bf16[448,256]{1,0:T(8,128)(2,1)S(1)}, bf16[448,256]{1,0:T(8,128)(2,1)S(1)}, u32[]{:S(2)}, u32[]{:S(2)}) collective-permute-start(bf16[448,256]{1,0:T(8,128)(2,1)S(1)} %bitcast.11), channel_id=1, source_target_pairs={{0,2},{2,0},{1,3},{3,1},{4,6},{6,4},{5,7},{7,5},{8,10},{10,8},{9,1... | collective-permute-start | bytes 688136 | tf_op jit(solution)/shard_map/ppermute | solution.py:311
  16.3 11.7 %collective-permute-start.9 = (f32[448,128]{1,0:T(8,128)S(1)}, f32[448,128]{1,0:T(8,128)S(1)}, u32[]{:S(2)}, u32[]{:S(2)}) collective-permute-start(f32[448,128]{1,0:T(8,128)S(1)} %get-tuple-element.75), channel_id=1, source_target_pairs={{0,2},{2,0},{1,3},{3,1},{4,6},{6,4},{5,7},{7,5},{8,10},{10,8},{9,1... | collective-permute-start | bytes 688136 | tf_op jit(solution)/shard_map/ppermute | solution.py:311
  18.3 9.4 %collective-permute-start.6 = (bf16[288,128]{1,0:T(8,128)(2,1)S(1)}, bf16[288,128]{1,0:T(8,128)(2,1)S(1)}, u32[]{:S(2)}, u32[]{:S(2)}) collective-permute-start(bf16[288,128]{1,0:T(8,128)(2,1)S(1)} %add_convert_fusion.1.refs_0_), channel_id=1, source_target_pairs={{0,4},{4,8},{8,12},{12,0},{1,5},{5,9},{9,13},{13,1},{2,6},{6,10},{... | collective-permute-start | bytes 221192 | tf_op jit(solution)/shard_map/ppermute | solution.py:311
  19.9 7.8 %collective-permute-start.7 = (bf16[288,128]{1,0:T(8,128)(2,1)S(1)}, bf16[288,128]{1,0:T(8,128)(2,1)S(1)}, u32[]{:S(2)}, u32[]{:S(2)}) collective-permute-start(bf16[288,128]{1,0:T(8,128)(2,1)S(1)} %add_convert_fusion.1.refs_0_), channel_id=1, source_target_pairs={{0,8},{4,12},{8,0},{12,4},{1,9},{5,13},{9,1},{13,5},{2,10},{6,14},... | collective-permute-start | bytes 221192 | tf_op jit(solution)/shard_map/ppermute | solution.py:311
  22.5 5.2 %collective-permute-start.8 = (bf16[288,128]{1,0:T(8,128)(2,1)S(1)}, bf16[288,128]{1,0:T(8,128)(2,1)S(1)}, u32[]{:S(2)}, u32[]{:S(2)}) collective-permute-start(bf16[288,128]{1,0:T(8,128)(2,1)S(1)} %add_convert_fusion.1.refs_0_), channel_id=1, source_target_pairs={{0,12},{4,0},{8,4},{12,8},{1,13},{5,1},{9,5},{13,9},{2,14},{6,2},{... | collective-permute-start | bytes 221192 | tf_op jit(solution)/shard_map/ppermute | solution.py:311
  23.9 12.5 %collective-permute-start.11 = (bf16[576,256]{1,0:T(8,128)(2,1)S(1)}, bf16[576,256]{1,0:T(8,128)(2,1)S(1)}, u32[]{:S(2)}, u32[]{:S(2)}) collective-permute-start(bf16[576,256]{1,0:T(8,128)(2,1)S(1)} %bitcast.20), channel_id=1, source_target_pairs={{0,2},{2,0},{1,3},{3,1},{4,6},{6,4},{5,7},{7,5},{8,10},{10,8},{9,1... | collective-permute-start | bytes 884744 | tf_op jit(solution)/shard_map/ppermute | solution.py:311
  27.7 10.9 %copy-start = (bf16[2304,512]{1,0:T(8,128)(2,1)S(1)}, bf16[2304,512]{1,0:T(8,128)(2,1)}, u32[]{:S(2)}) copy-start(bf16[2304,512]{1,0:T(8,128)(2,1)} %refs_2_.3) | copy-start | bytes 7077892
  28.1 16.4 %collective-permute-start.13 = (bf16[448,128]{1,0:T(8,128)(2,1)S(1)}, bf16[448,128]{1,0:T(8,128)(2,1)S(1)}, u32[]{:S(2)}, u32[]{:S(2)}) collective-permute-start(bf16[448,128]{1,0:T(8,128)(2,1)S(1)} %add_convert_fusion.refs_0_), channel_id=1, source_target_pairs={{0,4},{4,8},{8,12},{12,0},{1,5},{5,9},{9,13},{13,1},{2,6},{6,10},{... | collective-permute-start | bytes 344072 | tf_op jit(solution)/shard_map/ppermute | solution.py:311
  29.7 14.7 %collective-permute-start.14 = (bf16[448,128]{1,0:T(8,128)(2,1)S(1)}, bf16[448,128]{1,0:T(8,128)(2,1)S(1)}, u32[]{:S(2)}, u32[]{:S(2)}) collective-permute-start(bf16[448,128]{1,0:T(8,128)(2,1)S(1)} %add_convert_fusion.refs_0_), channel_id=1, source_target_pairs={{0,8},{4,12},{8,0},{12,4},{1,9},{5,13},{9,1},{13,5},{2,10},{6,14},... | collective-permute-start | bytes 344072 | tf_op jit(solution)/shard_map/ppermute | solution.py:311
  32.3 12.2 %collective-permute-start.15 = (bf16[448,128]{1,0:T(8,128)(2,1)S(1)}, bf16[448,128]{1,0:T(8,128)(2,1)S(1)}, u32[]{:S(2)}, u32[]{:S(2)}) collective-permute-start(bf16[448,128]{1,0:T(8,128)(2,1)S(1)} %add_convert_fusion.refs_0_), channel_id=1, source_target_pairs={{0,12},{4,0},{8,4},{12,8},{1,13},{5,1},{9,5},{13,9},{2,14},{6,2},{... | collective-permute-start | bytes 344072 | tf_op jit(solution)/shard_map/ppermute | solution.py:311
  33.6 7.2 %collective-permute-start.12 = (bf16[1152,128]{1,0:T(8,128)(2,1)S(1)}, bf16[1152,128]{1,0:T(8,128)(2,1)S(1)}, u32[]{:S(2)}, u32[]{:S(2)}) collective-permute-start(bf16[1152,128]{1,0:T(8,128)(2,1)S(1)} %shard_map.152), channel_id=1, source_target_pairs={{0,2},{2,0},{1,3},{3,1},{4,6},{6,4},{5,7},{7,5},{8,10},{10,8},{9,1... | collective-permute-start | bytes 884744 | tf_op jit(solution)/shard_map/ppermute | solution.py:311
  38.6 4.5 %copy-start.6 = (s32[256]{0:T(256)S(1)}, s32[256]{0:T(256)}, u32[]{:S(2)}) copy-start(s32[256]{0:T(256)} %param.17) | copy-start | bytes 3076
  47.0 12.3 %copy-start.8 = (s32[2]{0:T(128)S(1)}, s32[2]{0:T(128)}, u32[]{:S(2)}) copy-start(s32[2]{0:T(128)} %lens_ref.3) | copy-start | bytes 28
  48.4 3.7 %collective-permute-start.16 = (f32[8,256]{1,0:T(8,128)S(1)}, f32[8,256]{1,0:T(8,128)S(1)}, u32[]{:S(2)}, u32[]{:S(2)}) collective-permute-start(f32[8,256]{1,0:T(8,128)S(1)} %get-tuple-element.83.refs_0_), channel_id=1, source_target_pairs={{0,2},{2,0},{1,3},{3,1},{4,6},{6,4},{5,7},{7,5},{8,10},{10,8},{9,1... | collective-permute-start | bytes 24584 | tf_op jit(solution)/shard_map/ppermute | solution.py:311
  49.9 2.2 %collective-permute-start.17 = (f32[8,256]{1,0:T(8,128)S(1)}, f32[8,256]{1,0:T(8,128)S(1)}, u32[]{:S(2)}, u32[]{:S(2)}) collective-permute-start(f32[8,256]{1,0:T(8,128)S(1)} %get-tuple-element.83.refs_0_), channel_id=1, source_target_pairs={{0,1},{1,0},{2,3},{3,2},{4,5},{5,4},{6,7},{7,6},{8,9},{9,8},{10,11... | collective-permute-start | bytes 24584 | tf_op jit(solution)/shard_map/ppermute | solution.py:318
  49.9 3.1 %collective-permute-start.18 = (f32[8,256]{1,0:T(8,128)S(1)}, f32[8,256]{1,0:T(8,128)S(1)}, u32[]{:S(2)}, u32[]{:S(2)}) collective-permute-start(f32[8,256]{1,0:T(8,128)S(1)} %get-tuple-element.83.refs_0_), channel_id=1, source_target_pairs={{0,3},{1,2},{2,1},{3,0},{4,7},{5,6},{6,5},{7,4},{8,11},{9,10},{10,... | collective-permute-start | bytes 24584 | tf_op jit(solution)/shard_map/ppermute | solution.py:318
  53.0 5.5 %collective-permute-start.19 = (f32[8,256]{1,0:T(8,128)S(1)}, f32[8,256]{1,0:T(8,128)S(1)}, u32[]{:S(2)}, u32[]{:S(2)}) collective-permute-start(f32[8,256]{1,0:T(8,128)S(1)} %shard_map.156.refs_0_), channel_id=1, source_target_pairs={{0,4},{4,8},{8,12},{12,0},{1,5},{5,9},{9,13},{13,1},{2,6},{6,10},{... | collective-permute-start | bytes 24584 | tf_op jit(solution)/shard_map/ppermute | solution.py:311
  53.8 4.8 %collective-permute-start.20 = (f32[8,256]{1,0:T(8,128)S(1)}, f32[8,256]{1,0:T(8,128)S(1)}, u32[]{:S(2)}, u32[]{:S(2)}) collective-permute-start(f32[8,256]{1,0:T(8,128)S(1)} %shard_map.156.refs_0_), channel_id=1, source_target_pairs={{0,8},{4,12},{8,0},{12,4},{1,9},{5,13},{9,1},{13,5},{2,10},{6,14},... | collective-permute-start | bytes 24584 | tf_op jit(solution)/shard_map/ppermute | solution.py:311
  55.6 3.7 %collective-permute-start.21 = (f32[8,256]{1,0:T(8,128)S(1)}, f32[8,256]{1,0:T(8,128)S(1)}, u32[]{:S(2)}, u32[]{:S(2)}) collective-permute-start(f32[8,256]{1,0:T(8,128)S(1)} %shard_map.156.refs_0_), channel_id=1, source_target_pairs={{0,12},{4,0},{8,4},{12,8},{1,13},{5,1},{9,5},{13,9},{2,14},{6,2},{... | collective-permute-start | bytes 24584 | tf_op jit(solution)/shard_map/ppermute | solution.py:311

commit v6 on v5

--- a/solution.py
+++ b/solution.py
@@ -90,11 +90,16 @@
         share[...] = keep_ref[place, :] + got_ref[place, :]
 
 
-def collect(axis, *refs):
+def pairs_up(count):
+    return count & (count - 1) == 0
+
+
+def collect(axis, paired, *refs):
     *blocks, out_ref = refs
     rows = blocks[0].shape[0]
     for n, block in enumerate(blocks):
-        out_ref[part_of(behind(axis, n), rows), :] = block[...]
+        index = lax.axis_index(axis) ^ n if paired else behind(axis, n)
+        out_ref[part_of(index, rows), :] = block[...]
 
 
 def attend(blocks, lens_ref, states, matrix, *refs):
@@ -313,6 +318,10 @@
     def around(a, axis):
         return [shift(a, axis, n) for n in range(1, lax.axis_size(axis))]
 
+    def exchange(a, axis):
+        count = lax.axis_size(axis)
+        return [lax.ppermute(a, axis, [(i, i ^ n) for i in range(count)]) for n in range(1, count)]
+
     def cross(a, n):
         pairs = [(2 * i + c, (2 * (i + n) + 1 - c) % (CORES * chips)) for i in range(chips) for c in range(CORES)]
         return lax.ppermute(a, ("x", "core"), pairs)
@@ -353,7 +362,7 @@
         (parts_t[0], *other_t, part_s, mate_s)
     )
     into_t = functools.reduce(jnp.add, other_t, own_part).astype(BF16)
-    into_t = [into_t] + around(into_t, "sv")
+    into_t = [into_t] + (exchange(into_t, "sv") if pairs_up(sv_count) else around(into_t, "sv"))
     other_s = around(part_s, "x")
     far_t = around(after((t_t,), *other_t)[0], "x")
     s_blocks = [both(a) for a in after(far_s, *other_t)]
@@ -368,13 +377,13 @@
 
     *into_t, part_s, other_s, s_own = lax.optimization_barrier((*into_t, part_s, other_s, s_own))
     into_t = kernel_call(
-        functools.partial(collect, "sv"),
+        functools.partial(collect, "sv", pairs_up(sv_count)),
         shape((sv_count * into_t[0].shape[0], tokens), BF16),
         [VMEM] * sv_count,
     )(*into_t)
     into_t, part_s = lax.optimization_barrier((into_t, part_s))
     into_s = functools.reduce(jnp.add, other_s, part_s).astype(BF16)
-    into_s = [into_s] + around(into_s, "sv")
+    into_s = [into_s] + (exchange(into_s, "sv") if pairs_up(sv_count) else around(into_s, "sv"))
     t_shares = [into_t] + (around(into_t, "x") if split > 1 else [])
     t_shares = [both(a) for a in t_shares]
     t_blocks = [chip_t] + [both(a) for a in far_t]
@@ -392,7 +401,7 @@
     )(t_targets, t_own, *t_shares, teacher_head)
 
     into_s = kernel_call(
-        functools.partial(collect, "sv"),
+        functools.partial(collect, "sv", pairs_up(sv_count)),
         shape((sv_count * into_s[0].shape[0], tokens), BF16),
         [VMEM] * sv_count,
     )(*after(into_s, t_stats))

time: 61.6 us -> 62.1 us (level)
  waiting for transfers between devices: 5.71 us -> 8.01 us
  starting transfers between devices: 25.9 us -> 24.1 us
    ppermute x16 -> x10, starting transfers between devices: 24.5 us -> 13.5 us  [shift(): return lax.ppermute(a, axis, [(i, (i + n) % count) for i in range(count)])]
    ppermute x0 -> x6, starting transfers between devices: none -> 8.9 us  [exchange(): lax.ppermute(a, axis, [(i, i ^ n) for i in range(count)])]
    ppermute x0 -> x6, waiting for transfers between devices: none -> 2.29 us  [exchange(): lax.ppermute(a, axis, [(i, i ^ n) for i in range(count)])]
    ppermute x16 -> x10, waiting for transfers between devices: 4.78 us -> 5.09 us  [shift(): return lax.ppermute(a, axis, [(i, (i + n) % count) for i in range(count)])]
  transfers between devices with their start and end apart: 22 -> 22, of which waited for: 6 -> 9; matrix products, arithmetic and copies ran while one was open for 0% -> 0% of each run, Pallas kernels for 9% -> 9%
where the time goes in v6:
time: 62.1 us; the launch traced here: 61.9 us
  starting transfers between devices  24.1 us (39%)
  blocking collectives  16.3 us (26%)
  Pallas kernels  11.6 us (19%)
  waiting for transfers between devices  8.01 us (13%)
  local copies, waits for them, and re-layouts  1.01 us (2%)
  between operations  0.8 us (1%)
    all_gather x7, blocking collectives, both(): return lax.all_gather(a, 'core', axis=0, tiled=True)  16.3 us
    ppermute x10, starting transfers between devices, shift(): return lax.ppermute(a, axis, [(i, (i + n) % count) for i in range(count)])  13.5 us
    ppermute x6, starting transfers between devices, exchange(): lax.ppermute(a, axis, [(i, i ^ n) for i in range(count)])  8.9 us
    ppermute x10, waiting for transfers between devices, shift(): return lax.ppermute(a, axis, [(i, (i + n) % count) for i in range(count)])  5.09 us
    pallas_call x1, Pallas kernels, body(): kernel_call(prepare, [shape((2 * student_queries.shape[1], rows), BF16)]...  2.54 us
    ppermute x6, waiting for transfers between devices, exchange(): lax.ppermute(a, axis, [(i, i ^ n) for i in range(count)])  2.29 us
    pallas_call x1, Pallas kernels, body(): kernel_call(functools.partial(finish, sv_count), (shape((1, rows)), shape...  2.12 us
    pallas_call x1, Pallas kernels, body(): kernel_call(functools.partial(attend, len(qk_blocks)), (shape((w_s.shape[...  1.48 us
  transfers between devices with their start and end apart: 22, of which 9 were waited for; matrix products, arithmetic and copies ran while one was open for 0% of the time, Pallas kernels for 9%

profile of v6, /device:TPU:0, one launch (start us, length us, event | category | flops | bytes accessed | tf_op | source)
XLA Modules:
  0.0 61.9 jit_solution(17060516863500364750)
XLA Ops:
  0.6 0.0 copy-start.2
  0.7 2.5 %shard_map.147 = (bf16[128,256]{1,0:T(8,128)(2,1)}, f32[576,128]{1,0:T(8,128)}, f32[576,128]{1,0:T(8,128)}) custom-call(bf16[64,256]{1,0:T(8,128)(2,1)} %bitcast.21, bf16[64,256]{1,0:T(8,128)(2,1)} %bitcast.22, bf16[448,256]{1,0:T(8,128)(2,1)} %bitcast.9, bf16[448,576]{1,0:T(8,128)(2,1)} %own_w.1), custom_call_target="tpu_custom_call" | custom-call | tf_op jit(solution)/shard_map/pallas_call | solution.py:333
  3.2 0.6 collective-permute-start
  3.8 2.5 %collective-permute-start.2 = (bf16[128,256]{1,0:T(8,128)(2,1)}, bf16[128,256]{1,0:T(8,128)(2,1)S(1)}, u32[]{:S(2)}, u32[]{:S(2)}) collective-permute-start(bf16[128,256]{1,0:T(8,128)(2,1)} %get-tuple-element.54.refs_0_), channel_id=1, source_target_pairs={{0,2},{2,0},{1,3},{3,1},{4,6},{6,4},{5,7},{7,5},{8,10},{10,8},{9,1... | collective-permute-start | bytes 196616 | tf_op jit(solution)/shard_map/ppermute | solution.py:316
  6.3 0.2 collective-permute-start.3
  6.5 0.0 collective-permute-start.4
  6.5 1.0 %copy-done.3 = f32[576,128]{1,0:T(8,128)S(1)} copy-done((f32[576,128]{1,0:T(8,128)S(1)}, f32[576,128]{1,0:T(8,128)}, u32[]{:S(2)}) %copy-start.3) | copy-done | bytes 294936
  7.5 2.0 %collective-permute-start.1 = (f32[288,128]{1,0:T(8,128)S(1)}, f32[288,128]{1,0:T(8,128)S(1)}, u32[]{:S(2)}, u32[]{:S(2)}) collective-permute-start(f32[288,128]{1,0:T(8,128)S(1)} %get-tuple-element.51), channel_id=1, source_target_pairs={{0,2},{2,0},{1,3},{3,1},{4,6},{6,4},{5,7},{7,5},{8,10},{10,8},{9,1... | collective-permute-start | bytes 442376 | tf_op jit(solution)/shard_map/ppermute | solution.py:316
  9.5 0.0 collective-permute-start.5
  9.5 2.7 %all_gather.22.matrix = bf16[896,576]{1,0:T(8,128)(2,1)S(1)} all-gather(bf16[448,576]{1,0:T(8,128)(2,1)S(1)} %bitcast.18), channel_id=1, replica_groups=mesh['grp'=2,'sv'=4,'x'=2,'core'=2] {'core'}, dimensions={0}, use_global_device_ids=true | all-gather | bytes 1548288 | tf_op jit(solution)/shard_map/all_gather | solution.py:309
  12.3 2.3 %all_gather.21.states.refs_0_ = bf16[1152,256]{1,0:T(8,128)(2,1)S(1)} all-gather(bf16[576,256]{1,0:T(8,128)(2,1)S(1)} %bitcast.19), channel_id=1, replica_groups=mesh['grp'=2,'sv'=4,'x'=2,'core'=2] {'core'}, dimensions={0}, use_global_device_ids=true | all-gather | bytes 884736 | tf_op jit(solution)/shard_map/all_gather | solution.py:309
  14.6 0.1 collective-permute-start.10
  14.8 1.5 %shard_map.149 = (f32[448,128]{1,0:T(8,128)S(1)}, bf16[2,128,128]{2,1,0:T(8,128)(2,1)S(1)}) custom-call(s32[2]{0:T(128)S(1)} %copy-done.7, bf16[1152,256]{1,0:T(8,128)(2,1)S(1)} %all_gather.21.states.refs_0_, bf16[896,576]{1,0:T(8,128)(2,1)S(1)} %all_gather.22.matrix, bf16[128,256]{1,0:T(8,128)(2,1)S(1)} %copy-done.4, ...), custom_call_target="tpu_custom_call" | custom-call | tf_op jit(solution)/shard_map/pallas_call | solution.py:354
  16.3 2.0 %collective-permute-start.9 = (f32[448,128]{1,0:T(8,128)S(1)}, f32[448,128]{1,0:T(8,128)S(1)}, u32[]{:S(2)}, u32[]{:S(2)}) collective-permute-start(f32[448,128]{1,0:T(8,128)S(1)} %get-tuple-element.75), channel_id=1, source_target_pairs={{0,2},{2,0},{1,3},{3,1},{4,6},{6,4},{5,7},{7,5},{8,10},{10,8},{9,1... | collective-permute-start | bytes 688136 | tf_op jit(solution)/shard_map/ppermute | solution.py:316
  18.3 1.6 %collective-permute-start.6 = (bf16[288,128]{1,0:T(8,128)(2,1)S(1)}, bf16[288,128]{1,0:T(8,128)(2,1)S(1)}, u32[]{:S(2)}, u32[]{:S(2)}) collective-permute-start(bf16[288,128]{1,0:T(8,128)(2,1)S(1)} %add_convert_fusion.1.refs_0_), channel_id=1, source_target_pairs={{0,4},{4,0},{8,12},{12,8},{1,5},{5,1},{9,13},{13,9},{2,6},{6,2},{1... | collective-permute-start | bytes 221192 | tf_op jit(solution)/shard_map/ppermute | solution.py:323
  19.9 2.6 %collective-permute-start.7 = (bf16[288,128]{1,0:T(8,128)(2,1)S(1)}, bf16[288,128]{1,0:T(8,128)(2,1)S(1)}, u32[]{:S(2)}, u32[]{:S(2)}) collective-permute-start(bf16[288,128]{1,0:T(8,128)(2,1)S(1)} %add_convert_fusion.1.refs_0_), channel_id=1, source_target_pairs={{0,8},{4,12},{8,0},{12,4},{1,9},{5,13},{9,1},{13,5},{2,10},{6,14},... | collective-permute-start | bytes 221192 | tf_op jit(solution)/shard_map/ppermute | solution.py:323
  22.5 0.2 collective-permute-start.8
  22.7 0.3 collective-permute-done.10
  23.1 0.1 collective-permute-start.11
  23.2 2.1 %all_gather.23.refs_0_ = bf16[896,256]{1,0:T(8,128)(2,1)S(1)} all-gather(bf16[448,256]{1,0:T(8,128)(2,1)S(1)} %collective-permute-done.10), channel_id=1, replica_groups=mesh['grp'=2,'sv'=4,'x'=2,'core'=2] {'core'}, dimensions={0}, use_global_device_ids=true | all-gather | bytes 688128 | tf_op jit(solution)/shard_map/all_gather | solution.py:309
  25.3 1.2 %shard_map.150 = (f32[256,512]{1,0:T(8,128)S(1)}, f32[256,128]{1,0:T(8,128)S(1)}) custom-call(s32[1,256]{1,0:T(1,128)S(1)} %bitcast.13, bf16[448,256]{1,0:T(8,128)(2,1)S(1)} %bitcast.12, bf16[448,256]{1,0:T(8,128)(2,1)S(1)} %collective-permute-done.5.mate_s, bf16[896,256]{1,0:T(8,128)(2,1)S(1)} %all_gather.23.refs_0_, bf16[1792,512]{1,0:T(8,128)(2,1)S(1)} %copy-done.1), custom_call_target="tpu_custom_call" | custom-call | tf_op jit(solution)/shard_map/pallas_call | solution.py:371
  26.5 0.0 copy-start
  26.5 1.2 %collective-permute-done.7.refs_2_ = bf16[288,128]{1,0:T(8,128)(2,1)S(1)} collective-permute-done((bf16[288,128]{1,0:T(8,128)(2,1)S(1)}, bf16[288,128]{1,0:T(8,128)(2,1)S(1)}, u32[]{:S(2)}, u32[]{:S(2)}) %collective-permute-start.7) | collective-permute-done | bytes 73760 | tf_op jit(solution)/shard_map/ppermute | solution.py:323
  27.7 1.1 %collective-permute-done.8.refs_3_ = bf16[288,128]{1,0:T(8,128)(2,1)S(1)} collective-permute-done((bf16[288,128]{1,0:T(8,128)(2,1)S(1)}, bf16[288,128]{1,0:T(8,128)(2,1)S(1)}, u32[]{:S(2)}, u32[]{:S(2)}) %collective-permute-start.8) | collective-permute-done | bytes 73760 | tf_op jit(solution)/shard_map/ppermute | solution.py:323
  28.9 1.1 %collective-permute-start.13 = (bf16[448,128]{1,0:T(8,128)(2,1)S(1)}, bf16[448,128]{1,0:T(8,128)(2,1)S(1)}, u32[]{:S(2)}, u32[]{:S(2)}) collective-permute-start(bf16[448,128]{1,0:T(8,128)(2,1)S(1)} %add_convert_fusion.refs_0_), channel_id=1, source_target_pairs={{0,4},{4,0},{8,12},{12,8},{1,5},{5,1},{9,13},{13,9},{2,6},{6,2},{1... | collective-permute-start | bytes 344072 | tf_op jit(solution)/shard_map/ppermute | solution.py:323
  30.0 2.3 %collective-permute-start.14 = (bf16[448,128]{1,0:T(8,128)(2,1)S(1)}, bf16[448,128]{1,0:T(8,128)(2,1)S(1)}, u32[]{:S(2)}, u32[]{:S(2)}) collective-permute-start(bf16[448,128]{1,0:T(8,128)(2,1)S(1)} %add_convert_fusion.refs_0_), channel_id=1, source_target_pairs={{0,8},{4,12},{8,0},{12,4},{1,9},{5,13},{9,1},{13,5},{2,10},{6,14},... | collective-permute-start | bytes 344072 | tf_op jit(solution)/shard_map/ppermute | solution.py:323
  32.3 1.0 %collective-permute-start.15 = (bf16[448,128]{1,0:T(8,128)(2,1)S(1)}, bf16[448,128]{1,0:T(8,128)(2,1)S(1)}, u32[]{:S(2)}, u32[]{:S(2)}) collective-permute-start(bf16[448,128]{1,0:T(8,128)(2,1)S(1)} %add_convert_fusion.refs_0_), channel_id=1, source_target_pairs={{0,12},{4,8},{8,4},{12,0},{1,13},{5,9},{9,5},{13,1},{2,14},{6,10},... | collective-permute-start | bytes 344072 | tf_op jit(solution)/shard_map/ppermute | solution.py:323
  33.3 0.5 collective-permute-start.12
  33.9 2.2 %all_gather.25.refs_0_ = bf16[2304,128]{1,0:T(8,128)(2,1)S(1)} all-gather(bf16[1152,128]{1,0:T(8,128)(2,1)S(1)} %shard_map.152), channel_id=1, replica_groups=mesh['grp'=2,'sv'=4,'x'=2,'core'=2] {'core'}, dimensions={0}, use_global_device_ids=true | all-gather | bytes 884736 | tf_op jit(solution)/shard_map/all_gather | solution.py:309
  36.1 2.2 %all_gather.24.refs_1_ = bf16[1152,256]{1,0:T(8,128)(2,1)S(1)} all-gather(bf16[576,256]{1,0:T(8,128)(2,1)S(1)} %collective-permute-done.11), channel_id=1, replica_groups=mesh['grp'=2,'sv'=4,'x'=2,'core'=2] {'core'}, dimensions={0}, use_global_device_ids=true | all-gather | bytes 884736 | tf_op jit(solution)/shard_map/all_gather | solution.py:309
  38.3 1.3 %shard_map.151.own_ref.to_ref = f32[256,512]{1,0:T(8,128)S(1)} custom-call(bf16[2,128,128]{2,1,0:T(8,128)(2,1)S(1)} %get-tuple-element.65.weights_ref, bf16[1152,256]{1,0:T(8,128)(2,1)S(1)} %all_gather.21.states.refs_0_, bf16[1152,256]{1,0:T(8,128)(2,1)S(1)} %all_gather.24.refs_1_, bf16[2304,512]{1,0:T(8,128)(2,1)S(1)} %copy-done), custom_call_target="tpu_custom_call" | custom-call | tf_op jit(solution)/shard_map/pallas_call | solution.py:390
  39.6 0.4 collective-permute-done.12
  40.1 2.2 %all_gather.26.refs_1_ = bf16[2304,128]{1,0:T(8,128)(2,1)S(1)} all-gather(bf16[1152,128]{1,0:T(8,128)(2,1)S(1)} %collective-permute-done.12), channel_id=1, replica_groups=mesh['grp'=2,'sv'=4,'x'=2,'core'=2] {'core'}, dimensions={0}, use_global_device_ids=true | all-gather | bytes 884736 | tf_op jit(solution)/shard_map/all_gather | solution.py:309
  42.3 1.4 %shard_map.153 = (f32[256,512]{1,0:T(8,128)S(1)}, f32[8,256]{1,0:T(8,128)S(1)}) custom-call(s32[1,256]{1,0:T(1,128)S(1)} %bitcast.16, f32[256,512]{1,0:T(8,128)S(1)} %shard_map.151.own_ref.to_ref, bf16[2304,128]{1,0:T(8,128)(2,1)S(1)} %all_gather.25.refs_0_, bf16[2304,128]{1,0:T(8,128)(2,1)S(1)} %all_gather.26.refs_1_, bf16[2304,512]{1,0:T(8,128)(2,1)S(1)} %copy-done), custom_call_target="tpu_custom_call" | custom-call | tf_op jit(solution)/shard_map/pallas_call | solution.py:396
  43.7 0.0 collective-permute-done.15.refs_3_
  43.7 2.5 %all_gather.27.halves = bf16[3584,128]{1,0:T(8,128)(2,1)S(1)} all-gather(bf16[1792,128]{1,0:T(8,128)(2,1)S(1)} %shard_map.154), channel_id=1, replica_groups=mesh['grp'=2,'sv'=4,'x'=2,'core'=2] {'core'}, dimensions={0}, use_global_device_ids=true | all-gather | bytes 1376256 | tf_op jit(solution)/shard_map/all_gather | solution.py:309
  46.2 1.4 %shard_map.155 = (f32[256,512]{1,0:T(8,128)S(1)}, f32[8,256]{1,0:T(8,128)S(1)}) custom-call(s32[1,256]{1,0:T(1,128)S(1)} %bitcast.14, f32[8,256]{1,0:T(8,128)S(1)} %get-tuple-element.73.t_stats, f32[256,512]{1,0:T(8,128)S(1)} %get-tuple-element.64.own_ref.so_ref, f32[256,128]{1,0:T(8,128)S(1)} %get-tuple-element.74.notes_ref, ...), custom_call_target="tpu_custom_call" | custom-call | tf_op jit(solution)/shard_map/pallas_call | solution.py:408
  47.6 1.2 %collective-permute-start.16 = (f32[8,256]{1,0:T(8,128)S(1)}, f32[8,256]{1,0:T(8,128)S(1)}, u32[]{:S(2)}, u32[]{:S(2)}) collective-permute-start(f32[8,256]{1,0:T(8,128)S(1)} %get-tuple-element.83.refs_0_), channel_id=1, source_target_pairs={{0,2},{2,0},{1,3},{3,1},{4,6},{6,4},{5,7},{7,5},{8,10},{10,8},{9,1... | collective-permute-start | bytes 24584 | tf_op jit(solution)/shard_map/ppermute | solution.py:316
  48.8 0.9 %collective-permute-start.18 = (f32[8,256]{1,0:T(8,128)S(1)}, f32[8,256]{1,0:T(8,128)S(1)}, u32[]{:S(2)}, u32[]{:S(2)}) collective-permute-start(f32[8,256]{1,0:T(8,128)S(1)} %get-tuple-element.83.refs_0_), channel_id=1, source_target_pairs={{0,3},{1,2},{2,1},{3,0},{4,7},{5,6},{6,5},{7,4},{8,11},{9,10},{10,... | collective-permute-start | bytes 24584 | tf_op jit(solution)/shard_map/ppermute | solution.py:327
  49.8 1.5 %collective-permute-done.16.refs_1_ = f32[8,256]{1,0:T(8,128)S(1)} collective-permute-done((f32[8,256]{1,0:T(8,128)S(1)}, f32[8,256]{1,0:T(8,128)S(1)}, u32[]{:S(2)}, u32[]{:S(2)}) %collective-permute-start.16) | collective-permute-done | bytes 8224 | tf_op jit(solution)/shard_map/ppermute | solution.py:316
  51.3 0.6 %collective-permute-done.18.refs_3_ = f32[8,256]{1,0:T(8,128)S(1)} collective-permute-done((f32[8,256]{1,0:T(8,128)S(1)}, f32[8,256]{1,0:T(8,128)S(1)}, u32[]{:S(2)}, u32[]{:S(2)}) %collective-permute-start.18) | collective-permute-done | bytes 8224 | tf_op jit(solution)/shard_map/ppermute | solution.py:327
  52.0 1.1 %collective-permute-start.19 = (f32[8,256]{1,0:T(8,128)S(1)}, f32[8,256]{1,0:T(8,128)S(1)}, u32[]{:S(2)}, u32[]{:S(2)}) collective-permute-start(f32[8,256]{1,0:T(8,128)S(1)} %shard_map.156.refs_0_), channel_id=1, source_target_pairs={{0,4},{4,8},{8,12},{12,0},{1,5},{5,9},{9,13},{13,1},{2,6},{6,10},{... | collective-permute-start | bytes 24584 | tf_op jit(solution)/shard_map/ppermute | solution.py:316
  53.0 3.1 %collective-permute-start.20 = (f32[8,256]{1,0:T(8,128)S(1)}, f32[8,256]{1,0:T(8,128)S(1)}, u32[]{:S(2)}, u32[]{:S(2)}) collective-permute-start(f32[8,256]{1,0:T(8,128)S(1)} %shard_map.156.refs_0_), channel_id=1, source_target_pairs={{0,8},{4,12},{8,0},{12,4},{1,9},{5,13},{9,1},{13,5},{2,10},{6,14},... | collective-permute-start | bytes 24584 | tf_op jit(solution)/shard_map/ppermute | solution.py:316
  56.1 0.8 %collective-permute-start.21 = (f32[8,256]{1,0:T(8,128)S(1)}, f32[8,256]{1,0:T(8,128)S(1)}, u32[]{:S(2)}, u32[]{:S(2)}) collective-permute-start(f32[8,256]{1,0:T(8,128)S(1)} %shard_map.156.refs_0_), channel_id=1, source_target_pairs={{0,12},{4,0},{8,4},{12,8},{1,13},{5,1},{9,5},{13,9},{2,14},{6,2},{... | collective-permute-start | bytes 24584 | tf_op jit(solution)/shard_map/ppermute | solution.py:316
  57.0 0.5 collective-permute-done.19.refs_1_
  57.5 0.3 collective-permute-done.20.refs_2_
  57.8 2.0 %collective-permute-done.21.refs_3_ = f32[8,256]{1,0:T(8,128)S(1)} collective-permute-done((f32[8,256]{1,0:T(8,128)S(1)}, f32[8,256]{1,0:T(8,128)S(1)}, u32[]{:S(2)}, u32[]{:S(2)}) %collective-permute-start.21) | collective-permute-done | bytes 8224 | tf_op jit(solution)/shard_map/ppermute | solution.py:316
  59.8 2.1 %shard_map.157 = (f32[1,256]{1,0:T(1,128)}, f32[1,256]{1,0:T(1,128)}, bf16[256,512]{1,0:T(8,128)(2,1)}, bf16[256,512]{1,0:T(8,128)(2,1)}) custom-call(s32[2]{0:T(128)S(1)} %copy-done.8, s32[1,256]{1,0:T(1,128)S(1)} %bitcast.15, s32[1,256]{1,0:T(1,128)S(1)} %bitcast.17, f32[256,512]{1,0:T(8,128)S(1)} %get-tuple-element.64.own_ref.so_ref, ...), custom_call_target="tpu_custom_call" | custom-call | tf_op jit(solution)/shard_map/pallas_call | solution.py:415
  (38 shorter events, 0.3 us)
Async XLA Ops:
  0.6 8.9 %copy-start.9 = (bf16[576,448]{0,1:T(8,128)(2,1)S(1)}, bf16[576,448]{0,1:T(8,128)(2,1)}, u32[]{:S(2)}) copy-start(bf16[576,448]{0,1:T(8,128)(2,1)} %param.21) | copy-start | bytes 1548292
  0.6 14.0 %copy-start.2 = (bf16[256,448]{0,1:T(8,128)(2,1)S(1)}, bf16[256,448]{0,1:T(8,128)(2,1)}, u32[]{:S(2)}) copy-start(bf16[256,448]{0,1:T(8,128)(2,1)} %param.12) | copy-start | bytes 688132
  0.7 14.1 %copy-start.7 = (s32[2]{0:T(128)S(1)}, s32[2]{0:T(128)}, u32[]{:S(2)}) copy-start(s32[2]{0:T(128)} %lens_ref.2) | copy-start | bytes 28
  3.2 3.3 %collective-permute-start = (f32[576,128]{1,0:T(8,128)}, f32[576,128]{1,0:T(8,128)S(1)}, u32[]{:S(2)}, u32[]{:S(2)}) collective-permute-start(f32[576,128]{1,0:T(8,128)} %get-tuple-element.47), channel_id=1, source_target_pairs={{0,1},{1,0},{2,3},{3,2},{4,5},{5,4},{6,7},{7,6},{8,9},{9,8},{10,11... | collective-permute-start | bytes 884744 | tf_op jit(solution)/shard_map/ppermute | solution.py:312
  3.8 10.8 %collective-permute-start.2 = (bf16[128,256]{1,0:T(8,128)(2,1)}, bf16[128,256]{1,0:T(8,128)(2,1)S(1)}, u32[]{:S(2)}, u32[]{:S(2)}) collective-permute-start(bf16[128,256]{1,0:T(8,128)(2,1)} %get-tuple-element.54.refs_0_), channel_id=1, source_target_pairs={{0,2},{2,0},{1,3},{3,1},{4,6},{6,4},{5,7},{7,5},{8,10},{10,8},{9,1... | collective-permute-start | bytes 196616 | tf_op jit(solution)/shard_map/ppermute | solution.py:316
  6.3 8.5 %collective-permute-start.3 = (bf16[128,256]{1,0:T(8,128)(2,1)}, bf16[128,256]{1,0:T(8,128)(2,1)S(1)}, u32[]{:S(2)}, u32[]{:S(2)}) collective-permute-start(bf16[128,256]{1,0:T(8,128)(2,1)} %get-tuple-element.54.refs_0_), channel_id=1, source_target_pairs={{0,1},{1,0},{2,3},{3,2},{4,5},{5,4},{6,7},{7,6},{8,9},{9,8},{10,11... | collective-permute-start | bytes 196616 | tf_op jit(solution)/shard_map/ppermute | solution.py:327
  6.5 8.3 %collective-permute-start.4 = (bf16[128,256]{1,0:T(8,128)(2,1)}, bf16[128,256]{1,0:T(8,128)(2,1)S(1)}, u32[]{:S(2)}, u32[]{:S(2)}) collective-permute-start(bf16[128,256]{1,0:T(8,128)(2,1)} %get-tuple-element.54.refs_0_), channel_id=1, source_target_pairs={{0,3},{1,2},{2,1},{3,0},{4,7},{5,6},{6,5},{7,4},{8,11},{9,10},{10,... | collective-permute-start | bytes 196616 | tf_op jit(solution)/shard_map/ppermute | solution.py:327
  6.5 1.0 %copy-start.3 = (f32[576,128]{1,0:T(8,128)S(1)}, f32[576,128]{1,0:T(8,128)}, u32[]{:S(2)}) copy-start(f32[576,128]{1,0:T(8,128)} %get-tuple-element.46.keep_ref) | copy-start | bytes 884740
  7.5 4.8 %copy-start.10 = (bf16[256,576]{0,1:T(8,128)(2,1)S(1)}, bf16[256,576]{0,1:T(8,128)(2,1)}, u32[]{:S(2)}) copy-start(bf16[256,576]{0,1:T(8,128)(2,1)} %param.13) | copy-start | bytes 884740
  7.5 7.3 %copy-start.4 = (bf16[128,256]{1,0:T(8,128)(2,1)S(1)}, bf16[128,256]{1,0:T(8,128)(2,1)}, u32[]{:S(2)}) copy-start(bf16[128,256]{1,0:T(8,128)(2,1)} %get-tuple-element.54.refs_0_) | copy-start | bytes 196612
  7.5 8.8 %collective-permute-start.1 = (f32[288,128]{1,0:T(8,128)S(1)}, f32[288,128]{1,0:T(8,128)S(1)}, u32[]{:S(2)}, u32[]{:S(2)}) collective-permute-start(f32[288,128]{1,0:T(8,128)S(1)} %get-tuple-element.51), channel_id=1, source_target_pairs={{0,2},{2,0},{1,3},{3,1},{4,6},{6,4},{5,7},{7,5},{8,10},{10,8},{9,1... | collective-permute-start | bytes 442376 | tf_op jit(solution)/shard_map/ppermute | solution.py:316
  9.5 6.8 %collective-permute-start.5 = (bf16[448,256]{1,0:T(8,128)(2,1)}, bf16[448,256]{1,0:T(8,128)(2,1)S(1)}, u32[]{:S(2)}, u32[]{:S(2)}) collective-permute-start(bf16[448,256]{1,0:T(8,128)(2,1)} %bitcast.10), channel_id=1, source_target_pairs={{0,1},{1,0},{2,3},{3,2},{4,5},{5,4},{6,7},{7,6},{8,9},{9,8},{10,11... | collective-permute-start | bytes 688136 | tf_op jit(solution)/shard_map/ppermute | solution.py:312
  12.3 13.0 %copy-start.1 = (bf16[1792,512]{1,0:T(8,128)(2,1)S(1)}, bf16[1792,512]{1,0:T(8,128)(2,1)}, u32[]{:S(2)}) copy-start(bf16[1792,512]{1,0:T(8,128)(2,1)} %head.1) | copy-start | bytes 5505028
  12.3 13.0 %copy-start.5 = (s32[256]{0:T(256)S(1)}, s32[256]{0:T(256)}, u32[]{:S(2)}) copy-start(s32[256]{0:T(256)} %param.16) | copy-start | bytes 3076
  14.6 8.4 %collective-permute-start.10 = (bf16[448,256]{1,0:T(8,128)(2,1)S(1)}, bf16[448,256]{1,0:T(8,128)(2,1)S(1)}, u32[]{:S(2)}, u32[]{:S(2)}) collective-permute-start(bf16[448,256]{1,0:T(8,128)(2,1)S(1)} %bitcast.11), channel_id=1, source_target_pairs={{0,2},{2,0},{1,3},{3,1},{4,6},{6,4},{5,7},{7,5},{8,10},{10,8},{9,1... | collective-permute-start | bytes 688136 | tf_op jit(solution)/shard_map/ppermute | solution.py:316
  16.3 12.5 %collective-permute-start.9 = (f32[448,128]{1,0:T(8,128)S(1)}, f32[448,128]{1,0:T(8,128)S(1)}, u32[]{:S(2)}, u32[]{:S(2)}) collective-permute-start(f32[448,128]{1,0:T(8,128)S(1)} %get-tuple-element.75), channel_id=1, source_target_pairs={{0,2},{2,0},{1,3},{3,1},{4,6},{6,4},{5,7},{7,5},{8,10},{10,8},{9,1... | collective-permute-start | bytes 688136 | tf_op jit(solution)/shard_map/ppermute | solution.py:316
  18.3 8.2 %collective-permute-start.6 = (bf16[288,128]{1,0:T(8,128)(2,1)S(1)}, bf16[288,128]{1,0:T(8,128)(2,1)S(1)}, u32[]{:S(2)}, u32[]{:S(2)}) collective-permute-start(bf16[288,128]{1,0:T(8,128)(2,1)S(1)} %add_convert_fusion.1.refs_0_), channel_id=1, source_target_pairs={{0,4},{4,0},{8,12},{12,8},{1,5},{5,1},{9,13},{13,9},{2,6},{6,2},{1... | collective-permute-start | bytes 221192 | tf_op jit(solution)/shard_map/ppermute | solution.py:323
  19.9 7.8 %collective-permute-start.7 = (bf16[288,128]{1,0:T(8,128)(2,1)S(1)}, bf16[288,128]{1,0:T(8,128)(2,1)S(1)}, u32[]{:S(2)}, u32[]{:S(2)}) collective-permute-start(bf16[288,128]{1,0:T(8,128)(2,1)S(1)} %add_convert_fusion.1.refs_0_), channel_id=1, source_target_pairs={{0,8},{4,12},{8,0},{12,4},{1,9},{5,13},{9,1},{13,5},{2,10},{6,14},... | collective-permute-start | bytes 221192 | tf_op jit(solution)/shard_map/ppermute | solution.py:323
  22.5 6.3 %collective-permute-start.8 = (bf16[288,128]{1,0:T(8,128)(2,1)S(1)}, bf16[288,128]{1,0:T(8,128)(2,1)S(1)}, u32[]{:S(2)}, u32[]{:S(2)}) collective-permute-start(bf16[288,128]{1,0:T(8,128)(2,1)S(1)} %add_convert_fusion.1.refs_0_), channel_id=1, source_target_pairs={{0,12},{4,8},{8,4},{12,0},{1,13},{5,9},{9,5},{13,1},{2,14},{6,10},... | collective-permute-start | bytes 221192 | tf_op jit(solution)/shard_map/ppermute | solution.py:323
  23.1 13.0 %collective-permute-start.11 = (bf16[576,256]{1,0:T(8,128)(2,1)S(1)}, bf16[576,256]{1,0:T(8,128)(2,1)S(1)}, u32[]{:S(2)}, u32[]{:S(2)}) collective-permute-start(bf16[576,256]{1,0:T(8,128)(2,1)S(1)} %bitcast.20), channel_id=1, source_target_pairs={{0,2},{2,0},{1,3},{3,1},{4,6},{6,4},{5,7},{7,5},{8,10},{10,8},{9,1... | collective-permute-start | bytes 884744 | tf_op jit(solution)/shard_map/ppermute | solution.py:316
  26.5 11.8 %copy-start = (bf16[2304,512]{1,0:T(8,128)(2,1)S(1)}, bf16[2304,512]{1,0:T(8,128)(2,1)}, u32[]{:S(2)}) copy-start(bf16[2304,512]{1,0:T(8,128)(2,1)} %refs_2_.3) | copy-start | bytes 7077892
  28.9 14.8 %collective-permute-start.13 = (bf16[448,128]{1,0:T(8,128)(2,1)S(1)}, bf16[448,128]{1,0:T(8,128)(2,1)S(1)}, u32[]{:S(2)}, u32[]{:S(2)}) collective-permute-start(bf16[448,128]{1,0:T(8,128)(2,1)S(1)} %add_convert_fusion.refs_0_), channel_id=1, source_target_pairs={{0,4},{4,0},{8,12},{12,8},{1,5},{5,1},{9,13},{13,9},{2,6},{6,2},{1... | collective-permute-start | bytes 344072 | tf_op jit(solution)/shard_map/ppermute | solution.py:323
  30.0 13.7 %collective-permute-start.14 = (bf16[448,128]{1,0:T(8,128)(2,1)S(1)}, bf16[448,128]{1,0:T(8,128)(2,1)S(1)}, u32[]{:S(2)}, u32[]{:S(2)}) collective-permute-start(bf16[448,128]{1,0:T(8,128)(2,1)S(1)} %add_convert_fusion.refs_0_), channel_id=1, source_target_pairs={{0,8},{4,12},{8,0},{12,4},{1,9},{5,13},{9,1},{13,5},{2,10},{6,14},... | collective-permute-start | bytes 344072 | tf_op jit(solution)/shard_map/ppermute | solution.py:323
  32.3 11.4 %collective-permute-start.15 = (bf16[448,128]{1,0:T(8,128)(2,1)S(1)}, bf16[448,128]{1,0:T(8,128)(2,1)S(1)}, u32[]{:S(2)}, u32[]{:S(2)}) collective-permute-start(bf16[448,128]{1,0:T(8,128)(2,1)S(1)} %add_convert_fusion.refs_0_), channel_id=1, source_target_pairs={{0,12},{4,8},{8,4},{12,0},{1,13},{5,9},{9,5},{13,1},{2,14},{6,10},... | collective-permute-start | bytes 344072 | tf_op jit(solution)/shard_map/ppermute | solution.py:323
  33.3 6.8 %collective-permute-start.12 = (bf16[1152,128]{1,0:T(8,128)(2,1)S(1)}, bf16[1152,128]{1,0:T(8,128)(2,1)S(1)}, u32[]{:S(2)}, u32[]{:S(2)}) collective-permute-start(bf16[1152,128]{1,0:T(8,128)(2,1)S(1)} %shard_map.152), channel_id=1, source_target_pairs={{0,2},{2,0},{1,3},{3,1},{4,6},{6,4},{5,7},{7,5},{8,10},{10,8},{9,1... | collective-permute-start | bytes 884744 | tf_op jit(solution)/shard_map/ppermute | solution.py:316
  38.3 4.0 %copy-start.6 = (s32[256]{0:T(256)S(1)}, s32[256]{0:T(256)}, u32[]{:S(2)}) copy-start(s32[256]{0:T(256)} %param.17) | copy-start | bytes 3076
  46.2 13.6 %copy-start.8 = (s32[2]{0:T(128)S(1)}, s32[2]{0:T(128)}, u32[]{:S(2)}) copy-start(s32[2]{0:T(128)} %lens_ref.3) | copy-start | bytes 28
  47.6 3.7 %collective-permute-start.16 = (f32[8,256]{1,0:T(8,128)S(1)}, f32[8,256]{1,0:T(8,128)S(1)}, u32[]{:S(2)}, u32[]{:S(2)}) collective-permute-start(f32[8,256]{1,0:T(8,128)S(1)} %get-tuple-element.83.refs_0_), channel_id=1, source_target_pairs={{0,2},{2,0},{1,3},{3,1},{4,6},{6,4},{5,7},{7,5},{8,10},{10,8},{9,1... | collective-permute-start | bytes 24584 | tf_op jit(solution)/shard_map/ppermute | solution.py:316
  48.8 2.5 %collective-permute-start.17 = (f32[8,256]{1,0:T(8,128)S(1)}, f32[8,256]{1,0:T(8,128)S(1)}, u32[]{:S(2)}, u32[]{:S(2)}) collective-permute-start(f32[8,256]{1,0:T(8,128)S(1)} %get-tuple-element.83.refs_0_), channel_id=1, source_target_pairs={{0,1},{1,0},{2,3},{3,2},{4,5},{5,4},{6,7},{7,6},{8,9},{9,8},{10,11... | collective-permute-start | bytes 24584 | tf_op jit(solution)/shard_map/ppermute | solution.py:327
  48.8 3.1 %collective-permute-start.18 = (f32[8,256]{1,0:T(8,128)S(1)}, f32[8,256]{1,0:T(8,128)S(1)}, u32[]{:S(2)}, u32[]{:S(2)}) collective-permute-start(f32[8,256]{1,0:T(8,128)S(1)} %get-tuple-element.83.refs_0_), channel_id=1, source_target_pairs={{0,3},{1,2},{2,1},{3,0},{4,7},{5,6},{6,5},{7,4},{8,11},{9,10},{10,... | collective-permute-start | bytes 24584 | tf_op jit(solution)/shard_map/ppermute | solution.py:327
  52.0 5.5 %collective-permute-start.19 = (f32[8,256]{1,0:T(8,128)S(1)}, f32[8,256]{1,0:T(8,128)S(1)}, u32[]{:S(2)}, u32[]{:S(2)}) collective-permute-start(f32[8,256]{1,0:T(8,128)S(1)} %shard_map.156.refs_0_), channel_id=1, source_target_pairs={{0,4},{4,8},{8,12},{12,0},{1,5},{5,9},{9,13},{13,1},{2,6},{6,10},{... | collective-permute-start | bytes 24584 | tf_op jit(solution)/shard_map/ppermute | solution.py:316
  53.0 4.7 %collective-permute-start.20 = (f32[8,256]{1,0:T(8,128)S(1)}, f32[8,256]{1,0:T(8,128)S(1)}, u32[]{:S(2)}, u32[]{:S(2)}) collective-permute-start(f32[8,256]{1,0:T(8,128)S(1)} %shard_map.156.refs_0_), channel_id=1, source_target_pairs={{0,8},{4,12},{8,0},{12,4},{1,9},{5,13},{9,1},{13,5},{2,10},{6,14},... | collective-permute-start | bytes 24584 | tf_op jit(solution)/shard_map/ppermute | solution.py:316
  56.1 3.7 %collective-permute-start.21 = (f32[8,256]{1,0:T(8,128)S(1)}, f32[8,256]{1,0:T(8,128)S(1)}, u32[]{:S(2)}, u32[]{:S(2)}) collective-permute-start(f32[8,256]{1,0:T(8,128)S(1)} %shard_map.156.refs_0_), channel_id=1, source_target_pairs={{0,12},{4,0},{8,4},{12,8},{1,13},{5,1},{9,5},{13,9},{2,14},{6,2},{... | collective-permute-start | bytes 24584 | tf_op jit(solution)/shard_map/ppermute | solution.py:316
